TPU v7x, 32 devices: a whole 2x2x4 slice. The times are simulated.
32 devices in a mesh: ty: 4 (over y, x), tx: 8 (over z, core).
Axes of the slice: x: 2, y: 2, z: 4, core: 2. Of those that a mesh axis runs over, the one named last changes fastest.
Arguments:
- channel_cube: bfloat16 [256, 512, 128], P(('ty', 'tx'))
- footprint: int32 [32, 8], replicated, may hold values 0 or 1
- kernel_sigmas: int32 [4], replicated, may hold values from 1 to 3, as said below
- spectral_taps: int32 [2, 4], replicated, may hold values from 1 to 5, as said below
Outputs:
- snr_cubes: bfloat16 [4, 512, 128, 256], P(None, 'ty', 'tx')
Inputs may be any that keep to these rules, and one draw needn't show every extreme that they name: `kernel_sigmas`: some scale has exactly 3. `spectral_taps`: row 0 holds widths up to 5, row 1 dilations up to 4; some scale has width 5 and dilation 4 together.
All inputs are finite; a program needn't handle non-finite values.
Results may differ from a plain program's by a relative error of at most 0.0077.
Values may be sent and summed in bfloat16 or wider, within the bound.
No kernel may reach another device: no remote copies, remote signals or barrier semaphores. Data moves between devices by JAX's collectives and lax.ppermute only.
A program may use at most 192 MiB of HBM per device.

v0:
```python
import jax
import jax.numpy as jnp
from jax import lax
from jax.sharding import PartitionSpec as P

TILE_Y = 128
TILE_X = 16
NSC = 4
WMAX = 5
PT = 16
HALO = 9
PADC = 8


def with_halo(x, sides, width):
    for axis, dim in sides:
        peers, length = (lax.axis_size(axis), x.shape[dim])
        up = [(i, (i + 1) % peers) for i in range(peers - 1)]
        down = [(j, i) for i, j in up]
        last = lax.slice_in_dim(x, length - width, length, axis=dim)
        leading = lax.slice_in_dim(x, 0, width, axis=dim)
        before = lax.ppermute(last, axis, up)
        after = lax.ppermute(leading, axis, down)
        x = jnp.concatenate([before, x, after], axis=dim)
    return x


def gauss_taps(sigma_value):
    offsets = jnp.arange(-HALO, HALO + 1).astype(jnp.float32)
    spread = sigma_value.astype(jnp.float32)
    weights = jnp.exp(-offsets * offsets / (2.0 * spread * spread))
    weights = jnp.where(jnp.abs(offsets) <= 3.0 * spread, weights, jnp.float32(0.0))
    return weights / jnp.sum(weights)


def boxcar(field, width, dilation):
    last = field.ndim - 1
    channels = field.shape[last]
    pads = [(0, 0)] * last + [(PADC, PADC)]
    padded = jnp.pad(field, pads)
    total = jnp.zeros(field.shape, jnp.float32)
    for step in range(WMAX):
        start = PADC + dilation * (step - (width - 1) // 2)
        piece = lax.dynamic_slice_in_dim(padded, start, channels, last)
        total = total + jnp.where(step < width, piece, jnp.float32(0.0))
    return total / width.astype(jnp.float32)


def band_matrix(taps_bf, length):
    out_index = jnp.arange(length)[:, None, None]
    in_index = jnp.arange(length + 2 * HALO)[None, :, None]
    tap_index = jnp.arange(2 * HALO + 1)[None, None, :]
    chosen = jnp.where(
        in_index - out_index == tap_index,
        taps_bf.astype(jnp.float32)[None, None, :],
        jnp.float32(0.0),
    )
    return jnp.sum(chosen, axis=2).astype(jnp.bfloat16)


def relay(pieces):
    ch_local, n_rows, n_cols, cells = pieces.shape
    arrived = lax.all_to_all(
        pieces.reshape(ch_local, n_rows * n_cols, cells),
        ("ty", "tx"),
        split_axis=1,
        concat_axis=0,
        tiled=True,
    )
    return arrived.reshape(-1, cells)


def local(channel_cube, footprint, kernel_sigmas, spectral_taps):
    n_rows = lax.axis_size("ty")
    n_cols = lax.axis_size("tx")
    ch_local, full_y, full_x = channel_cube.shape
    pixel_mask = jnp.repeat(jnp.repeat(footprint, PT, 0), PT, 1).astype(jnp.float32)
    count = jnp.maximum(jnp.sum(pixel_mask), jnp.float32(1.0))
    row_start = lax.axis_index("ty") * TILE_Y
    col_start = lax.axis_index("tx") * TILE_X
    tile_mask = lax.dynamic_slice(pixel_mask, (row_start, col_start), (TILE_Y, TILE_X))
    plane_vals = jnp.where(
        pixel_mask[None] > 0.5, channel_cube.astype(jnp.float32), jnp.float32(0.0)
    )
    local_squares = jnp.sum(plane_vals * plane_vals, axis=(1, 2))
    squares = lax.all_gather(local_squares, ("ty", "tx"), axis=0, tiled=True)
    pieces = channel_cube.reshape(ch_local, n_rows, TILE_Y, n_cols, TILE_X).transpose(0, 1, 3, 2, 4)
    arrived = relay(pieces.reshape(ch_local, n_rows, n_cols, TILE_Y * TILE_X))
    channels = arrived.shape[0]
    tile_cells = arrived.T.reshape(TILE_Y, TILE_X, channels)
    tile_cells = jnp.where(tile_mask[:, :, None] > 0.5, tile_cells, jnp.zeros_like(tile_cells))
    padded = with_halo(tile_cells, (("ty", 0), ("tx", 1)), HALO)
    channel_noise = jnp.sqrt(squares / count + 1e-06)
    results = []
    for scale_idx in range(NSC):
        taps = gauss_taps(kernel_sigmas[scale_idx])
        taps_bf = taps.astype(jnp.bfloat16)
        row_band = band_matrix(taps_bf, TILE_Y)
        col_band = band_matrix(taps_bf, TILE_X)
        rows_pass = jnp.einsum(
            "ij,jxc->ixc", row_band, padded, preferred_element_type=jnp.float32
        ).astype(jnp.bfloat16)
        smooth = jnp.einsum("xk,ykc->yxc", col_band, rows_pass, preferred_element_type=jnp.float32)
        width = spectral_taps[0, scale_idx]
        dilation = spectral_taps[1, scale_idx]
        boxed = boxcar(smooth, width, dilation)
        knorm = jnp.sum(taps * taps) / jnp.sqrt(width.astype(jnp.float32))
        scaled = boxed * tile_mask[:, :, None] / (channel_noise[None, None, :] * knorm)
        results.append(scaled.astype(jnp.bfloat16))
    return jnp.stack(results)


def solution(mesh):
    placed = (P(("ty", "tx"), None, None), P(), P(), P())
    return jax.shard_map(
        local, mesh=mesh, in_specs=placed, out_specs=P(None, "ty", "tx", None), check_vma=False
    )
```

profile of v0, /device:TPU:1, one launch (start us, length us, event | category | flops | bytes accessed | tf_op | source)
XLA Modules:
  0.0 176.0 jit_solution(6123437555780068440)
XLA Ops:
  0.0 1.5 copy.34
  1.8 5.8 %copy.45 = bf16[8,4,8,128,16]{4,3,0,2,1:T(8,128)(2,1)} copy(bf16[8,4,8,128,16]{3,1,4,2,0:T(4,128)(2,1)S(1)} %bitcast.95) | data formatting | bytes 2097152 | tf_op jit(solution)/shard_map/reshape;reshape | solution.py:64
  7.5 15.8 %reshape.174 = bf16[8,32,2048]{2,0,1:T(8,128)(2,1)} reshape(bf16[8,4,8,128,16]{4,3,0,2,1:T(8,128)(2,1)} %copy.45) | data formatting | bytes 2097152 | tf_op jit(solution)/shard_map/reshape;reshape | solution.py:64
  23.4 7.1 %all-to-all-start = ((bf16[8,32,2048]{2,0,1:T(8,128)(2,1)}), bf16[8,32,2048]{2,0,1:T(8,128)(2,1)S(1)}, u32[]{:S(2)}, u32[]{:S(2)}) async-start(bf16[8,32,2048]{2,0,1:T(8,128)(2,1)} %reshape.174), calls=%async_computation | async-start | bytes 2097152 | tf_op jit(solution)/shard_map/all_to_all | solution.py:63
  66.4 1.3 multiply_reduce_fusion.4
  75.4 1.4 multiply_reduce_fusion.1
  78.2 39.2 %all-reduce.4 = f32[256]{0:T(256)S(1)} all-reduce(f32[256]{0:T(256)S(1)} %dynamic-update-slice), channel_id=1, replica_groups=mesh['ty'=4,'tx'=8] {'ty','tx'}, use_global_device_ids=true, to_apply=%add.4 | all-reduce | flops 256 | bytes 2048
  118.6 1.3 convert_convert_fusion.2
  121.4 3.0 %collective-permute-start = (bf16[9,16,256]{2,0,1:T(8,128)(2,1)S(1)}, bf16[9,16,256]{2,0,1:T(8,128)(2,1)S(1)}, u32[]{:S(2)}, u32[]{:S(2)}) collective-permute-start(bf16[9,16,256]{2,0,1:T(8,128)(2,1)S(1)} %get-tuple-element.19), channel_id=1, source_target_pairs={{0,8},{8,16},{16,24},{1,9},{9,17},{17,25},{2,10},{10,18},{18,26},{... | collective-permute-start | bytes 221192 | tf_op jit(solution)/shard_map/ppermute | solution.py:22
  124.4 1.3 collective-permute-start.1
  126.3 4.5 %collective-permute-done.1 = bf16[9,16,256]{2,0,1:T(8,128)(2,1)S(1)} collective-permute-done((bf16[9,16,256]{2,0,1:T(8,128)(2,1)S(1)}, bf16[9,16,256]{2,0,1:T(8,128)(2,1)S(1)}, u32[]{:S(2)}, u32[]{:S(2)}) %collective-permute-start.1) | collective-permute-done | bytes 73760 | tf_op jit(solution)/shard_map/ppermute | solution.py:23
  131.5 6.1 %collective-permute-start.2 = (bf16[146,9,256]{2,0,1:T(8,128)(2,1)S(1)}, bf16[146,9,256]{2,0,1:T(8,128)(2,1)S(1)}, u32[]{:S(2)}, u32[]{:S(2)}) collective-permute-start(bf16[146,9,256]{2,0,1:T(8,128)(2,1)S(1)} %get-tuple-element.17), channel_id=1, source_target_pairs={{0,1},{1,2},{2,3},{3,4},{4,5},{5,6},{6,7},{8,9},{9,10},{10,11},{11... | collective-permute-start | bytes 2018312 | tf_op jit(solution)/shard_map/ppermute | solution.py:22
  137.6 2.1 %collective-permute-start.3 = (bf16[146,9,256]{2,0,1:T(8,128)(2,1)S(1)}, bf16[146,9,256]{2,0,1:T(8,128)(2,1)S(1)}, u32[]{:S(2)}, u32[]{:S(2)}) collective-permute-start(bf16[146,9,256]{2,0,1:T(8,128)(2,1)S(1)} %get-tuple-element.18), channel_id=1, source_target_pairs={{1,0},{2,1},{3,2},{4,3},{5,4},{6,5},{7,6},{9,8},{10,9},{11,10},{12... | collective-permute-start | bytes 2018312 | tf_op jit(solution)/shard_map/ppermute | solution.py:23
  140.6 5.0 %collective-permute-done.2 = bf16[146,9,256]{2,0,1:T(8,128)(2,1)S(1)} collective-permute-done((bf16[146,9,256]{2,0,1:T(8,128)(2,1)S(1)}, bf16[146,9,256]{2,0,1:T(8,128)(2,1)S(1)}, u32[]{:S(2)}, u32[]{:S(2)}) %collective-permute-start.2) | collective-permute-done | bytes 672800 | tf_op jit(solution)/shard_map/ppermute | solution.py:22
  145.6 4.4 %collective-permute-done.3 = bf16[146,9,256]{2,0,1:T(8,128)(2,1)S(1)} collective-permute-done((bf16[146,9,256]{2,0,1:T(8,128)(2,1)S(1)}, bf16[146,9,256]{2,0,1:T(8,128)(2,1)S(1)}, u32[]{:S(2)}, u32[]{:S(2)}) %collective-permute-start.3) | collective-permute-done | bytes 672800 | tf_op jit(solution)/shard_map/ppermute | solution.py:23
  151.2 1.3 fusion.48
  153.8 1.3 fusion.51
  156.4 1.3 fusion.54
  158.9 1.3 fusion.57
  160.3 3.3 %fusion.60 = bf16[1,128,16,256]{3,2,1,0:T(8,128)(2,1)S(1)} fusion(f32[256]{0:T(256)S(1)} %get-tuple-element.13, f32[128,16]{1,0:T(8,128)S(1)} %copy.40, f32[]{:T(128)} %bitcast.18, s32[]{:T(128)S(6)} %select_n.301, f32[128,16,256]{2,1,0:T(8,128)S(1)} %fusion.48, pred[]{:T(512)} %bitcast.17, s32[]{:T(128)S(6)} %select_n.298, pred[]{:T(512)} %bitcast.16, ...), kind=kLoop, calls=%fused_computation.90 | loop fusion | flops 6815744 | bytes 3154973 | tf_op jit(solution)/shard_map/stack | solution.py:110
  163.5 3.3 %fusion.61 = bf16[1,128,16,256]{3,2,1,0:T(8,128)(2,1)S(1)} fusion(f32[256]{0:T(256)S(1)} %get-tuple-element.29, f32[128,16]{1,0:T(8,128)S(1)} %copy.40, f32[]{:T(128)} %bitcast.31, s32[]{:T(128)S(6)} %select_n.321, f32[128,16,256]{2,1,0:T(8,128)S(1)} %fusion.51, pred[]{:T(512)} %bitcast.30, s32[]{:T(128)S(6)} %select_n.318, pred[]{:T(512)} %bitcast.29, ...), kind=kLoop, calls=%fused_computation.91 | loop fusion | flops 6815744 | bytes 3154973 | tf_op jit(solution)/shard_map/stack | solution.py:110
  166.8 3.5 %fusion.62 = bf16[1,128,16,256]{3,2,1,0:T(8,128)(2,1)S(1)} fusion(f32[256]{0:T(256)S(1)} %get-tuple-element.30, f32[128,16]{1,0:T(8,128)S(1)} %copy.40, f32[]{:T(128)} %bitcast.44, s32[]{:T(128)S(6)} %select_n.340, f32[128,16,256]{2,1,0:T(8,128)S(1)} %fusion.54, pred[]{:T(512)} %bitcast.43, s32[]{:T(128)S(6)} %select_n.337, pred[]{:T(512)} %bitcast.42, ...), kind=kLoop, calls=%fused_computation.92 | loop fusion | flops 6815744 | bytes 3154973 | tf_op jit(solution)/shard_map/stack | solution.py:110
  170.3 3.4 %fusion.63 = bf16[1,128,16,256]{3,2,1,0:T(8,128)(2,1)S(1)} fusion(f32[256]{0:T(256)S(1)} %get-tuple-element.31, f32[128,16]{1,0:T(8,128)S(1)} %copy.40, f32[]{:T(128)} %bitcast.57, s32[]{:T(128)S(6)} %select_n.359, f32[128,16,256]{2,1,0:T(8,128)S(1)} %fusion.57, pred[]{:T(512)} %bitcast.56, s32[]{:T(128)S(6)} %select_n.356, pred[]{:T(512)} %bitcast.55, ...), kind=kLoop, calls=%fused_computation.93 | loop fusion | flops 6815744 | bytes 3154973 | tf_op jit(solution)/shard_map/stack | solution.py:110
  173.7 2.3 %pad_maximum_fusion = bf16[4,128,16,256]{3,2,1,0:T(8,128)(2,1)} fusion(bf16[1,128,16,256]{3,2,1,0:T(8,128)(2,1)S(1)} %fusion.63, bf16[1,128,16,256]{3,2,1,0:T(8,128)(2,1)S(1)} %fusion.62, bf16[1,128,16,256]{3,2,1,0:T(8,128)(2,1)S(1)} %fusion.61, bf16[1,128,16,256]{3,2,1,0:T(8,128)(2,1)S(1)} %fusion.60), kind=kLoop, calls=%fused_computation.20 | loop fusion | flops 6291456 | bytes 8388608 | tf_op jit(solution)/shard_map/stack | solution.py:110
  (47 shorter events, 18.3 us)
Async XLA Ops:
  23.3 7.1 %copy-start.2 = (s32[4]{0:T(128)S(1)}, s32[4]{0:T(128)}, u32[]{:S(2)}) copy-start(s32[4]{0:T(128)} %param.6) | copy-start | bytes 52
  23.3 10.5 %copy-start.1 = (s32[2,4]{1,0:T(2,128)S(1)}, s32[2,4]{1,0:T(2,128)}, u32[]{:S(2)}) copy-start(s32[2,4]{1,0:T(2,128)} %param.7) | copy-start | bytes 100
  23.3 41.5 %copy-start.3 = (s32[32,8]{0,1:T(8,128)S(1)}, s32[32,8]{0,1:T(8,128)}, u32[]{:S(2)}) copy-start(s32[32,8]{0,1:T(8,128)} %param.5) | copy-start | bytes 3076
  23.3 54.1 %copy-start = (bf16[8,512,128]{2,1,0:T(8,128)(2,1)S(1)}, bf16[8,512,128]{2,1,0:T(8,128)(2,1)}, u32[]{:S(2)}) copy-start(bf16[8,512,128]{2,1,0:T(8,128)(2,1)} %param.4) | copy-start | bytes 3145732
  23.4 96.7 %all-to-all-start = ((bf16[8,32,2048]{2,0,1:T(8,128)(2,1)}), bf16[8,32,2048]{2,0,1:T(8,128)(2,1)S(1)}, u32[]{:S(2)}, u32[]{:S(2)}) async-start(bf16[8,32,2048]{2,0,1:T(8,128)(2,1)} %reshape.174), calls=%async_computation | async-start | bytes 2097152 | tf_op jit(solution)/shard_map/all_to_all | solution.py:63
  121.4 4.9 %collective-permute-start = (bf16[9,16,256]{2,0,1:T(8,128)(2,1)S(1)}, bf16[9,16,256]{2,0,1:T(8,128)(2,1)S(1)}, u32[]{:S(2)}, u32[]{:S(2)}) collective-permute-start(bf16[9,16,256]{2,0,1:T(8,128)(2,1)S(1)} %get-tuple-element.19), channel_id=1, source_target_pairs={{0,8},{8,16},{16,24},{1,9},{9,17},{17,25},{2,10},{10,18},{18,26},{... | collective-permute-start | bytes 221192 | tf_op jit(solution)/shard_map/ppermute | solution.py:22
  124.4 6.5 %collective-permute-start.1 = (bf16[9,16,256]{2,0,1:T(8,128)(2,1)S(1)}, bf16[9,16,256]{2,0,1:T(8,128)(2,1)S(1)}, u32[]{:S(2)}, u32[]{:S(2)}) collective-permute-start(bf16[9,16,256]{2,0,1:T(8,128)(2,1)S(1)} %get-tuple-element.20), channel_id=1, source_target_pairs={{8,0},{16,8},{24,16},{9,1},{17,9},{25,17},{10,2},{18,10},{26,18},{... | collective-permute-start | bytes 221192 | tf_op jit(solution)/shard_map/ppermute | solution.py:23
  131.5 14.1 %collective-permute-start.2 = (bf16[146,9,256]{2,0,1:T(8,128)(2,1)S(1)}, bf16[146,9,256]{2,0,1:T(8,128)(2,1)S(1)}, u32[]{:S(2)}, u32[]{:S(2)}) collective-permute-start(bf16[146,9,256]{2,0,1:T(8,128)(2,1)S(1)} %get-tuple-element.17), channel_id=1, source_target_pairs={{0,1},{1,2},{2,3},{3,4},{4,5},{5,6},{6,7},{8,9},{9,10},{10,11},{11... | collective-permute-start | bytes 2018312 | tf_op jit(solution)/shard_map/ppermute | solution.py:22
  137.6 12.4 %collective-permute-start.3 = (bf16[146,9,256]{2,0,1:T(8,128)(2,1)S(1)}, bf16[146,9,256]{2,0,1:T(8,128)(2,1)S(1)}, u32[]{:S(2)}, u32[]{:S(2)}) collective-permute-start(bf16[146,9,256]{2,0,1:T(8,128)(2,1)S(1)} %get-tuple-element.18), channel_id=1, source_target_pairs={{1,0},{2,1},{3,2},{4,3},{5,4},{6,5},{7,6},{9,8},{10,9},{11,10},{12... | collective-permute-start | bytes 2018312 | tf_op jit(solution)/shard_map/ppermute | solution.py:23
where the time goes:
time: 177 us; the launch traced here: 176 us
  blocking collectives  39.2 us (22%)
  between operations  37 us (21%)
  other arithmetic  29.4 us (17%)
  local copies, waits for them, and re-layouts  26 us (15%)
  starting transfers between devices  19.6 us (11%)
  waiting for transfers between devices  14.5 us (8%)
  matrix products  10.3 us (6%)
    unnamed x1, blocking collectives  39.2 us
    another operation x2, local copies, waits for them, and re-layouts, relay(): pieces.reshape(ch_local, n_rows * n_cols, cells)  21.6 us
    another operation x5, other arithmetic, local(): return jnp.stack(results)  15.7 us
    ppermute x2, starting transfers between devices, with_halo(): before = lax.ppermute(last, axis, up)  9.12 us
    ppermute x2, waiting for transfers between devices, with_halo(): after = lax.ppermute(leading, axis, down)  8.93 us
    all_to_all x1, starting transfers between devices, relay(): lax.all_to_all(pieces.reshape(ch_local, n_rows * n_cols, cells), ('ty', '...  7.09 us
    ppermute x2, waiting for transfers between devices, with_halo(): before = lax.ppermute(last, axis, up)  5.61 us
    dot_general x4, matrix products, local(): jnp.einsum('xk,ykc->yxc', col_band, rows_pass, preferred_element_type=jnp...  5.34 us
  transfers between devices with their start and end apart: 5, of which 4 were waited for; matrix products, arithmetic and copies ran while one was open for 8% of the time, Pallas kernels for 0%

commit v1 on v0

v1 whole, which is shorter than its diff:
```python
import functools

import jax
import jax.numpy as jnp
import numpy as np
from jax import lax
from jax.experimental import pallas as pl
from jax.experimental.pallas import tpu as pltpu
from jax.sharding import PartitionSpec as P

TILE_Y = 128
TILE_X = 16
NSC = 4
WMAX = 5
PT = 16
HALO = 9
SMAX = 3
LANES = 128
WIN_X = TILE_X + 2 * HALO
PACK = 7
HALO_GROUPS = (0, 10, 18)
GROUPS = TILE_X + 3
SIDE = 11
BF16 = jnp.bfloat16
F32 = jnp.float32
BIG = 3.3895313892515355e38
NT = (((1,), (1,)), ((), ()))


def column_group(x):
    return x + 1 if x < HALO else x + 2


def tap_table():
    offsets = np.arange(-HALO, HALO + 1).astype(np.float32)
    rows = []
    for sigma in range(1, SMAX + 1):
        spread = np.float32(sigma)
        weights = np.exp(-offsets * offsets / (np.float32(2.0) * spread * spread))
        weights = np.where(np.abs(offsets) <= 3.0 * spread, weights, np.float32(0.0)).astype(np.float32)
        rows.append(weights / np.sum(weights, dtype=np.float32))
    return rows


def rounded(value):
    return float(np.asarray(value, np.float32).astype(jnp.bfloat16).astype(np.float32))


def taps_at(diff, taps, sigma):
    total = jnp.zeros(diff.shape, F32)
    for k in range(-3 * sigma, 3 * sigma + 1):
        total = jnp.where(diff == k, F32(rounded(taps[k + HALO])), total)
    return total


def iota(shape, axis):
    return lax.broadcasted_iota(jnp.int32, shape, axis)


def tables_kernel(channels, taps_ref, main_ref, halo_ref, *rest):
    x_refs, box_ref = rest[:SMAX], rest[SMAX]
    taps = tap_table()
    for index in range(SMAX):
        sigma = index + 1
        rows = pl.ds(index * TILE_Y, TILE_Y)
        out_y, lane = iota((TILE_Y, LANES), 0), iota((TILE_Y, LANES), 1)
        main_ref[rows, :] = taps_at(lane - out_y, taps[index], sigma).astype(BF16)
        slot, part = lane // (2 * HALO), lane % (2 * HALO)
        in_y = jnp.where(part < HALO, part - HALO, part - HALO + TILE_Y)
        halo = taps_at(in_y - out_y, taps[index], sigma)
        for member in range(PACK):
            halo_ref[member, rows, :] = jnp.where(slot == member, halo, F32(0.0)).astype(BF16)
        shape = x_refs[index].shape
        row, col = iota(shape, 0), iota(shape, 1)
        weight = taps_at(col // PT - row % TILE_X - 3 * sigma, taps[index], sigma)
        x_refs[index][...] = jnp.where(row // TILE_X == col % PT, weight, F32(0.0)).astype(BF16)
    for scale in range(NSC):
        width, dilation = taps_ref[0, scale], taps_ref[1, scale]
        diff = iota((channels, channels), 0) - iota((channels, channels), 1)
        hit = jnp.zeros((channels, channels), F32)
        for step in range(WMAX):
            offset = jnp.where(step < width, dilation * (step - (width - 1) // 2), channels)
            hit = jnp.where(diff == offset, F32(1.0), hit)
        box_ref[scale] = hit.astype(BF16)


def tables(spectral_taps, channels):
    shapes = [(SMAX * TILE_Y, LANES), (PACK, SMAX * TILE_Y, LANES)]
    shapes += [(PT * TILE_X, (TILE_X + 6 * (i + 1)) * PT) for i in range(SMAX)]
    shapes += [(NSC, channels, channels)]
    return pl.pallas_call(
        functools.partial(tables_kernel, channels),
        out_shape=[jax.ShapeDtypeStruct(s, BF16) for s in shapes],
        in_specs=[pl.BlockSpec(memory_space=pltpu.SMEM)],
        out_specs=[pl.BlockSpec(memory_space=pltpu.VMEM)] * len(shapes),
        cost_estimate=pl.CostEstimate(flops=10**7, bytes_accessed=4 * 10**6, transcendentals=0),
        name="tables",
    )(spectral_taps)


def pack_kernel(cube_ref, mask_ref, out_ref, flat_ref):
    ch, ny, nx = cube_ref.shape
    n_rows, n_cols = ny // TILE_Y, nx // TILE_X
    lane_tile = iota((mask_ref.shape[0], nx), 1) // PT
    wide = jnp.zeros((mask_ref.shape[0], nx), F32)
    for j in range(mask_ref.shape[1]):
        column = jnp.broadcast_to(mask_ref[:, j : j + 1].astype(F32), wide.shape)
        wide = jnp.where(lane_tile == j, column, wide)
    mask = jnp.broadcast_to(wide[:, None, :], (ny // PT, PT, nx)).reshape(ny, nx)
    sums = []
    for c in range(ch):
        plane = jnp.where(mask > 0.5, cube_ref[c].astype(F32), F32(0.0))
        sums.append(jnp.sum(plane * plane, axis=0, keepdims=True))
        flat_ref[:, c * nx : (c + 1) * nx] = plane.astype(BF16)
    squares = jnp.minimum(jnp.sum(jnp.concatenate(sums, axis=0), axis=1, keepdims=True), F32(BIG))
    high = squares.astype(BF16).astype(F32)
    mid = (squares - high).astype(BF16).astype(F32)
    low = squares - high - mid

    x_row, x_col = iota((TILE_X * ch, nx), 0), iota((TILE_X * ch, nx), 1)
    code = (x_col - x_row // ch) * ch + x_row % ch
    blocks = [
        jnp.concatenate([jnp.where(code == t * TILE_X * ch + c, F32(1.0), F32(0.0)).astype(BF16) for c in range(ch)], axis=1)
        for t in range(n_cols)
    ]
    h_rows = len(HALO_GROUPS) * ch
    h_row, h_col = iota((h_rows, nx), 0), iota((h_rows, nx), 1)
    h_hit = jnp.where((h_col % TILE_X) // PACK == h_row // ch, h_col // TILE_X * ch + h_row % ch, -1)
    h_blocks = [
        jnp.concatenate([jnp.where(h_hit == t * ch + c, F32(1.0), F32(0.0)).astype(BF16) for c in range(ch)], axis=1)
        for t in range(n_cols)
    ]
    member = (iota((LANES, ch * nx), 1) % TILE_X) % PACK
    slot = iota((LANES, ch * nx), 0) // (2 * HALO)
    keep = member == slot
    spread_row, spread_col = iota((LANES, 2 * PT), 0), iota((LANES, 2 * PT), 1)
    part = spread_row % (2 * HALO)
    spread = jnp.where((spread_col == part + PT - HALO) & (spread_row < PACK * 2 * HALO), F32(1.0), F32(0.0)).astype(BF16)
    s_row, s_col = iota((h_rows, LANES), 0), iota((h_rows, LANES), 1)
    three = lambda value: jnp.concatenate([jnp.broadcast_to(value, (ch, LANES))] * len(HALO_GROUPS), axis=0)
    extra = jnp.where((s_row < ch) & (s_col == LANES - 2), three(high), F32(0.0))
    extra = jnp.where((s_row < ch) & (s_col == LANES - 1), three(mid), extra)
    extra = jnp.where((s_row >= ch) & (s_row < 2 * ch) & (s_col == LANES - 2), three(low), extra)

    zeros = jnp.zeros((PT, ch * nx), BF16)
    for r in range(n_rows):
        above = flat_ref[r * TILE_Y - PT : r * TILE_Y, :] if r else zeros
        below = flat_ref[(r + 1) * TILE_Y : (r + 1) * TILE_Y + PT, :] if r < n_rows - 1 else zeros
        edge = jnp.concatenate([above, below], axis=0)
        edges = jnp.dot(spread, edge, preferred_element_type=F32)
        edges = jnp.where(keep, edges, F32(0.0)).astype(BF16)
        here = flat_ref[r * TILE_Y : (r + 1) * TILE_Y, :]
        for t in range(n_cols):
            main = lax.dot_general(blocks[t], here, NT, preferred_element_type=F32).astype(BF16)
            halo = (lax.dot_general(h_blocks[t], edges, NT, preferred_element_type=F32) + extra).astype(BF16)
            dest = r * n_cols + t
            base = dest * GROUPS * ch
            cut = HALO * ch
            out_ref[dest, ch : ch + cut, :] = main[:cut]
            out_ref[dest, (HALO_GROUPS[1] + 1) * ch : HALO_GROUPS[2] * ch, :] = main[cut:]
            for index, group in enumerate(HALO_GROUPS):
                out_ref[dest, group * ch : (group + 1) * ch, :] = halo[index * ch : (index + 1) * ch]


def pack(cube, footprint):
    ch, ny, nx = cube.shape
    tiles = (ny // TILE_Y) * (nx // TILE_X)
    return pl.pallas_call(
        pack_kernel,
        out_shape=jax.ShapeDtypeStruct((tiles, GROUPS * ch, LANES), BF16),
        in_specs=[pl.BlockSpec(memory_space=pltpu.VMEM)] * 2,
        out_specs=pl.BlockSpec(memory_space=pltpu.VMEM),
        scratch_shapes=[pltpu.VMEM((ny, ch * nx), BF16)],
        name="pack",
    )(cube, footprint)


def main_kernel(
    sigma_ref, taps_ref, tile_mask_ref, footprint_ref, own_ref, left_ref, right_ref,
    main_ref, halo_ref, *rest,
):
    x_refs, box_ref = rest[:SMAX], rest[SMAX]
    out_ref, rows_ref, scale_ref = rest[SMAX + 1 :]
    senders, _, ch, _ = own_ref.shape
    channels = senders * ch
    part = min(senders, 256 // ch)
    step = pl.program_id(0)

    def load(ref, first, group):
        block = ref[pl.ds(first, part), group].astype(F32)
        return block.reshape(part * ch, LANES).astype(BF16)

    @pl.when(step == 0)
    def _():
        lane = iota((8, 2 * LANES), 1)
        pick = jnp.where((lane >= LANES - 2) & (lane <= LANES) | (lane == 2 * LANES - 2), F32(1.0), F32(0.0))
        pick = jnp.where(lane == LANES, F32(0.0), pick).astype(BF16)
        for first in range(0, senders, part):
            both = jnp.concatenate([load(own_ref, first, HALO_GROUPS[0]), load(own_ref, first, HALO_GROUPS[1])], axis=1)
            squares = lax.dot_general(pick, both, NT, preferred_element_type=F32)
            squares = jnp.where(squares >= F32(BIG), F32(jnp.inf), squares)
            count = jnp.maximum(jnp.sum(footprint_ref[...].astype(F32), keepdims=True) * F32(PT * PT), F32(1.0))
            noise = jnp.sqrt(squares / count + F32(1e-06))
            taps = tap_table()
            for scale in range(NSC):
                width = jnp.full(noise.shape, taps_ref[0, scale], jnp.int32).astype(F32)
                sigma = sigma_ref[scale]
                energy = [F32(float(np.sum(t * t, dtype=np.float32))) for t in taps]
                knorm = jnp.full(noise.shape, energy[0], F32)
                for index in range(1, SMAX):
                    knorm = jnp.where(sigma == index + 1, energy[index], knorm)
                knorm = knorm / jnp.sqrt(width)
                scale_ref[scale, :, first * ch : (first + part) * ch] = F32(1.0) / (noise * knorm * width)

        def y_pass(ref, first, group, halo_group, member, x):
            data = jnp.concatenate([load(ref, first, group), load(ref, first, halo_group)], axis=1)
            band = jnp.concatenate([main_ref[...], halo_ref[member]], axis=1)
            rows = lax.dot_general(band, data, NT, preferred_element_type=F32).astype(BF16)
            rows = rows.reshape(SMAX, TILE_Y // PT, PT, part * ch)
            rows_ref[:, :, x, :, first * ch : (first + part) * ch] = rows

        for first in range(0, senders, part):
            for ref, columns, base, at in (
                (left_ref, range(TILE_X - HALO, TILE_X), column_group(TILE_X - HALO), HALO - TILE_X),
                (own_ref, range(TILE_X), 0, HALO),
                (right_ref, range(HALO), 0, HALO + TILE_X),
            ):
                for x in columns:
                    y_pass(ref, first, column_group(x) - base, HALO_GROUPS[x // PACK] - base, x % PACK, x + at)

    seen = tile_mask_ref[step].astype(F32)
    smooth = []
    for index in range(SMAX):
        reach = 3 * (index + 1)
        slab = rows_ref[index, step, HALO - reach : HALO + TILE_X + reach]
        slab = slab.reshape((TILE_X + 2 * reach) * PT, channels)
        smooth.append(jnp.dot(x_refs[index][...], slab, preferred_element_type=F32))
    for scale in range(NSC):
        sigma = sigma_ref[scale]
        field = smooth[0]
        for index in range(1, SMAX):
            field = jnp.where(sigma == index + 1, smooth[index], field)
        boxed = jnp.dot(field.astype(BF16), box_ref[scale], preferred_element_type=F32)
        scaled = boxed * (scale_ref[scale, 0:1, :] * seen)
        out_ref[scale] = scaled.astype(BF16).reshape(PT, TILE_X, channels)


def finish(kernel_sigmas, spectral_taps, tile_mask, footprint, own, left, right, consts):
    senders, _, ch, _ = own.shape
    channels = senders * ch
    smem = pl.BlockSpec(memory_space=pltpu.SMEM)
    vmem = pl.BlockSpec(memory_space=pltpu.VMEM)
    return pl.pallas_call(
        main_kernel,
        grid=(TILE_Y // PT,),
        out_shape=jax.ShapeDtypeStruct((NSC, TILE_Y, TILE_X, channels), BF16),
        in_specs=[smem] * 3 + [vmem] * (4 + len(consts)),
        out_specs=pl.BlockSpec((NSC, PT, TILE_X, channels), lambda i: (0, i, 0, 0)),
        scratch_shapes=[
            pltpu.VMEM((SMAX, TILE_Y // PT, WIN_X, PT, channels), BF16),
            pltpu.VMEM((NSC, 8, channels), F32),
        ],
        compiler_params=pltpu.CompilerParams(vmem_limit_bytes=60 * 2**20),
        name="finish",
    )(kernel_sigmas, spectral_taps, tile_mask, footprint, own, left, right, *consts)


def local(channel_cube, footprint, kernel_sigmas, spectral_taps):
    n_cols = lax.axis_size("tx")
    ch = channel_cube.shape[0]
    channels = ch * lax.axis_size("ty") * n_cols
    packed = pack(channel_cube, footprint)
    own = lax.all_to_all(packed, ("ty", "tx"), split_axis=0, concat_axis=0, tiled=True)
    consts = tables(spectral_taps, channels)
    tile_rows = TILE_Y // PT
    tile_mask = lax.dynamic_slice(
        footprint, (lax.axis_index("ty") * tile_rows, lax.axis_index("tx") * (TILE_X // PT)), (tile_rows, 1)
    )[:, 0]
    up = [(i, i + 1) for i in range(n_cols - 1)]
    down = [(i + 1, i) for i in range(n_cols - 1)]
    left = lax.ppermute(own[:, (GROUPS - SIDE) * ch :], "tx", up)
    right = lax.ppermute(own[:, : SIDE * ch], "tx", down)
    split = lambda block: block.reshape(block.shape[0], -1, ch, LANES)
    return finish(kernel_sigmas, spectral_taps, tile_mask, footprint, split(own), split(left), split(right), consts)


def solution(mesh):
    placed = (P(("ty", "tx"), None, None), P(), P(), P())
    return jax.shard_map(
        local, mesh=mesh, in_specs=placed, out_specs=P(None, "ty", "tx", None), check_vma=False
    )
```

time: 177 us -> 75.7 us (0.43)
  between operations: 37 us -> 0.03 us
  other arithmetic: 29.4 us -> 0 us
  Pallas kernels: 0 us -> 24.2 us
  local copies, waits for them, and re-layouts: 26 us -> 4.55 us
  starting transfers between devices: 19.6 us -> 5.55 us
  waiting for transfers between devices: 14.5 us -> 2.32 us
  matrix products: 10.3 us -> 0 us
    unnamed x1 -> x0, blocking collectives: 39.2 us -> none
    all_to_all x0 -> x1, blocking collectives: none -> 38.7 us  [local(): lax.all_to_all(packed, ('ty', 'tx'), split_axis=0, concat_axis=0, tiled=T...]
    pallas_call x0 -> x3, Pallas kernels: none -> 24.2 us  [the longest x1 11.8 us: finish(): pl.pallas_call(main_kernel, grid=(TILE_Y // PT,), out_shape=jax.ShapeDtyp...]
    another operation x2 -> x0, local copies, waits for them, and re-layouts: 21.6 us -> none  [relay(): pieces.reshape(ch_local, n_rows * n_cols, cells)]
    another operation x5 -> x0, other arithmetic: 15.7 us -> none  [local(): return jnp.stack(results)]
    ppermute x4 -> x2, waiting for transfers between devices: 14.5 us -> 2.32 us  [the longest x1 1.18 us: local(): left = lax.ppermute(own[:, (GROUPS - SIDE) * ch:], 'tx', up)]
    dot_general x8 -> x0, matrix products: 10.3 us -> none  [the longest x4 5.34 us: local(): jnp.einsum('xk,ykc->yxc', col_band, rows_pass, preferred_element_type=jnp...]
    reduce_sum x12 -> x0, other arithmetic: 9.87 us -> none  [the longest x4 5.12 us: local(): knorm = jnp.sum(taps * taps) / jnp.sqrt(width.astype(jnp.float32))]
  transfers between devices with their start and end apart: 5 -> 2, of which waited for: 4 -> 2; matrix products, arithmetic and copies ran while one was open for 8% -> 2% of each run, Pallas kernels for 0% -> 6%
where the time goes in v1:
time: 75.7 us; the launch traced here: 75.3 us
  blocking collectives  38.7 us (51%)
  Pallas kernels  24.2 us (32%)
  starting transfers between devices  5.55 us (7%)
  local copies, waits for them, and re-layouts  4.55 us (6%)
  waiting for transfers between devices  2.32 us (3%)
    all_to_all x1, blocking collectives, local(): lax.all_to_all(packed, ('ty', 'tx'), split_axis=0, concat_axis=0, tiled=T...  38.7 us
    pallas_call x1, Pallas kernels, finish(): pl.pallas_call(main_kernel, grid=(TILE_Y // PT,), out_shape=jax.ShapeDtyp...  11.8 us
    pallas_call x1, Pallas kernels, pack(): pl.pallas_call(pack_kernel, out_shape=jax.ShapeDtypeStruct((tiles, GROUPS...  7.72 us
    pallas_call x1, Pallas kernels, tables(): pl.pallas_call(functools.partial(tables_kernel, channels), out_shape=[jax...  4.65 us
    ppermute x1, starting transfers between devices, local(): left = lax.ppermute(own[:, (GROUPS - SIDE) * ch:], 'tx', up)  3.34 us
    unnamed x7, local copies, waits for them, and re-layouts  3.21 us
    ppermute x1, starting transfers between devices, local(): right = lax.ppermute(own[:, :SIDE * ch], 'tx', down)  2.21 us
  transfers between devices with their start and end apart: 2, of which 2 were waited for; matrix products, arithmetic and copies ran while one was open for 2% of the time, Pallas kernels for 6%

profile of v1, /device:TPU:1, one launch (start us, length us, event | category | flops | bytes accessed | tf_op | source)
XLA Modules:
  0.0 75.3 jit_solution(17065841843848021350)
XLA Ops:
  0.0 1.4 %copy.6.mask_ref.footprint_ref = s32[32,8]{1,0:T(8,128)} copy(s32[32,8]{0,1:T(8,128)} %param.5) | data formatting | bytes 2048 | tf_op args[1]
  1.4 7.7 %pack.1 = bf16[32,152,128]{2,1,0:T(8,128)(2,1)} custom-call(bf16[8,512,128]{2,1,0:T(8,128)(2,1)} %cube_ref.1, s32[32,8]{1,0:T(8,128)} %copy.6.mask_ref.footprint_ref), custom_call_target="tpu_custom_call" | custom-call | tf_op jit(solution)/shard_map/pack/pallas_call | solution.py:168
  9.1 38.7 %all_to_all.5 = bf16[32,152,128]{2,1,0:T(8,128)(2,1)S(1)} all-to-all(bf16[32,152,128]{2,1,0:T(8,128)(2,1)} %pack.1), channel_id=1, replica_groups=mesh['ty'=4,'tx'=8] {'ty','tx'}, dimensions={0} | all-to-all | bytes 2490368 | tf_op jit(solution)/shard_map/all_to_all | solution.py:273
  47.8 0.0 copy-start
  47.8 0.1 fusion
  47.9 0.9 %copy-done = bf16[32,152,128]{2,1,0:T(8,128)(2,1)} copy-done((bf16[32,152,128]{2,1,0:T(8,128)(2,1)}, bf16[32,152,128]{2,1,0:T(8,128)(2,1)S(1)}, u32[]{:S(2)}) %copy-start) | copy-done | bytes 1245208
  48.8 2.2 %collective-permute-start.1 = (bf16[32,88,128]{2,1,0:T(8,128)(2,1)S(1)}, bf16[32,88,128]{2,1,0:T(8,128)(2,1)S(1)}, u32[]{:S(2)}, u32[]{:S(2)}) collective-permute-start(bf16[32,88,128]{2,1,0:T(8,128)(2,1)S(1)} %get-tuple-element.17), channel_id=1, source_target_pairs={{1,0},{2,1},{3,2},{4,3},{5,4},{6,5},{7,6},{9,8},{10,9},{11,10},{12... | collective-permute-start | bytes 2162696 | tf_op jit(solution)/shard_map/ppermute | solution.py:282
  51.1 3.3 %collective-permute-start = (bf16[32,88,128]{2,1,0:T(8,128)(2,1)S(1)}, bf16[32,88,128]{2,1,0:T(8,128)(2,1)S(1)}, u32[]{:S(2)}, u32[]{:S(2)}) collective-permute-start(bf16[32,88,128]{2,1,0:T(8,128)(2,1)S(1)} %get-tuple-element.18), channel_id=1, source_target_pairs={{0,1},{1,2},{2,3},{3,4},{4,5},{5,6},{6,7},{8,9},{9,10},{10,11},{11... | collective-permute-start | bytes 2162696 | tf_op jit(solution)/shard_map/ppermute | solution.py:281
  54.4 4.7 %tables.1 = (bf16[384,128]{1,0:T(8,128)(2,1)}, bf16[7,384,128]{2,1,0:T(8,128)(2,1)}, bf16[256,352]{1,0:T(8,128)(2,1)}, bf16[256,448]{1,0:T(8,128)(2,1)}, bf16[25...) custom-call(s32[2,4]{1,0:T(2,128)} %taps_ref.3), custom_call_target="tpu_custom_call" | custom-call | flops 10000000 | bytes 4000000 | tf_op jit(solution)/shard_map/tables/pallas_call | solution.py:91
  59.1 1.2 %dynamic-slice_bitcast_fusion.tile_mask_ref = s32[8]{0:T(128)} fusion(s32[32,8]{0,1:T(8,128)} %param.5, s32[]{:T(128)S(6)} %select_n.6, s32[]{:T(128)S(6)} %select_n.7), kind=kLoop, calls=%fused_computation | loop fusion | bytes 72 | tf_op jit(solution)/shard_map/squeeze | solution.py:276
  60.3 1.1 %collective-permute-done.1 = bf16[32,88,128]{2,1,0:T(8,128)(2,1)S(1)} collective-permute-done((bf16[32,88,128]{2,1,0:T(8,128)(2,1)S(1)}, bf16[32,88,128]{2,1,0:T(8,128)(2,1)S(1)}, u32[]{:S(2)}, u32[]{:S(2)}) %collective-permute-start.1) | collective-permute-done | bytes 720928 | tf_op jit(solution)/shard_map/ppermute | solution.py:282
  61.4 0.0 copy-start.1
  61.4 1.2 %collective-permute-done = bf16[32,88,128]{2,1,0:T(8,128)(2,1)S(1)} collective-permute-done((bf16[32,88,128]{2,1,0:T(8,128)(2,1)S(1)}, bf16[32,88,128]{2,1,0:T(8,128)(2,1)S(1)}, u32[]{:S(2)}, u32[]{:S(2)}) %collective-permute-start) | collective-permute-done | bytes 720928 | tf_op jit(solution)/shard_map/ppermute | solution.py:281
  62.6 0.0 copy-start.2
  62.6 0.0 copy-done.1
  62.6 0.9 %copy-done.2 = bf16[32,88,128]{2,1,0:T(8,128)(2,1)} copy-done((bf16[32,88,128]{2,1,0:T(8,128)(2,1)}, bf16[32,88,128]{2,1,0:T(8,128)(2,1)S(1)}, u32[]{:S(2)}) %copy-start.2) | copy-done | bytes 720920
  63.5 11.8 %finish.1 = bf16[4,128,16,256]{3,2,1,0:T(8,128)(2,1)} custom-call(s32[4]{0:T(128)} %sigma_ref.1, s32[2,4]{1,0:T(2,128)} %taps_ref.3, s32[8]{0:T(128)} %dynamic-slice_bitcast_fusion.tile_mask_ref, s32[32,8]{1,0:T(8,128)} %copy.6.mask_ref.footprint_ref, bf16[32,19,8,128]{3,2,1,0:T(8,128)(2,1)} %bitcast.5, bf16[32,11,8,128]{3,2,1,0:T(8,128)(2,1)} %bitcast.7, ...), custom_call_target="tpu_custom_call" | custom-call | tf_op jit(solution)/shard_map/finish/pallas_call | solution.py:253
Async XLA Ops:
  47.8 1.0 %copy-start = (bf16[32,152,128]{2,1,0:T(8,128)(2,1)}, bf16[32,152,128]{2,1,0:T(8,128)(2,1)S(1)}, u32[]{:S(2)}) copy-start(bf16[32,152,128]{2,1,0:T(8,128)(2,1)S(1)} %all_to_all.5) | copy-start | bytes 3735556
  48.8 12.6 %collective-permute-start.1 = (bf16[32,88,128]{2,1,0:T(8,128)(2,1)S(1)}, bf16[32,88,128]{2,1,0:T(8,128)(2,1)S(1)}, u32[]{:S(2)}, u32[]{:S(2)}) collective-permute-start(bf16[32,88,128]{2,1,0:T(8,128)(2,1)S(1)} %get-tuple-element.17), channel_id=1, source_target_pairs={{1,0},{2,1},{3,2},{4,3},{5,4},{6,5},{7,6},{9,8},{10,9},{11,10},{12... | collective-permute-start | bytes 2162696 | tf_op jit(solution)/shard_map/ppermute | solution.py:282
  51.1 11.6 %collective-permute-start = (bf16[32,88,128]{2,1,0:T(8,128)(2,1)S(1)}, bf16[32,88,128]{2,1,0:T(8,128)(2,1)S(1)}, u32[]{:S(2)}, u32[]{:S(2)}) collective-permute-start(bf16[32,88,128]{2,1,0:T(8,128)(2,1)S(1)} %get-tuple-element.18), channel_id=1, source_target_pairs={{0,1},{1,2},{2,3},{3,4},{4,5},{5,6},{6,7},{8,9},{9,10},{10,11},{11... | collective-permute-start | bytes 2162696 | tf_op jit(solution)/shard_map/ppermute | solution.py:281
  61.4 1.2 %copy-start.1 = (bf16[32,88,128]{2,1,0:T(8,128)(2,1)}, bf16[32,88,128]{2,1,0:T(8,128)(2,1)S(1)}, u32[]{:S(2)}) copy-start(bf16[32,88,128]{2,1,0:T(8,128)(2,1)S(1)} %collective-permute-done.1) | copy-start | bytes 2162692
  62.6 0.9 %copy-start.2 = (bf16[32,88,128]{2,1,0:T(8,128)(2,1)}, bf16[32,88,128]{2,1,0:T(8,128)(2,1)S(1)}, u32[]{:S(2)}) copy-start(bf16[32,88,128]{2,1,0:T(8,128)(2,1)S(1)} %collective-permute-done) | copy-start | bytes 2162692

commit v2 on v1

v2 whole, which is shorter than its diff:
```python
import functools

import jax
import jax.numpy as jnp
import numpy as np
from jax import lax
from jax.experimental import pallas as pl
from jax.experimental.pallas import tpu as pltpu
from jax.sharding import PartitionSpec as P

TILE_Y = 128
TILE_X = 16
NSC = 4
WMAX = 5
PT = 16
HALO = 9
SMAX = 3
LANES = 128
WIN_X = TILE_X + 2 * HALO
PACK = 7
HALO_GROUPS = (0, 10, 18)
GROUPS = TILE_X + 3
SIDE = 11
SPAN = 4
WIDE = 256
BF16 = jnp.bfloat16
F32 = jnp.float32
BIG = 3.3895313892515355e38
NT = (((1,), (1,)), ((), ()))


def column_group(x):
    return x + 1 if x < HALO else x + 2


def tap_table():
    offsets = np.arange(-HALO, HALO + 1).astype(np.float32)
    rows = []
    for sigma in range(1, SMAX + 1):
        spread = np.float32(sigma)
        weights = np.exp(-offsets * offsets / (np.float32(2.0) * spread * spread))
        weights = np.where(np.abs(offsets) <= 3.0 * spread, weights, np.float32(0.0)).astype(np.float32)
        rows.append(weights / np.sum(weights, dtype=np.float32))
    return rows


def rounded(value):
    return float(np.asarray(value, np.float32).astype(jnp.bfloat16).astype(np.float32))


def taps_at(diff, taps, sigma):
    total = jnp.zeros(diff.shape, F32)
    for k in range(-3 * sigma, 3 * sigma + 1):
        total = jnp.where(diff == k, F32(rounded(taps[k + HALO])), total)
    return total


def margin(channels):
    return 0 if channels <= WIDE else LANES


def in_hbm(x):
    return pltpu.with_memory_space_constraint(x, pltpu.MemorySpace.HBM)


def iota(shape, axis):
    return lax.broadcasted_iota(jnp.int32, shape, axis)


def tables_kernel(channels, taps_ref, main_ref, halo_ref, *rest):
    x_refs, box_ref = rest[:SMAX], rest[SMAX]
    taps = tap_table()
    for index in range(SMAX):
        sigma = index + 1
        rows = pl.ds(index * TILE_Y, TILE_Y)
        out_y, lane = iota((TILE_Y, LANES), 0), iota((TILE_Y, LANES), 1)
        main_ref[rows, :] = taps_at(lane - out_y, taps[index], sigma).astype(BF16)
        slot, part = lane // (2 * HALO), lane % (2 * HALO)
        in_y = jnp.where(part < HALO, part - HALO, part - HALO + TILE_Y)
        halo = taps_at(in_y - out_y, taps[index], sigma)
        for member in range(PACK):
            halo_ref[member, rows, :] = jnp.where(slot == member, halo, F32(0.0)).astype(BF16)
        shape = x_refs[index].shape
        row, col = iota(shape, 0), iota(shape, 1)
        weight = taps_at(col // PT - row % TILE_X - 3 * sigma, taps[index], sigma)
        x_refs[index][...] = jnp.where(row // TILE_X == col % PT, weight, F32(0.0)).astype(BF16)
    for scale in range(NSC):
        width, dilation = taps_ref[0, scale], taps_ref[1, scale]
        shape = box_ref.shape[1:]
        diff = iota(shape, 0) - (shape[0] - shape[1]) // 2 - iota(shape, 1)
        hit = jnp.zeros(shape, F32)
        for step in range(WMAX):
            offset = jnp.where(step < width, dilation * (step - (width - 1) // 2), 2 * channels)
            hit = jnp.where(diff == offset, F32(1.0), hit)
        box_ref[scale] = hit.astype(BF16)


def tables(spectral_taps, channels):
    shapes = [(SMAX * TILE_Y, LANES), (PACK, SMAX * TILE_Y, LANES)]
    shapes += [(PT * TILE_X, (TILE_X + 6 * (i + 1)) * PT) for i in range(SMAX)]
    wide = min(channels, WIDE)
    shapes += [(NSC, wide + 2 * margin(channels), wide)]
    return pl.pallas_call(
        functools.partial(tables_kernel, channels),
        out_shape=[jax.ShapeDtypeStruct(s, BF16) for s in shapes],
        in_specs=[pl.BlockSpec(memory_space=pltpu.SMEM)],
        out_specs=[pl.BlockSpec(memory_space=pltpu.VMEM)] * len(shapes),
        compiler_params=pltpu.CompilerParams(vmem_limit_bytes=16 * 2**20),
        cost_estimate=pl.CostEstimate(flops=10**7, bytes_accessed=4 * 10**6, transcendentals=0),
        name="tables",
    )(spectral_taps)


def pack_kernel(cube_ref, cover_hbm, out_ref, land_ref, cover_ref, flat_ref, perm_ref, pick_ref, edge_ref, sems):
    ch, ny, nx = cube_ref.shape
    n_rows, n_cols = ny // TILE_Y, nx // TILE_X
    copies = [pltpu.make_async_copy(cube_ref.at[c], land_ref.at[c], sems.at[c]) for c in range(ch)]
    cover_copy = pltpu.make_async_copy(cover_hbm, cover_ref, sems.at[ch])
    cover_copy.start()
    for copy in copies:
        copy.start()

    block = TILE_X * ch
    x_row, x_col = iota((block, nx), 0), iota((block, nx), 1)
    code = (x_col - x_row // ch) * ch + x_row % ch
    h_rows = len(HALO_GROUPS) * ch
    h_row, h_col = iota((h_rows, nx), 0), iota((h_rows, nx), 1)
    h_code = jnp.where((h_col % TILE_X) // PACK == h_row // ch, h_col // TILE_X * ch + h_row % ch, -1)
    for t in range(n_cols):
        for c in range(ch):
            lanes = slice(c * nx, (c + 1) * nx)
            perm_ref[t * block : (t + 1) * block, lanes] = jnp.where(code == t * block + c, F32(1.0), F32(0.0)).astype(BF16)
            pick_ref[t * h_rows : (t + 1) * h_rows, lanes] = jnp.where(h_code == t * ch + c, F32(1.0), F32(0.0)).astype(BF16)

    cover_copy.wait()
    tile_x, tile_y = cover_ref.shape
    eye = jnp.where(iota((tile_y, tile_y), 0) == iota((tile_y, tile_y), 1), F32(1.0), F32(0.0)).astype(BF16)
    cover = lax.dot_general(eye, cover_ref[...].astype(F32).astype(BF16), NT, preferred_element_type=F32)
    lane_tile = iota((tile_y, nx), 1) // PT
    wide = jnp.zeros((tile_y, nx), F32)
    for j in range(tile_x):
        wide = jnp.where(lane_tile == j, jnp.broadcast_to(cover[:, j : j + 1], wide.shape), wide)
    mask = jnp.broadcast_to(wide[:, None, :], (tile_y, PT, nx)).reshape(ny, nx) > 0.5
    sums = []
    for c in range(ch):
        copies[c].wait()
        plane = jnp.where(mask, land_ref[c].astype(F32), F32(0.0))
        sums.append(jnp.sum(plane * plane, axis=0, keepdims=True))
        flat_ref[:, c * nx : (c + 1) * nx] = plane.astype(BF16)

    cut = HALO * ch
    for first in range(0, n_rows, 2):
        pair = range(first, min(first + 2, n_rows))
        here = flat_ref[first * TILE_Y : (pair[-1] + 1) * TILE_Y, :]
        main = lax.dot_general(perm_ref[...], here, NT, preferred_element_type=F32).astype(BF16)
        for r in pair:
            lanes = slice((r - first) * TILE_Y, (r - first + 1) * TILE_Y)
            for t in range(n_cols):
                tile = main[t * block : (t + 1) * block, lanes]
                out_ref[r * n_cols + t, ch : ch + cut, :] = tile[:cut]
                out_ref[r * n_cols + t, (HALO_GROUPS[1] + 1) * ch : HALO_GROUPS[2] * ch, :] = tile[cut:]

    squares = jnp.minimum(jnp.sum(jnp.concatenate(sums, axis=0), axis=1, keepdims=True), F32(BIG))
    high = squares.astype(BF16).astype(F32)
    mid = (squares - high).astype(BF16).astype(F32)
    low = squares - high - mid
    keep = (iota((LANES, ch * nx), 1) % TILE_X) % PACK == iota((LANES, ch * nx), 0) // (2 * HALO)
    spread_row, spread_col = iota((LANES, 2 * PT), 0), iota((LANES, 2 * PT), 1)
    part = spread_row % (2 * HALO)
    spread = jnp.where((spread_col == part + PT - HALO) & (spread_row < PACK * 2 * HALO), F32(1.0), F32(0.0)).astype(BF16)
    s_row, s_col = iota((h_rows, LANES), 0), iota((h_rows, LANES), 1)
    three = lambda value: jnp.concatenate([jnp.broadcast_to(value, (ch, LANES))] * len(HALO_GROUPS), axis=0)
    extra = jnp.where((s_row < ch) & (s_col == LANES - 2), three(high), F32(0.0))
    extra = jnp.where((s_row < ch) & (s_col == LANES - 1), three(mid), extra)
    extra = jnp.where((s_row >= ch) & (s_row < 2 * ch) & (s_col == LANES - 2), three(low), extra)
    zeros = jnp.zeros((PT, ch * nx), BF16)
    for r in range(n_rows):
        above = flat_ref[r * TILE_Y - PT : r * TILE_Y, :] if r else zeros
        below = flat_ref[(r + 1) * TILE_Y : (r + 1) * TILE_Y + PT, :] if r < n_rows - 1 else zeros
        edge = jnp.dot(spread, jnp.concatenate([above, below], axis=0), preferred_element_type=F32)
        edge_ref[r * LANES : (r + 1) * LANES, :] = jnp.where(keep, edge, F32(0.0)).astype(BF16)
    halos = lax.dot_general(pick_ref[...], edge_ref[...], NT, preferred_element_type=F32)
    for r in range(n_rows):
        for t in range(n_cols):
            halo = (halos[t * h_rows : (t + 1) * h_rows, r * LANES : (r + 1) * LANES] + extra).astype(BF16)
            for index, group in enumerate(HALO_GROUPS):
                out_ref[r * n_cols + t, group * ch : (group + 1) * ch, :] = halo[index * ch : (index + 1) * ch]


def pack(cube, footprint):
    ch, ny, nx = cube.shape
    n_rows, n_cols = ny // TILE_Y, nx // TILE_X
    h_rows = len(HALO_GROUPS) * ch
    need = 2 * (4 * ch * ny * nx + (n_cols * (TILE_X * ch + h_rows) + n_rows * LANES) * ch * nx)
    return pl.pallas_call(
        pack_kernel,
        out_shape=jax.ShapeDtypeStruct((n_rows * n_cols, GROUPS * ch, LANES), BF16),
        in_specs=[pl.BlockSpec(memory_space=pltpu.MemorySpace.HBM)] * 2,
        out_specs=pl.BlockSpec(memory_space=pltpu.VMEM),
        scratch_shapes=[
            pltpu.VMEM((ch, ny, nx), BF16),
            pltpu.VMEM((nx // PT, ny // PT), jnp.int32),
            pltpu.VMEM((ny, ch * nx), BF16),
            pltpu.VMEM((n_cols * TILE_X * ch, ch * nx), BF16),
            pltpu.VMEM((n_cols * h_rows, ch * nx), BF16),
            pltpu.VMEM((n_rows * LANES, ch * nx), BF16),
            pltpu.SemaphoreType.DMA((ch + 1,)),
        ],
        compiler_params=pltpu.CompilerParams(vmem_limit_bytes=min(need + 12 * 2**20, 62 * 2**20)),
        name="pack",
    )(in_hbm(cube), in_hbm(footprint.T))


def main_kernel(
    sigma_ref, taps_ref, tile_mask_ref, footprint_ref, own_ref, left_ref, right_ref,
    main_ref, halo_ref, *rest,
):
    x_refs, box_ref = rest[:SMAX], rest[SMAX]
    out_ref, rows_ref, scale_ref, stage_ref, sems = rest[SMAX + 1 : SMAX + 6]
    smooth_refs = rest[SMAX + 6 :]
    senders, _, ch, _ = own_ref.shape
    channels = senders * ch
    part = min(senders, WIDE // ch)

    def load(ref, first, group):
        block = ref[pl.ds(first, part), group].astype(F32)
        return block.reshape(part * ch, LANES).astype(BF16)

    lane = iota((8, 2 * LANES), 1)
    pick = jnp.where((lane >= LANES - 2) & (lane <= LANES) | (lane == 2 * LANES - 2), F32(1.0), F32(0.0))
    pick = jnp.where(lane == LANES, F32(0.0), pick).astype(BF16)
    for first in range(0, senders, part):
        both = jnp.concatenate([load(own_ref, first, HALO_GROUPS[0]), load(own_ref, first, HALO_GROUPS[1])], axis=1)
        squares = lax.dot_general(pick, both, NT, preferred_element_type=F32)
        squares = jnp.where(squares >= F32(BIG), F32(jnp.inf), squares)
        count = jnp.maximum(jnp.sum(footprint_ref[...].astype(F32), keepdims=True) * F32(PT * PT), F32(1.0))
        noise = jnp.sqrt(squares / count + F32(1e-06))
        taps = tap_table()
        for scale in range(NSC):
            width = jnp.full(noise.shape, taps_ref[0, scale], jnp.int32).astype(F32)
            sigma = sigma_ref[scale]
            energy = [F32(float(np.sum(t * t, dtype=np.float32))) for t in taps]
            knorm = jnp.full(noise.shape, energy[0], F32)
            for index in range(1, SMAX):
                knorm = jnp.where(sigma == index + 1, energy[index], knorm)
            knorm = knorm / jnp.sqrt(width)
            scale_ref[scale, :, first * ch : (first + part) * ch] = F32(1.0) / (noise * knorm * width)

    def y_pass(ref, first, group, halo_group, member, x):
        data = jnp.concatenate([load(ref, first, group), load(ref, first, halo_group)], axis=1)
        band = jnp.concatenate([main_ref[...], halo_ref[member]], axis=1)
        rows = lax.dot_general(band, data, NT, preferred_element_type=F32).astype(BF16)
        rows = rows.reshape(SMAX, TILE_Y // PT, PT, part * ch)
        rows_ref[:, :, x, :, first * ch : (first + part) * ch] = rows

    for first in range(0, senders, part):
        for ref, columns, base, at in (
            (left_ref, range(TILE_X - HALO, TILE_X), column_group(TILE_X - HALO), HALO - TILE_X),
            (own_ref, range(TILE_X), 0, HALO),
            (right_ref, range(HALO), 0, HALO + TILE_X),
        ):
            for x in columns:
                y_pass(ref, first, column_group(x) - base, HALO_GROUPS[x // PACK] - base, x % PACK, x + at)

    slots, _, tall = stage_ref.shape[:3]
    span, phases = tall // PT, TILE_Y // tall
    wide, edge = min(channels, WIDE), margin(channels)

    def out_copy(phase, slot, scale):
        there = out_ref.at[scale, pl.ds(phase * tall, tall)]
        return pltpu.make_async_copy(stage_ref.at[slot, scale], there, sems.at[slot, scale])

    def x_pass(phase, smooth_ref):
        for kind in range(SMAX):
            reach = 3 * (kind + 1)
            for row in range(span):
                for at in range(0, channels, wide):
                    lanes = slice(at, at + wide)
                    slab = rows_ref[kind, phase * span + row, HALO - reach : HALO + TILE_X + reach, :, lanes]
                    slab = slab.reshape((TILE_X + 2 * reach) * PT, wide)
                    field = jnp.dot(x_refs[kind][...], slab, preferred_element_type=F32)
                    smooth_ref[kind, row, :, lanes] = field.astype(BF16)

    def box_pass(phase, slot, smooth_ref, reused):
        for scale in range(NSC):
            if reused:
                out_copy(phase - slots, slot, scale).wait()
            for row in range(span):
                seen = tile_mask_ref[phase * span + row].astype(F32)
                for at in range(0, channels, wide):
                    lanes, first = slice(at, at + wide), at - edge
                    low, high = max(first, 0), min(at + wide + edge, channels)
                    field = smooth_ref[sigma_ref[scale] - 1, row, :, low:high]
                    boxed = jnp.dot(field, box_ref[scale, low - first : high - first], preferred_element_type=F32)
                    scaled = (boxed * (scale_ref[scale, 0:1, lanes] * seen)).astype(BF16)
                    stage_ref[slot, scale, row * PT : (row + 1) * PT, :, lanes] = scaled.reshape(PT, TILE_X, wide)
            out_copy(phase, slot, scale).start()

    for phase in range(slots):
        x_pass(phase, smooth_refs[phase])
        box_pass(phase, phase, smooth_refs[phase], False)

    def again(phase, carry):
        x_pass(phase, smooth_refs[0])
        box_pass(phase, lax.rem(phase, slots), smooth_refs[0], True)
        return carry

    if phases > slots:
        lax.fori_loop(slots, phases, again, 0)
    for phase in range(phases - slots, phases):
        for scale in range(NSC):
            out_copy(phase, phase % slots, scale).wait()


def finish(kernel_sigmas, spectral_taps, tile_mask, footprint, own, left, right, consts):
    senders, _, ch, _ = own.shape
    channels = senders * ch
    span, slots = (SPAN, TILE_Y // PT // SPAN) if channels <= WIDE else (1, 2)
    need = 2 * channels * (SMAX * TILE_Y * WIN_X + slots * span * (NSC + SMAX) * PT * TILE_X)
    smem = pl.BlockSpec(memory_space=pltpu.SMEM)
    vmem = pl.BlockSpec(memory_space=pltpu.VMEM)
    return pl.pallas_call(
        main_kernel,
        out_shape=jax.ShapeDtypeStruct((NSC, TILE_Y, TILE_X, channels), BF16),
        in_specs=[smem] * 3 + [vmem] * (4 + len(consts)),
        out_specs=pl.BlockSpec(memory_space=pltpu.MemorySpace.HBM),
        scratch_shapes=[
            pltpu.VMEM((SMAX, TILE_Y // PT, WIN_X, PT, channels), BF16),
            pltpu.VMEM((NSC, 8, channels), F32),
            pltpu.VMEM((slots, NSC, span * PT, TILE_X, channels), BF16),
            pltpu.SemaphoreType.DMA((slots, NSC)),
        ]
        + [pltpu.VMEM((SMAX, span, PT * TILE_X, channels), BF16)] * slots,
        compiler_params=pltpu.CompilerParams(vmem_limit_bytes=need + 6 * 2**20 if channels <= WIDE else 62 * 2**20),
        name="finish",
    )(kernel_sigmas, spectral_taps, tile_mask, footprint.T, own, left, right, *consts)


def local(channel_cube, footprint, kernel_sigmas, spectral_taps):
    n_cols = lax.axis_size("tx")
    ch = channel_cube.shape[0]
    channels = ch * lax.axis_size("ty") * n_cols
    packed = pack(channel_cube, footprint)
    own = lax.all_to_all(packed, ("ty", "tx"), split_axis=0, concat_axis=0, tiled=True)
    consts = tables(spectral_taps, channels)
    tile_rows = TILE_Y // PT
    tile_mask = lax.dynamic_slice(
        footprint, (lax.axis_index("ty") * tile_rows, lax.axis_index("tx") * (TILE_X // PT)), (tile_rows, 1)
    )[:, 0]
    up = [(i, i + 1) for i in range(n_cols - 1)]
    down = [(i + 1, i) for i in range(n_cols - 1)]
    left = lax.ppermute(own[:, (GROUPS - SIDE) * ch :], "tx", up)
    right = lax.ppermute(own[:, : SIDE * ch], "tx", down)
    split = lambda block: block.reshape(block.shape[0], -1, ch, LANES)
    return finish(kernel_sigmas, spectral_taps, tile_mask, footprint, split(own), split(left), split(right), consts)


def solution(mesh):
    placed = (P(("ty", "tx"), None, None), P(), P(), P())
    return jax.shard_map(
        local, mesh=mesh, in_specs=placed, out_specs=P(None, "ty", "tx", None), check_vma=False
    )
```

time: 75.7 us -> 63.9 us (0.84)
  Pallas kernels: 24.2 us -> 13.8 us
  local copies, waits for them, and re-layouts: 4.55 us -> 1.05 us
  waiting for transfers between devices: 2.32 us -> 4.61 us
    pallas_call x2, Pallas kernels: 19.5 us -> 10.4 us  [the longest x1 6.83 us: finish(): pl.pallas_call(main_kernel, out_shape=jax.ShapeDtypeStruct((NSC, TILE_Y,...]
    unnamed x7 -> x6, local copies, waits for them, and re-layouts: 3.21 us -> 0.01 us
    ppermute x1, waiting for transfers between devices: 1.14 us -> 3.63 us  [local(): right = lax.ppermute(own[:, :SIDE * ch], 'tx', down)]
    pallas_call x1, Pallas kernels: 4.65 us -> 3.49 us  [tables(): pl.pallas_call(functools.partial(tables_kernel, channels), out_shape=[jax...]
    squeeze x1, local copies, waits for them, and re-layouts: 1.24 us -> 0.08 us  [local(): lax.dynamic_slice(footprint, (lax.axis_index('ty') * tile_rows, lax.axis_...]
    slice x1, local copies, waits for them, and re-layouts: 0.11 us -> 0.96 us  [local(): right = lax.ppermute(own[:, :SIDE * ch], 'tx', down)]
  transfers between devices with their start and end apart: 2 -> 2, of which waited for: 2 -> 2; matrix products, arithmetic and copies ran while one was open for 2% -> 0% of each run, Pallas kernels for 6% -> 5%
where the time goes in v2:
time: 63.9 us; the launch traced here: 63.6 us
  blocking collectives  38.5 us (60%)
  Pallas kernels  13.8 us (22%)
  starting transfers between devices  5.55 us (9%)
  waiting for transfers between devices  4.61 us (7%)
  local copies, waits for them, and re-layouts  1.05 us (2%)
    all_to_all x1, blocking collectives, local(): lax.all_to_all(packed, ('ty', 'tx'), split_axis=0, concat_axis=0, tiled=T...  38.5 us
    pallas_call x1, Pallas kernels, finish(): pl.pallas_call(main_kernel, out_shape=jax.ShapeDtypeStruct((NSC, TILE_Y,...  6.83 us
    ppermute x1, waiting for transfers between devices, local(): right = lax.ppermute(own[:, :SIDE * ch], 'tx', down)  3.63 us
    pallas_call x1, Pallas kernels, pack(): pl.pallas_call(pack_kernel, out_shape=jax.ShapeDtypeStruct((n_rows * n_co...  3.53 us
    pallas_call x1, Pallas kernels, tables(): pl.pallas_call(functools.partial(tables_kernel, channels), out_shape=[jax...  3.49 us
    ppermute x1, starting transfers between devices, local(): left = lax.ppermute(own[:, (GROUPS - SIDE) * ch:], 'tx', up)  3.34 us
    ppermute x1, starting transfers between devices, local(): right = lax.ppermute(own[:, :SIDE * ch], 'tx', down)  2.21 us
  transfers between devices with their start and end apart: 2, of which 2 were waited for; matrix products, arithmetic and copies ran while one was open for 0% of the time, Pallas kernels for 5%

profile of v2, /device:TPU:1, one launch (start us, length us, event | category | flops | bytes accessed | tf_op | source)
XLA Modules:
  0.0 63.6 jit_solution(130503373723437356)
XLA Ops:
  0.0 3.5 %pack.1 = bf16[32,152,128]{2,1,0:T(8,128)(2,1)S(1)} custom-call(bf16[8,512,128]{2,1,0:T(8,128)(2,1)} %cube_ref.1, s32[8,32]{1,0:T(8,128)} %bitcast.9), custom_call_target="tpu_custom_call" | custom-call | tf_op jit(solution)/shard_map/pack/pallas_call | solution.py:195
  3.5 38.5 %all_to_all.5 = bf16[32,152,128]{2,1,0:T(8,128)(2,1)S(1)} all-to-all(bf16[32,152,128]{2,1,0:T(8,128)(2,1)S(1)} %pack.1), channel_id=1, replica_groups=mesh['ty'=4,'tx'=8] {'ty','tx'}, dimensions={0} | all-to-all | bytes 2490368 | tf_op jit(solution)/shard_map/all_to_all | solution.py:344
  42.1 0.0 copy-start.1
  42.1 0.0 copy-start
  42.1 0.0 copy-start.2
  42.1 1.0 %fusion = (bf16[32,88,128]{2,1,0:T(8,128)(2,1)}, bf16[32,88,128]{2,1,0:T(8,128)(2,1)S(1)}) fusion(bf16[32,152,128]{2,1,0:T(8,128)(2,1)S(1)} %all_to_all.5), kind=kLoop, calls=%fused_computation.1 | loop fusion | bytes 2883584 | tf_op jit(solution)/shard_map/slice | solution.py:353
  43.0 2.2 %collective-permute-start.1 = (bf16[32,88,128]{2,1,0:T(8,128)(2,1)}, bf16[32,88,128]{2,1,0:T(8,128)(2,1)S(1)}, u32[]{:S(2)}, u32[]{:S(2)}) collective-permute-start(bf16[32,88,128]{2,1,0:T(8,128)(2,1)} %get-tuple-element.17), channel_id=1, source_target_pairs={{1,0},{2,1},{3,2},{4,3},{5,4},{6,5},{7,6},{9,8},{10,9},{11,10},{12... | collective-permute-start | bytes 2162696 | tf_op jit(solution)/shard_map/ppermute | solution.py:353
  45.2 3.3 %collective-permute-start = (bf16[32,88,128]{2,1,0:T(8,128)(2,1)S(1)}, bf16[32,88,128]{2,1,0:T(8,128)(2,1)S(1)}, u32[]{:S(2)}, u32[]{:S(2)}) collective-permute-start(bf16[32,88,128]{2,1,0:T(8,128)(2,1)S(1)} %get-tuple-element.18), channel_id=1, source_target_pairs={{0,1},{1,2},{2,3},{3,4},{4,5},{5,6},{6,7},{8,9},{9,10},{10,11},{11... | collective-permute-start | bytes 2162696 | tf_op jit(solution)/shard_map/ppermute | solution.py:352
  48.6 0.0 copy-done.1
  48.6 3.5 %tables.1 = (bf16[384,128]{1,0:T(8,128)(2,1)S(1)}, bf16[7,384,128]{2,1,0:T(8,128)(2,1)S(1)}, bf16[256,352]{1,0:T(8,128)(2,1)S(1)}, bf16[256,448]{1,0:T(8,128)(2,...) custom-call(s32[2,4]{1,0:T(2,128)S(1)} %copy-done.1), custom_call_target="tpu_custom_call" | custom-call | flops 10000000 | bytes 4000000 | tf_op jit(solution)/shard_map/tables/pallas_call | solution.py:103
  52.1 0.0 copy-done
  52.1 0.1 dynamic-slice_bitcast_fusion.tile_mask_ref
  52.2 3.6 %collective-permute-done.1 = bf16[32,88,128]{2,1,0:T(8,128)(2,1)S(1)} collective-permute-done((bf16[32,88,128]{2,1,0:T(8,128)(2,1)}, bf16[32,88,128]{2,1,0:T(8,128)(2,1)S(1)}, u32[]{:S(2)}, u32[]{:S(2)}) %collective-permute-start.1) | collective-permute-done | bytes 720928 | tf_op jit(solution)/shard_map/ppermute | solution.py:353
  55.8 1.0 %collective-permute-done = bf16[32,88,128]{2,1,0:T(8,128)(2,1)S(1)} collective-permute-done((bf16[32,88,128]{2,1,0:T(8,128)(2,1)S(1)}, bf16[32,88,128]{2,1,0:T(8,128)(2,1)S(1)}, u32[]{:S(2)}, u32[]{:S(2)}) %collective-permute-start) | collective-permute-done | bytes 720928 | tf_op jit(solution)/shard_map/ppermute | solution.py:352
  56.8 0.0 copy-done.2
  56.8 6.8 %finish.1 = bf16[4,128,16,256]{3,2,1,0:T(8,128)(2,1)} custom-call(s32[4]{0:T(128)S(1)} %copy-done.2, s32[2,4]{1,0:T(2,128)S(1)} %copy-done.1, s32[8]{0:T(128)S(1)} %dynamic-slice_bitcast_fusion.tile_mask_ref, s32[8,32]{1,0:T(8,128)S(1)} %bitcast.10, bf16[32,19,8,128]{3,2,1,0:T(8,128)(2,1)S(1)} %bitcast.6, bf16[32,11,8,128]{3,2,1,0:T(8,128)(2,1)S(1)} %bitcast.8, ...), custom_call_target="tpu_custom_call" | custom-call | tf_op jit(solution)/shard_map/finish/pallas_call | solution.py:322
Async XLA Ops:
  42.1 6.5 %copy-start.1 = (s32[2,4]{1,0:T(2,128)S(1)}, s32[2,4]{1,0:T(2,128)}, u32[]{:S(2)}) copy-start(s32[2,4]{1,0:T(2,128)} %taps_ref.3) | copy-start | bytes 100
  42.1 10.1 %copy-start = (s32[32,8]{0,1:T(8,128)S(1)}, s32[32,8]{0,1:T(8,128)}, u32[]{:S(2)}) copy-start(s32[32,8]{0,1:T(8,128)} %param.5) | copy-start | bytes 3076
  42.1 14.7 %copy-start.2 = (s32[4]{0:T(128)S(1)}, s32[4]{0:T(128)}, u32[]{:S(2)}) copy-start(s32[4]{0:T(128)} %sigma_ref.1) | copy-start | bytes 52
  43.0 12.8 %collective-permute-start.1 = (bf16[32,88,128]{2,1,0:T(8,128)(2,1)}, bf16[32,88,128]{2,1,0:T(8,128)(2,1)S(1)}, u32[]{:S(2)}, u32[]{:S(2)}) collective-permute-start(bf16[32,88,128]{2,1,0:T(8,128)(2,1)} %get-tuple-element.17), channel_id=1, source_target_pairs={{1,0},{2,1},{3,2},{4,3},{5,4},{6,5},{7,6},{9,8},{10,9},{11,10},{12... | collective-permute-start | bytes 2162696 | tf_op jit(solution)/shard_map/ppermute | solution.py:353
  45.2 11.6 %collective-permute-start = (bf16[32,88,128]{2,1,0:T(8,128)(2,1)S(1)}, bf16[32,88,128]{2,1,0:T(8,128)(2,1)S(1)}, u32[]{:S(2)}, u32[]{:S(2)}) collective-permute-start(bf16[32,88,128]{2,1,0:T(8,128)(2,1)S(1)} %get-tuple-element.18), channel_id=1, source_target_pairs={{0,1},{1,2},{2,3},{3,4},{4,5},{5,6},{6,7},{8,9},{9,10},{10,11},{11... | collective-permute-start | bytes 2162696 | tf_op jit(solution)/shard_map/ppermute | solution.py:352

commit v3 on v2

--- a/solution.py
+++ b/solution.py
@@ -7,6 +7,7 @@
 from jax.experimental import pallas as pl
 from jax.experimental.pallas import tpu as pltpu
 from jax.sharding import PartitionSpec as P
+
 
 TILE_Y = 128
 TILE_X = 16
@@ -16,7 +17,6 @@
 HALO = 9
 SMAX = 3
 LANES = 128
-WIN_X = TILE_X + 2 * HALO
 PACK = 7
 HALO_GROUPS = (0, 10, 18)
 GROUPS = TILE_X + 3
@@ -33,6 +33,23 @@
     return x + 1 if x < HALO else x + 2
 
 
+def left_column(i):
+    x, base = TILE_X - HALO + i, GROUPS - SIDE
+    return column_group(x) - base, HALO_GROUPS[x // PACK] - base, x % PACK
+
+
+def right_column(i):
+    return column_group(i), HALO_GROUPS[i // PACK], i % PACK
+
+
+def odd_tile():
+    return lax.rem(lax.axis_index("tx"), 2)
+
+
+def choose(flag, one, other):
+    return jnp.where(flag == 1, jnp.int32(one), jnp.int32(other))
+
+
 def tap_table():
     offsets = np.arange(-HALO, HALO + 1).astype(np.float32)
     rows = []
@@ -68,7 +85,8 @@
 
 
 def tables_kernel(channels, taps_ref, main_ref, halo_ref, *rest):
-    x_refs, box_ref = rest[:SMAX], rest[SMAX]
+    x_refs, far_refs, box_ref = rest[:SMAX], rest[SMAX : 2 * SMAX], rest[2 * SMAX]
+    odd = odd_tile()
     taps = tap_table()
     for index in range(SMAX):
         sigma = index + 1
@@ -80,10 +98,11 @@
         halo = taps_at(in_y - out_y, taps[index], sigma)
         for member in range(PACK):
             halo_ref[member, rows, :] = jnp.where(slot == member, halo, F32(0.0)).astype(BF16)
-        shape = x_refs[index].shape
-        row, col = iota(shape, 0), iota(shape, 1)
-        weight = taps_at(col // PT - row % TILE_X - 3 * sigma, taps[index], sigma)
-        x_refs[index][...] = jnp.where(row // TILE_X == col % PT, weight, F32(0.0)).astype(BF16)
+        reach = 3 * sigma
+        for ref, shift in ((x_refs[index], choose(odd, -reach, 0)), (far_refs[index], choose(odd, TILE_X, -reach))):
+            row, col = iota(ref.shape, 0), iota(ref.shape, 1)
+            weight = taps_at(col // PT - row % TILE_X + shift, taps[index], sigma)
+            ref[...] = jnp.where(row // TILE_X == col % PT, weight, F32(0.0)).astype(BF16)
     for scale in range(NSC):
         width, dilation = taps_ref[0, scale], taps_ref[1, scale]
         shape = box_ref.shape[1:]
@@ -97,7 +116,8 @@
 
 def tables(spectral_taps, channels):
     shapes = [(SMAX * TILE_Y, LANES), (PACK, SMAX * TILE_Y, LANES)]
-    shapes += [(PT * TILE_X, (TILE_X + 6 * (i + 1)) * PT) for i in range(SMAX)]
+    shapes += [(PT * TILE_X, (TILE_X + 3 * (i + 1)) * PT) for i in range(SMAX)]
+    shapes += [(PT * TILE_X, 3 * (i + 1) * PT) for i in range(SMAX)]
     wide = min(channels, WIDE)
     shapes += [(NSC, wide + 2 * margin(channels), wide)]
     return pl.pallas_call(
@@ -211,129 +231,194 @@
     )(in_hbm(cube), in_hbm(footprint.T))
 
 
-def main_kernel(
-    sigma_ref, taps_ref, tile_mask_ref, footprint_ref, own_ref, left_ref, right_ref,
-    main_ref, halo_ref, *rest,
-):
-    x_refs, box_ref = rest[:SMAX], rest[SMAX]
-    out_ref, rows_ref, scale_ref, stage_ref, sems = rest[SMAX + 1 : SMAX + 6]
+def cut_kernel(far, own_ref, out_ref):
+    odd = odd_tile()
+    first = (odd if far else 1 - odd) * (GROUPS - SIDE)
+    out_ref[...] = own_ref[:, pl.ds(first, SIDE)]
+
+
+def cut(own, far):
+    senders, _, ch, lanes = own.shape
+    return pl.pallas_call(
+        functools.partial(cut_kernel, far),
+        out_shape=jax.ShapeDtypeStruct((senders, SIDE, ch, lanes), BF16),
+        in_specs=[pl.BlockSpec(memory_space=pltpu.VMEM)],
+        out_specs=pl.BlockSpec(memory_space=pltpu.VMEM),
+        compiler_params=pltpu.CompilerParams(vmem_limit_bytes=6 * 2**20 if senders <= 32 else 24 * 2**20),
+        name="cut_far" if far else "cut_near",
+    )(own)
+
+
+def load(ref, first, part, group):
+    block = ref[pl.ds(first, part), group].astype(F32)
+    return block.reshape(part * ref.shape[2], LANES).astype(BF16)
+
+
+def y_pass(ref, first, part, group, halo_group, member, main_ref, halo_ref, rows_ref, x):
+    data = jnp.concatenate([load(ref, first, part, group), load(ref, first, part, halo_group)], axis=1)
+    band = jnp.concatenate([main_ref[...], halo_ref[member]], axis=1)
+    rows = lax.dot_general(band, data, NT, preferred_element_type=F32).astype(BF16)
+    rows_ref[:, :, x] = rows.reshape(SMAX, TILE_Y // PT, PT, rows.shape[1])
+
+
+def x_pass(rows_ref, kind, group, start, count, weights_ref):
+    slab = rows_ref[kind, group, pl.ds(start, count)]
+    slab = slab.reshape(count * PT, slab.shape[-1])
+    return jnp.dot(weights_ref[...], slab, preferred_element_type=F32)
+
+
+def begin_kernel(own_ref, near_ref, main_ref, halo_ref, *rest):
+    x_refs, sum_ref, rows_ref = rest[:SMAX], rest[SMAX], rest[SMAX + 1]
+    senders, _, ch, _ = own_ref.shape
+    part = min(senders, WIDE // ch)
+    odd = odd_tile()
+
+    def one(index, carry):
+        first = index * part
+        passed = functools.partial(y_pass, main_ref=main_ref, halo_ref=halo_ref, rows_ref=rows_ref)
+        for i in range(HALO):
+            where = [choose(odd, a, b) for a, b in zip(left_column(i), right_column(i))]
+            passed(near_ref, first, part, *where, x=choose(odd, i, TILE_X + i))
+        for x in range(TILE_X):
+            passed(own_ref, first, part, *right_column(x), x=choose(odd, HALO + x, x))
+        lanes = pl.ds(pl.multiple_of(first * ch, part * ch), part * ch)
+        for group in range(TILE_Y // PT):
+            for kind in range(SMAX):
+                reach = 3 * (kind + 1)
+                start = choose(odd, HALO - reach, 0)
+                sum_ref[kind, group, :, lanes] = x_pass(rows_ref, kind, group, start, TILE_X + reach, x_refs[kind])
+        return carry
+
+    if senders == part:
+        one(0, 0)
+    else:
+        lax.fori_loop(0, senders // part, one, 0)
+
+
+def begin(own, near, main, halo, weights):
+    senders, _, ch, _ = own.shape
+    channels = senders * ch
+    wide = min(channels, WIDE)
+    rows = (SMAX, TILE_Y // PT, TILE_X + HALO, PT, wide)
+    sums = (SMAX, TILE_Y // PT, PT * TILE_X, channels)
+    vmem = pl.BlockSpec(memory_space=pltpu.VMEM)
+    limit = 2 * int(np.prod(rows)) + 6 * 2**20 if channels <= WIDE else 62 * 2**20
+    return pl.pallas_call(
+        begin_kernel,
+        out_shape=jax.ShapeDtypeStruct(sums, F32),
+        in_specs=[vmem] * (4 + len(weights)),
+        out_specs=vmem,
+        scratch_shapes=[pltpu.VMEM(rows, BF16)],
+        compiler_params=pltpu.CompilerParams(vmem_limit_bytes=limit),
+        cost_estimate=pl.CostEstimate(flops=10**9, bytes_accessed=8 * 10**6, transcendentals=0),
+        name="begin",
+    )(own, near, main, halo, *weights)
+
+
+def finish_kernel(sigma_ref, taps_ref, cover_ref, footprint_ref, own_ref, far_ref, sum_ref, main_ref, halo_ref, *rest):
+    far_refs, box_ref, out_ref, rows_ref, scale_ref, stage_ref, sems = rest[:SMAX], *rest[SMAX : SMAX + 6]
     smooth_refs = rest[SMAX + 6 :]
     senders, _, ch, _ = own_ref.shape
     channels = senders * ch
     part = min(senders, WIDE // ch)
-
-    def load(ref, first, group):
-        block = ref[pl.ds(first, part), group].astype(F32)
-        return block.reshape(part * ch, LANES).astype(BF16)
+    odd = odd_tile()
+    tile_x, tile_y = lax.axis_index("tx") * (TILE_X // PT), lax.axis_index("ty") * (TILE_Y // PT)
+    slots, _, tall = stage_ref.shape[:3]
+    span, phases = tall // PT, TILE_Y // tall
+    wide, edge = min(channels, WIDE), margin(channels)
 
     lane = iota((8, 2 * LANES), 1)
-    pick = jnp.where((lane >= LANES - 2) & (lane <= LANES) | (lane == 2 * LANES - 2), F32(1.0), F32(0.0))
-    pick = jnp.where(lane == LANES, F32(0.0), pick).astype(BF16)
+    pick = jnp.where((lane >= LANES - 2) & (lane < LANES) | (lane == 2 * LANES - 2), F32(1.0), F32(0.0)).astype(BF16)
     for first in range(0, senders, part):
-        both = jnp.concatenate([load(own_ref, first, HALO_GROUPS[0]), load(own_ref, first, HALO_GROUPS[1])], axis=1)
+        both = jnp.concatenate([load(own_ref, first, part, group) for group in HALO_GROUPS[:2]], axis=1)
         squares = lax.dot_general(pick, both, NT, preferred_element_type=F32)
         squares = jnp.where(squares >= F32(BIG), F32(jnp.inf), squares)
         count = jnp.maximum(jnp.sum(footprint_ref[...].astype(F32), keepdims=True) * F32(PT * PT), F32(1.0))
         noise = jnp.sqrt(squares / count + F32(1e-06))
-        taps = tap_table()
+        energy = [F32(float(np.sum(t * t, dtype=np.float32))) for t in tap_table()]
         for scale in range(NSC):
             width = jnp.full(noise.shape, taps_ref[0, scale], jnp.int32).astype(F32)
-            sigma = sigma_ref[scale]
-            energy = [F32(float(np.sum(t * t, dtype=np.float32))) for t in taps]
             knorm = jnp.full(noise.shape, energy[0], F32)
             for index in range(1, SMAX):
-                knorm = jnp.where(sigma == index + 1, energy[index], knorm)
+                knorm = jnp.where(sigma_ref[scale] == index + 1, energy[index], knorm)
             knorm = knorm / jnp.sqrt(width)
             scale_ref[scale, :, first * ch : (first + part) * ch] = F32(1.0) / (noise * knorm * width)
-
-    def y_pass(ref, first, group, halo_group, member, x):
-        data = jnp.concatenate([load(ref, first, group), load(ref, first, halo_group)], axis=1)
-        band = jnp.concatenate([main_ref[...], halo_ref[member]], axis=1)
-        rows = lax.dot_general(band, data, NT, preferred_element_type=F32).astype(BF16)
-        rows = rows.reshape(SMAX, TILE_Y // PT, PT, part * ch)
-        rows_ref[:, :, x, :, first * ch : (first + part) * ch] = rows
-
-    for first in range(0, senders, part):
-        for ref, columns, base, at in (
-            (left_ref, range(TILE_X - HALO, TILE_X), column_group(TILE_X - HALO), HALO - TILE_X),
-            (own_ref, range(TILE_X), 0, HALO),
-            (right_ref, range(HALO), 0, HALO + TILE_X),
-        ):
-            for x in columns:
-                y_pass(ref, first, column_group(x) - base, HALO_GROUPS[x // PACK] - base, x % PACK, x + at)
-
-    slots, _, tall = stage_ref.shape[:3]
-    span, phases = tall // PT, TILE_Y // tall
-    wide, edge = min(channels, WIDE), margin(channels)
 
     def out_copy(phase, slot, scale):
         there = out_ref.at[scale, pl.ds(phase * tall, tall)]
         return pltpu.make_async_copy(stage_ref.at[slot, scale], there, sems.at[slot, scale])
 
-    def x_pass(phase, smooth_ref):
+    def far_y(first):
+        for i in range(HALO):
+            where = [choose(odd, a, b) for a, b in zip(right_column(i), left_column(i))]
+            y_pass(far_ref, first, part, *where, main_ref, halo_ref, rows_ref, i)
+
+    def far_x(first, phase):
+        lanes = slice(first * ch, (first + part) * ch)
         for kind in range(SMAX):
             reach = 3 * (kind + 1)
             for row in range(span):
-                for at in range(0, channels, wide):
-                    lanes = slice(at, at + wide)
-                    slab = rows_ref[kind, phase * span + row, HALO - reach : HALO + TILE_X + reach, :, lanes]
-                    slab = slab.reshape((TILE_X + 2 * reach) * PT, wide)
-                    field = jnp.dot(x_refs[kind][...], slab, preferred_element_type=F32)
-                    smooth_ref[kind, row, :, lanes] = field.astype(BF16)
-
-    def box_pass(phase, slot, smooth_ref, reused):
+                group = phase * span + row
+                added = x_pass(rows_ref, kind, group, choose(odd, 0, HALO - reach), reach, far_refs[kind])
+                smooth_refs[phase][kind, row, :, lanes] = (sum_ref[kind, group, :, lanes] + added).astype(BF16)
+
+    def box_pass(phase, slot):
         for scale in range(NSC):
-            if reused:
+            if phase >= slots:
                 out_copy(phase - slots, slot, scale).wait()
             for row in range(span):
-                seen = tile_mask_ref[phase * span + row].astype(F32)
+                seen = cover_ref[tile_x, tile_y + phase * span + row].astype(F32)
                 for at in range(0, channels, wide):
                     lanes, first = slice(at, at + wide), at - edge
                     low, high = max(first, 0), min(at + wide + edge, channels)
-                    field = smooth_ref[sigma_ref[scale] - 1, row, :, low:high]
+                    field = smooth_refs[phase][sigma_ref[scale] - 1, row, :, low:high]
                     boxed = jnp.dot(field, box_ref[scale, low - first : high - first], preferred_element_type=F32)
                     scaled = (boxed * (scale_ref[scale, 0:1, lanes] * seen)).astype(BF16)
                     stage_ref[slot, scale, row * PT : (row + 1) * PT, :, lanes] = scaled.reshape(PT, TILE_X, wide)
             out_copy(phase, slot, scale).start()
 
-    for phase in range(slots):
-        x_pass(phase, smooth_refs[phase])
-        box_pass(phase, phase, smooth_refs[phase], False)
-
-    def again(phase, carry):
-        x_pass(phase, smooth_refs[0])
-        box_pass(phase, lax.rem(phase, slots), smooth_refs[0], True)
-        return carry
-
-    if phases > slots:
-        lax.fori_loop(slots, phases, again, 0)
+    whole = senders == part
+    for first in range(0, senders, part):
+        far_y(first)
+        if not whole:
+            for phase in range(phases):
+                far_x(first, phase)
+    for phase in range(phases):
+        if whole:
+            far_x(0, phase)
+        box_pass(phase, phase % slots)
     for phase in range(phases - slots, phases):
         for scale in range(NSC):
             out_copy(phase, phase % slots, scale).wait()
 
 
-def finish(kernel_sigmas, spectral_taps, tile_mask, footprint, own, left, right, consts):
+def finish(kernel_sigmas, spectral_taps, footprint, own, far, sums, main, halo, weights, box):
     senders, _, ch, _ = own.shape
     channels = senders * ch
-    span, slots = (SPAN, TILE_Y // PT // SPAN) if channels <= WIDE else (1, 2)
-    need = 2 * channels * (SMAX * TILE_Y * WIN_X + slots * span * (NSC + SMAX) * PT * TILE_X)
+    wide = min(channels, WIDE)
+    span = SPAN if channels <= WIDE else 1
+    phases = TILE_Y // PT // span
+    rows = (SMAX, TILE_Y // PT, HALO, PT, wide)
+    need = 2 * int(np.prod(rows)) + 2 * channels * (2 * span * NSC + SMAX * TILE_Y // PT) * PT * TILE_X
     smem = pl.BlockSpec(memory_space=pltpu.SMEM)
     vmem = pl.BlockSpec(memory_space=pltpu.VMEM)
     return pl.pallas_call(
-        main_kernel,
+        finish_kernel,
         out_shape=jax.ShapeDtypeStruct((NSC, TILE_Y, TILE_X, channels), BF16),
-        in_specs=[smem] * 3 + [vmem] * (4 + len(consts)),
+        in_specs=[smem] * 3 + [vmem] * (7 + len(weights)),
         out_specs=pl.BlockSpec(memory_space=pltpu.MemorySpace.HBM),
         scratch_shapes=[
-            pltpu.VMEM((SMAX, TILE_Y // PT, WIN_X, PT, channels), BF16),
+            pltpu.VMEM(rows, BF16),
             pltpu.VMEM((NSC, 8, channels), F32),
-            pltpu.VMEM((slots, NSC, span * PT, TILE_X, channels), BF16),
-            pltpu.SemaphoreType.DMA((slots, NSC)),
+            pltpu.VMEM((2, NSC, span * PT, TILE_X, channels), BF16),
+            pltpu.SemaphoreType.DMA((2, NSC)),
         ]
-        + [pltpu.VMEM((SMAX, span, PT * TILE_X, channels), BF16)] * slots,
-        compiler_params=pltpu.CompilerParams(vmem_limit_bytes=need + 6 * 2**20 if channels <= WIDE else 62 * 2**20),
+        + [pltpu.VMEM((SMAX, span, PT * TILE_X, channels), BF16)] * phases,
+        compiler_params=pltpu.CompilerParams(
+            vmem_limit_bytes=need + 6 * 2**20 if channels <= WIDE else 62 * 2**20
+        ),
         name="finish",
-    )(kernel_sigmas, spectral_taps, tile_mask, footprint.T, own, left, right, *consts)
+    )(kernel_sigmas, spectral_taps, footprint.T, footprint.T, own, far, sums, main, halo, *weights, box)
 
 
 def local(channel_cube, footprint, kernel_sigmas, spectral_taps):
@@ -342,21 +427,18 @@
     channels = ch * lax.axis_size("ty") * n_cols
     packed = pack(channel_cube, footprint)
     own = lax.all_to_all(packed, ("ty", "tx"), split_axis=0, concat_axis=0, tiled=True)
-    consts = tables(spectral_taps, channels)
-    tile_rows = TILE_Y // PT
-    tile_mask = lax.dynamic_slice(
-        footprint, (lax.axis_index("ty") * tile_rows, lax.axis_index("tx") * (TILE_X // PT)), (tile_rows, 1)
-    )[:, 0]
-    up = [(i, i + 1) for i in range(n_cols - 1)]
-    down = [(i + 1, i) for i in range(n_cols - 1)]
-    left = lax.ppermute(own[:, (GROUPS - SIDE) * ch :], "tx", up)
-    right = lax.ppermute(own[:, : SIDE * ch], "tx", down)
-    split = lambda block: block.reshape(block.shape[0], -1, ch, LANES)
-    return finish(kernel_sigmas, spectral_taps, tile_mask, footprint, split(own), split(left), split(right), consts)
+    own = own.reshape(own.shape[0], GROUPS, ch, LANES)
+    far_pairs = [(i, i + 1) for i in range(1, n_cols - 1, 2)]
+    near_pairs = [(i, i + 1) for i in range(0, n_cols - 1, 2)]
+    both = lambda pairs: pairs + [(j, i) for i, j in pairs]
+    far, near = cut(own, True), cut(own, False)
+    far = lax.ppermute(far, "tx", both(far_pairs))
+    near = lax.ppermute(near, "tx", both(near_pairs))
+    main, halo, *weights, box = tables(spectral_taps, channels)
+    sums = begin(own, near, main, halo, weights[:SMAX])
+    return finish(kernel_sigmas, spectral_taps, footprint, own, far, sums, main, halo, weights[SMAX:], box)
 
 
 def solution(mesh):
     placed = (P(("ty", "tx"), None, None), P(), P(), P())
-    return jax.shard_map(
-        local, mesh=mesh, in_specs=placed, out_specs=P(None, "ty", "tx", None), check_vma=False
-    )
+    return jax.shard_map(local, mesh=mesh, in_specs=placed, out_specs=P(None, "ty", "tx", None), check_vma=False)

time: 63.9 us -> 60.2 us (0.942)
  starting transfers between devices: 5.55 us -> 2.5 us
  Pallas kernels: 13.8 us -> 14.9 us
  local copies, waits for them, and re-layouts: 1.05 us -> 0.02 us
  waiting for transfers between devices: 4.61 us -> 3.85 us
    ppermute x2, starting transfers between devices: 5.55 us -> 2.5 us  [the longest x1 2.12 us: local(): far = lax.ppermute(far, 'tx', both(far_pairs))]
    pallas_call x1 -> x4, Pallas kernels: 6.83 us -> 8.06 us  [the longest x1 4.67 us: finish(): pl.pallas_call(finish_kernel, out_shape=jax.ShapeDtypeStruct((NSC, TILE_Y...]
    slice x1 -> x0, local copies, waits for them, and re-layouts: 0.96 us -> none  [local(): right = lax.ppermute(own[:, :SIDE * ch], 'tx', down)]
    ppermute x2, waiting for transfers between devices: 4.61 us -> 3.85 us  [the longest x1 3.85 us: local(): far = lax.ppermute(far, 'tx', both(far_pairs))]
  transfers between devices with their start and end apart: 2 -> 2, of which waited for: 2 -> 1; matrix products, arithmetic and copies ran while one was open for 0% -> 0% of each run, Pallas kernels for 5% -> 11%
where the time goes in v3:
time: 60.2 us; the launch traced here: 60 us
  blocking collectives  38.5 us (64%)
  Pallas kernels  14.9 us (25%)
  waiting for transfers between devices  3.85 us (6%)
  starting transfers between devices  2.5 us (4%)
    all_to_all x1, blocking collectives, local(): lax.all_to_all(packed, ('ty', 'tx'), split_axis=0, concat_axis=0, tiled=T...  38.5 us
    pallas_call x1, Pallas kernels, finish(): pl.pallas_call(finish_kernel, out_shape=jax.ShapeDtypeStruct((NSC, TILE_Y...  4.67 us
    ppermute x1, waiting for transfers between devices, local(): far = lax.ppermute(far, 'tx', both(far_pairs))  3.85 us
    pallas_call x1, Pallas kernels, pack(): pl.pallas_call(pack_kernel, out_shape=jax.ShapeDtypeStruct((n_rows * n_co...  3.54 us
    pallas_call x1, Pallas kernels, begin(): pl.pallas_call(begin_kernel, out_shape=jax.ShapeDtypeStruct(sums, F32), i...  3.29 us
    pallas_call x1, Pallas kernels, tables(): pl.pallas_call(functools.partial(tables_kernel, channels), out_shape=[jax...  3.28 us
    ppermute x1, starting transfers between devices, local(): far = lax.ppermute(far, 'tx', both(far_pairs))  2.12 us
  transfers between devices with their start and end apart: 2, of which 1 were waited for; matrix products, arithmetic and copies ran while one was open for 0% of the time, Pallas kernels for 11%

profile of v3, /device:TPU:1, one launch (start us, length us, event | category | flops | bytes accessed | tf_op | source)
XLA Modules:
  0.0 60.0 jit_solution(4743312667535511926)
XLA Ops:
  0.0 0.0 copy-start.1
  0.0 3.5 %pack.1 = bf16[32,152,128]{2,1,0:T(8,128)(2,1)S(1)} custom-call(bf16[8,512,128]{2,1,0:T(8,128)(2,1)} %cube_ref.1, s32[8,32]{1,0:T(8,128)} %bitcast.6), custom_call_target="tpu_custom_call" | custom-call | tf_op jit(solution)/shard_map/pack/pallas_call | solution.py:215
  3.6 38.5 %all_to_all.5 = bf16[32,152,128]{2,1,0:T(8,128)(2,1)S(1)} all-to-all(bf16[32,152,128]{2,1,0:T(8,128)(2,1)S(1)} %pack.1), channel_id=1, replica_groups=mesh['ty'=4,'tx'=8] {'ty','tx'}, dimensions={0} | all-to-all | bytes 2490368 | tf_op jit(solution)/shard_map/all_to_all | solution.py:429
  42.1 0.1 cut_near.1
  42.1 0.4 collective-permute-start.1
  42.5 0.1 cut_far.1
  42.6 2.1 %collective-permute-start = (bf16[32,11,8,128]{3,2,1,0:T(8,128)(2,1)S(1)}, bf16[32,11,8,128]{3,2,1,0:T(8,128)(2,1)S(1)}, u32[]{:S(2)}, u32[]{:S(2)}) collective-permute-start(bf16[32,11,8,128]{3,2,1,0:T(8,128)(2,1)S(1)} %cut_far.1), channel_id=1, source_target_pairs={{1,2},{3,4},{5,6},{2,1},{4,3},{6,5},{9,10},{11,12},{13,14},{10,9},... | collective-permute-start | bytes 2162696 | tf_op jit(solution)/shard_map/ppermute | solution.py:435
  44.7 0.0 copy-done.1
  44.7 3.3 %tables.1 = (bf16[384,128]{1,0:T(8,128)(2,1)S(1)}, bf16[7,384,128]{2,1,0:T(8,128)(2,1)S(1)}, bf16[256,304]{1,0:T(8,128)(2,1)S(1)}, bf16[256,352]{1,0:T(8,128)(2,...) custom-call(s32[2,4]{1,0:T(2,128)S(1)} %copy-done.1), custom_call_target="tpu_custom_call" | custom-call | flops 10000000 | bytes 4000000 | tf_op jit(solution)/shard_map/tables/pallas_call | solution.py:123
  48.0 0.0 collective-permute-done.1.near_ref
  48.0 0.0 copy-start
  48.0 0.0 copy-start.2
  48.0 3.3 %begin.1.sum_ref = f32[3,8,256,256]{3,2,1,0:T(8,128)S(1)} custom-call(bf16[32,19,8,128]{3,2,1,0:T(8,128)(2,1)S(1)} %bitcast.4, bf16[32,11,8,128]{3,2,1,0:T(8,128)(2,1)S(1)} %collective-permute-done.1.near_ref, bf16[384,128]{1,0:T(8,128)(2,1)S(1)} %get-tuple-element.14.main_ref, bf16[7,384,128]{2,1,0:T(8,128)(2,1)S(1)} %get-tuple-element.15.halo_ref, ...), custom_call_target="tpu_custom_call" | custom-call | flops 1000000000 | bytes 8000000 | tf_op jit(solution)/shard_map/begin/pallas_call | solution.py:306
  51.3 3.8 %collective-permute-done.far_ref = bf16[32,11,8,128]{3,2,1,0:T(8,128)(2,1)S(1)} collective-permute-done((bf16[32,11,8,128]{3,2,1,0:T(8,128)(2,1)S(1)}, bf16[32,11,8,128]{3,2,1,0:T(8,128)(2,1)S(1)}, u32[]{:S(2)}, u32[]{:S(2)}) %collective-permute-start) | collective-permute-done | bytes 720928 | tf_op jit(solution)/shard_map/ppermute | solution.py:435
  55.2 0.0 copy-done
  55.2 0.0 copy-done.2
  55.2 4.7 %finish.1 = bf16[4,128,16,256]{3,2,1,0:T(8,128)(2,1)} custom-call(s32[4]{0:T(128)S(1)} %copy-done.2, s32[2,4]{1,0:T(2,128)S(1)} %copy-done.1, s32[8,32]{1,0:T(8,128)S(1)} %bitcast.7, s32[8,32]{1,0:T(8,128)S(1)} %bitcast.8, bf16[32,19,8,128]{3,2,1,0:T(8,128)(2,1)S(1)} %bitcast.5, bf16[32,11,8,128]{3,2,1,0:T(8,128)(2,1)S(1)} %collective-permute-done.far_ref, ...), custom_call_target="tpu_custom_call" | custom-call | tf_op jit(solution)/shard_map/finish/pallas_call | solution.py:405
Async XLA Ops:
  0.0 44.7 %copy-start.1 = (s32[2,4]{1,0:T(2,128)S(1)}, s32[2,4]{1,0:T(2,128)}, u32[]{:S(2)}) copy-start(s32[2,4]{1,0:T(2,128)} %taps_ref.3) | copy-start | bytes 100
  42.1 5.9 %collective-permute-start.1 = (bf16[32,11,8,128]{3,2,1,0:T(8,128)(2,1)S(1)}, bf16[32,11,8,128]{3,2,1,0:T(8,128)(2,1)S(1)}, u32[]{:S(2)}, u32[]{:S(2)}) collective-permute-start(bf16[32,11,8,128]{3,2,1,0:T(8,128)(2,1)S(1)} %cut_near.1), channel_id=1, source_target_pairs={{0,1},{2,3},{4,5},{6,7},{1,0},{3,2},{5,4},{7,6},{8,9},{10,11},{12,... | collective-permute-start | bytes 2162696 | tf_op jit(solution)/shard_map/ppermute | solution.py:436
  42.6 12.6 %collective-permute-start = (bf16[32,11,8,128]{3,2,1,0:T(8,128)(2,1)S(1)}, bf16[32,11,8,128]{3,2,1,0:T(8,128)(2,1)S(1)}, u32[]{:S(2)}, u32[]{:S(2)}) collective-permute-start(bf16[32,11,8,128]{3,2,1,0:T(8,128)(2,1)S(1)} %cut_far.1), channel_id=1, source_target_pairs={{1,2},{3,4},{5,6},{2,1},{4,3},{6,5},{9,10},{11,12},{13,14},{10,9},... | collective-permute-start | bytes 2162696 | tf_op jit(solution)/shard_map/ppermute | solution.py:435
  48.0 7.2 %copy-start = (s32[32,8]{0,1:T(8,128)S(1)}, s32[32,8]{0,1:T(8,128)}, u32[]{:S(2)}) copy-start(s32[32,8]{0,1:T(8,128)} %param.5) | copy-start | bytes 3076
  48.0 7.2 %copy-start.2 = (s32[4]{0:T(128)S(1)}, s32[4]{0:T(128)}, u32[]{:S(2)}) copy-start(s32[4]{0:T(128)} %sigma_ref.1) | copy-start | bytes 52

commit v4 on v3

--- a/solution.py
+++ b/solution.py
@@ -17,6 +17,7 @@
 HALO = 9
 SMAX = 3
 LANES = 128
+TURN = LANES + 8
 PACK = 7
 HALO_GROUPS = (0, 10, 18)
 GROUPS = TILE_X + 3
@@ -131,60 +132,63 @@
     )(spectral_taps)
 
 
-def pack_kernel(cube_ref, cover_hbm, out_ref, land_ref, cover_ref, flat_ref, perm_ref, pick_ref, edge_ref, sems):
+def pack_kernel(cube_ref, cover_hbm, out_ref, land_ref, cover_ref, flat_ref, turned_ref, sums_ref, pick_ref, edge_ref, sems):
     ch, ny, nx = cube_ref.shape
-    n_rows, n_cols = ny // TILE_Y, nx // TILE_X
+    n_rows, spans = ny // TILE_Y, nx // LANES
+    n_cols, tiles = nx // TILE_X, LANES // TILE_X
     copies = [pltpu.make_async_copy(cube_ref.at[c], land_ref.at[c], sems.at[c]) for c in range(ch)]
     cover_copy = pltpu.make_async_copy(cover_hbm, cover_ref, sems.at[ch])
     cover_copy.start()
     for copy in copies:
         copy.start()
 
-    block = TILE_X * ch
-    x_row, x_col = iota((block, nx), 0), iota((block, nx), 1)
-    code = (x_col - x_row // ch) * ch + x_row % ch
     h_rows = len(HALO_GROUPS) * ch
-    h_row, h_col = iota((h_rows, nx), 0), iota((h_rows, nx), 1)
+    h_row, h_col = iota((h_rows, LANES), 0), iota((h_rows, LANES), 1)
     h_code = jnp.where((h_col % TILE_X) // PACK == h_row // ch, h_col // TILE_X * ch + h_row % ch, -1)
-    for t in range(n_cols):
+    for t in range(tiles):
         for c in range(ch):
-            lanes = slice(c * nx, (c + 1) * nx)
-            perm_ref[t * block : (t + 1) * block, lanes] = jnp.where(code == t * block + c, F32(1.0), F32(0.0)).astype(BF16)
-            pick_ref[t * h_rows : (t + 1) * h_rows, lanes] = jnp.where(h_code == t * ch + c, F32(1.0), F32(0.0)).astype(BF16)
+            hit = jnp.where(h_code == t * ch + c, F32(1.0), F32(0.0)).astype(BF16)
+            pick_ref[t * h_rows : (t + 1) * h_rows, c * LANES : (c + 1) * LANES] = hit
+    sums_ref[...] = jnp.zeros(sums_ref.shape, F32)
 
     cover_copy.wait()
     tile_x, tile_y = cover_ref.shape
     eye = jnp.where(iota((tile_y, tile_y), 0) == iota((tile_y, tile_y), 1), F32(1.0), F32(0.0)).astype(BF16)
-    cover = lax.dot_general(eye, cover_ref[...].astype(F32).astype(BF16), NT, preferred_element_type=F32)
-    lane_tile = iota((tile_y, nx), 1) // PT
-    wide = jnp.zeros((tile_y, nx), F32)
-    for j in range(tile_x):
-        wide = jnp.where(lane_tile == j, jnp.broadcast_to(cover[:, j : j + 1], wide.shape), wide)
-    mask = jnp.broadcast_to(wide[:, None, :], (tile_y, PT, nx)).reshape(ny, nx) > 0.5
-    sums = []
-    for c in range(ch):
-        copies[c].wait()
-        plane = jnp.where(mask, land_ref[c].astype(F32), F32(0.0))
-        sums.append(jnp.sum(plane * plane, axis=0, keepdims=True))
-        flat_ref[:, c * nx : (c + 1) * nx] = plane.astype(BF16)
-
-    cut = HALO * ch
-    for first in range(0, n_rows, 2):
-        pair = range(first, min(first + 2, n_rows))
-        here = flat_ref[first * TILE_Y : (pair[-1] + 1) * TILE_Y, :]
-        main = lax.dot_general(perm_ref[...], here, NT, preferred_element_type=F32).astype(BF16)
-        for r in pair:
-            lanes = slice((r - first) * TILE_Y, (r - first + 1) * TILE_Y)
-            for t in range(n_cols):
-                tile = main[t * block : (t + 1) * block, lanes]
-                out_ref[r * n_cols + t, ch : ch + cut, :] = tile[:cut]
-                out_ref[r * n_cols + t, (HALO_GROUPS[1] + 1) * ch : HALO_GROUPS[2] * ch, :] = tile[cut:]
-
-    squares = jnp.minimum(jnp.sum(jnp.concatenate(sums, axis=0), axis=1, keepdims=True), F32(BIG))
+    cover = lax.dot_general(eye, cover_ref[...].astype(F32).astype(BF16), NT, preferred_element_type=F32).astype(BF16)
+
+    def transpose(span, wait):
+        at = span * LANES if isinstance(span, int) else pl.multiple_of(span * LANES, LANES)
+        widen = jnp.where(iota((tile_x, LANES), 0) == span * tiles + iota((tile_x, LANES), 1) // PT, F32(1.0), F32(0.0))
+        wide = jnp.dot(cover, widen.astype(BF16), preferred_element_type=F32)
+        mask = jnp.broadcast_to(wide[:, None, :], (tile_y, PT, LANES)).reshape(ny, LANES) > 0.5
+        for c in range(ch):
+            if wait:
+                copies[c].wait()
+            plane = jnp.where(mask, land_ref[c, :, pl.ds(at, LANES)].astype(F32), F32(0.0))
+            sums_ref[c : c + 1, :] += jnp.sum(plane * plane, axis=0, keepdims=True)
+            flat_ref[span, :, c * LANES : (c + 1) * LANES] = plane.astype(BF16)
+            turned = plane.T
+            for r in range(n_rows):
+                turned_ref[r, c * TURN : c * TURN + LANES, :] = turned[:, r * TILE_Y : (r + 1) * TILE_Y]
+        for x in range(LANES):
+            group = column_group(x % TILE_X)
+            for r in range(n_rows):
+                dest = r * n_cols + span * tiles + x // TILE_X
+                column = turned_ref[r, pl.ds(x, ch, stride=TURN), :]
+                out_ref[dest, group * ch : (group + 1) * ch, :] = column.astype(BF16)
+
+    if spans == 1:
+        transpose(0, True)
+    else:
+        for copy in copies:
+            copy.wait()
+        lax.fori_loop(0, spans, lambda span, carry: (transpose(span, False), carry)[1], 0)
+
+    squares = jnp.minimum(jnp.sum(sums_ref[...], axis=1, keepdims=True), F32(BIG))
     high = squares.astype(BF16).astype(F32)
     mid = (squares - high).astype(BF16).astype(F32)
     low = squares - high - mid
-    keep = (iota((LANES, ch * nx), 1) % TILE_X) % PACK == iota((LANES, ch * nx), 0) // (2 * HALO)
+    keep = (iota((LANES, ch * LANES), 1) % TILE_X) % PACK == iota((LANES, ch * LANES), 0) // (2 * HALO)
     spread_row, spread_col = iota((LANES, 2 * PT), 0), iota((LANES, 2 * PT), 1)
     part = spread_row % (2 * HALO)
     spread = jnp.where((spread_col == part + PT - HALO) & (spread_row < PACK * 2 * HALO), F32(1.0), F32(0.0)).astype(BF16)
@@ -193,25 +197,33 @@
     extra = jnp.where((s_row < ch) & (s_col == LANES - 2), three(high), F32(0.0))
     extra = jnp.where((s_row < ch) & (s_col == LANES - 1), three(mid), extra)
     extra = jnp.where((s_row >= ch) & (s_row < 2 * ch) & (s_col == LANES - 2), three(low), extra)
-    zeros = jnp.zeros((PT, ch * nx), BF16)
-    for r in range(n_rows):
-        above = flat_ref[r * TILE_Y - PT : r * TILE_Y, :] if r else zeros
-        below = flat_ref[(r + 1) * TILE_Y : (r + 1) * TILE_Y + PT, :] if r < n_rows - 1 else zeros
-        edge = jnp.dot(spread, jnp.concatenate([above, below], axis=0), preferred_element_type=F32)
-        edge_ref[r * LANES : (r + 1) * LANES, :] = jnp.where(keep, edge, F32(0.0)).astype(BF16)
-    halos = lax.dot_general(pick_ref[...], edge_ref[...], NT, preferred_element_type=F32)
-    for r in range(n_rows):
-        for t in range(n_cols):
-            halo = (halos[t * h_rows : (t + 1) * h_rows, r * LANES : (r + 1) * LANES] + extra).astype(BF16)
-            for index, group in enumerate(HALO_GROUPS):
-                out_ref[r * n_cols + t, group * ch : (group + 1) * ch, :] = halo[index * ch : (index + 1) * ch]
+    zeros = jnp.zeros((PT, ch * LANES), BF16)
+
+    def halos(span):
+        for r in range(n_rows):
+            above = flat_ref[span, r * TILE_Y - PT : r * TILE_Y, :] if r else zeros
+            below = flat_ref[span, (r + 1) * TILE_Y : (r + 1) * TILE_Y + PT, :] if r < n_rows - 1 else zeros
+            edge = jnp.dot(spread, jnp.concatenate([above, below], axis=0), preferred_element_type=F32)
+            edge_ref[r * LANES : (r + 1) * LANES, :] = jnp.where(keep, edge, F32(0.0)).astype(BF16)
+        packed = lax.dot_general(pick_ref[...], edge_ref[...], NT, preferred_element_type=F32)
+        for r in range(n_rows):
+            for t in range(tiles):
+                halo = (packed[t * h_rows : (t + 1) * h_rows, r * LANES : (r + 1) * LANES] + extra).astype(BF16)
+                for index, group in enumerate(HALO_GROUPS):
+                    rows = halo[index * ch : (index + 1) * ch]
+                    out_ref[r * n_cols + span * tiles + t, group * ch : (group + 1) * ch, :] = rows
+
+    if spans == 1:
+        halos(0)
+    else:
+        lax.fori_loop(0, spans, lambda span, carry: (halos(span), carry)[1], 0)
 
 
 def pack(cube, footprint):
     ch, ny, nx = cube.shape
-    n_rows, n_cols = ny // TILE_Y, nx // TILE_X
-    h_rows = len(HALO_GROUPS) * ch
-    need = 2 * (4 * ch * ny * nx + (n_cols * (TILE_X * ch + h_rows) + n_rows * LANES) * ch * nx)
+    n_rows, n_cols, spans = ny // TILE_Y, nx // TILE_X, nx // LANES
+    h_rows = len(HALO_GROUPS) * ch * (LANES // TILE_X)
+    need = 2 * ch * (3 * ny * nx + (2 * ny + h_rows + n_rows * LANES) * LANES)
     return pl.pallas_call(
         pack_kernel,
         out_shape=jax.ShapeDtypeStruct((n_rows * n_cols, GROUPS * ch, LANES), BF16),
@@ -220,10 +232,11 @@
         scratch_shapes=[
             pltpu.VMEM((ch, ny, nx), BF16),
             pltpu.VMEM((nx // PT, ny // PT), jnp.int32),
-            pltpu.VMEM((ny, ch * nx), BF16),
-            pltpu.VMEM((n_cols * TILE_X * ch, ch * nx), BF16),
-            pltpu.VMEM((n_cols * h_rows, ch * nx), BF16),
-            pltpu.VMEM((n_rows * LANES, ch * nx), BF16),
+            pltpu.VMEM((spans, ny, ch * LANES), BF16),
+            pltpu.VMEM((n_rows, ch * TURN, TILE_Y), F32),
+            pltpu.VMEM((ch, LANES), F32),
+            pltpu.VMEM((h_rows, ch * LANES), BF16),
+            pltpu.VMEM((n_rows * LANES, ch * LANES), BF16),
             pltpu.SemaphoreType.DMA((ch + 1,)),
         ],
         compiler_params=pltpu.CompilerParams(vmem_limit_bytes=min(need + 12 * 2**20, 62 * 2**20)),
@@ -267,8 +280,29 @@
     return jnp.dot(weights_ref[...], slab, preferred_element_type=F32)
 
 
-def begin_kernel(own_ref, near_ref, main_ref, halo_ref, *rest):
-    x_refs, sum_ref, rows_ref = rest[:SMAX], rest[SMAX], rest[SMAX + 1]
+def scale_rows(sigma_ref, taps_ref, cover_ref, footprint_ref, own_ref, first, part):
+    lane = iota((8, 2 * LANES), 1)
+    pick = jnp.where((lane >= LANES - 2) & (lane < LANES) | (lane == 2 * LANES - 2), F32(1.0), F32(0.0)).astype(BF16)
+    both = jnp.concatenate([load(own_ref, first, part, group) for group in HALO_GROUPS[:2]], axis=1)
+    squares = lax.dot_general(pick, both, NT, preferred_element_type=F32)
+    squares = jnp.where(squares >= F32(BIG), F32(jnp.inf), squares)
+    count = jnp.maximum(jnp.sum(footprint_ref[...].astype(F32), keepdims=True) * F32(PT * PT), F32(1.0))
+    noise = jnp.sqrt(squares / count + F32(1e-06))
+    tile_x, tile_y = lax.axis_index("tx") * (TILE_X // PT), lax.axis_index("ty") * (TILE_Y // PT)
+    seen = jnp.zeros(noise.shape, F32)
+    for group in range(TILE_Y // PT):
+        seen = jnp.where(iota(noise.shape, 0) == group, cover_ref[tile_x, tile_y + group].astype(F32), seen)
+    energy = [F32(float(np.sum(t * t, dtype=np.float32))) for t in tap_table()]
+    for scale in range(NSC):
+        width = jnp.full(noise.shape, taps_ref[0, scale], jnp.int32).astype(F32)
+        knorm = jnp.full(noise.shape, energy[0], F32)
+        for index in range(1, SMAX):
+            knorm = jnp.where(sigma_ref[scale] == index + 1, energy[index], knorm)
+        yield scale, seen / (noise * (knorm / jnp.sqrt(width)) * width)
+
+
+def begin_kernel(sigma_ref, taps_ref, cover_ref, footprint_ref, own_ref, near_ref, main_ref, halo_ref, *rest):
+    x_refs, sum_ref, scale_ref, rows_ref = rest[:SMAX], *rest[SMAX : SMAX + 3]
     senders, _, ch, _ = own_ref.shape
     part = min(senders, WIDE // ch)
     odd = odd_tile()
@@ -282,6 +316,8 @@
         for x in range(TILE_X):
             passed(own_ref, first, part, *right_column(x), x=choose(odd, HALO + x, x))
         lanes = pl.ds(pl.multiple_of(first * ch, part * ch), part * ch)
+        for scale, value in scale_rows(sigma_ref, taps_ref, cover_ref, footprint_ref, own_ref, first, part):
+            scale_ref[scale, :, lanes] = value
         for group in range(TILE_Y // PT):
             for kind in range(SMAX):
                 reach = 3 * (kind + 1)
@@ -295,54 +331,37 @@
         lax.fori_loop(0, senders // part, one, 0)
 
 
-def begin(own, near, main, halo, weights):
+def begin(kernel_sigmas, spectral_taps, footprint, own, near, main, halo, weights):
     senders, _, ch, _ = own.shape
     channels = senders * ch
     wide = min(channels, WIDE)
     rows = (SMAX, TILE_Y // PT, TILE_X + HALO, PT, wide)
     sums = (SMAX, TILE_Y // PT, PT * TILE_X, channels)
+    smem = pl.BlockSpec(memory_space=pltpu.SMEM)
     vmem = pl.BlockSpec(memory_space=pltpu.VMEM)
     limit = 2 * int(np.prod(rows)) + 6 * 2**20 if channels <= WIDE else 62 * 2**20
     return pl.pallas_call(
         begin_kernel,
-        out_shape=jax.ShapeDtypeStruct(sums, F32),
-        in_specs=[vmem] * (4 + len(weights)),
-        out_specs=vmem,
+        out_shape=[jax.ShapeDtypeStruct(sums, F32), jax.ShapeDtypeStruct((NSC, TILE_Y // PT, channels), F32)],
+        in_specs=[smem] * 3 + [vmem] * (5 + len(weights)),
+        out_specs=[vmem] * 2,
         scratch_shapes=[pltpu.VMEM(rows, BF16)],
         compiler_params=pltpu.CompilerParams(vmem_limit_bytes=limit),
         cost_estimate=pl.CostEstimate(flops=10**9, bytes_accessed=8 * 10**6, transcendentals=0),
         name="begin",
-    )(own, near, main, halo, *weights)
-
-
-def finish_kernel(sigma_ref, taps_ref, cover_ref, footprint_ref, own_ref, far_ref, sum_ref, main_ref, halo_ref, *rest):
-    far_refs, box_ref, out_ref, rows_ref, scale_ref, stage_ref, sems = rest[:SMAX], *rest[SMAX : SMAX + 6]
-    smooth_refs = rest[SMAX + 6 :]
-    senders, _, ch, _ = own_ref.shape
+    )(kernel_sigmas, spectral_taps, footprint.T, footprint.T, own, near, main, halo, *weights)
+
+
+def finish_kernel(sigma_ref, far_ref, sum_ref, scale_ref, main_ref, halo_ref, *rest):
+    far_refs, box_ref, out_ref, rows_ref, stage_ref, sems = rest[:SMAX], *rest[SMAX : SMAX + 5]
+    smooth_refs = rest[SMAX + 5 :]
+    senders, _, ch, _ = far_ref.shape
     channels = senders * ch
     part = min(senders, WIDE // ch)
     odd = odd_tile()
-    tile_x, tile_y = lax.axis_index("tx") * (TILE_X // PT), lax.axis_index("ty") * (TILE_Y // PT)
     slots, _, tall = stage_ref.shape[:3]
     span, phases = tall // PT, TILE_Y // tall
     wide, edge = min(channels, WIDE), margin(channels)
-
-    lane = iota((8, 2 * LANES), 1)
-    pick = jnp.where((lane >= LANES - 2) & (lane < LANES) | (lane == 2 * LANES - 2), F32(1.0), F32(0.0)).astype(BF16)
-    for first in range(0, senders, part):
-        both = jnp.concatenate([load(own_ref, first, part, group) for group in HALO_GROUPS[:2]], axis=1)
-        squares = lax.dot_general(pick, both, NT, preferred_element_type=F32)
-        squares = jnp.where(squares >= F32(BIG), F32(jnp.inf), squares)
-        count = jnp.maximum(jnp.sum(footprint_ref[...].astype(F32), keepdims=True) * F32(PT * PT), F32(1.0))
-        noise = jnp.sqrt(squares / count + F32(1e-06))
-        energy = [F32(float(np.sum(t * t, dtype=np.float32))) for t in tap_table()]
-        for scale in range(NSC):
-            width = jnp.full(noise.shape, taps_ref[0, scale], jnp.int32).astype(F32)
-            knorm = jnp.full(noise.shape, energy[0], F32)
-            for index in range(1, SMAX):
-                knorm = jnp.where(sigma_ref[scale] == index + 1, energy[index], knorm)
-            knorm = knorm / jnp.sqrt(width)
-            scale_ref[scale, :, first * ch : (first + part) * ch] = F32(1.0) / (noise * knorm * width)
 
     def out_copy(phase, slot, scale):
         there = out_ref.at[scale, pl.ds(phase * tall, tall)]
@@ -367,13 +386,13 @@
             if phase >= slots:
                 out_copy(phase - slots, slot, scale).wait()
             for row in range(span):
-                seen = cover_ref[tile_x, tile_y + phase * span + row].astype(F32)
+                group = phase * span + row
                 for at in range(0, channels, wide):
                     lanes, first = slice(at, at + wide), at - edge
                     low, high = max(first, 0), min(at + wide + edge, channels)
                     field = smooth_refs[phase][sigma_ref[scale] - 1, row, :, low:high]
                     boxed = jnp.dot(field, box_ref[scale, low - first : high - first], preferred_element_type=F32)
-                    scaled = (boxed * (scale_ref[scale, 0:1, lanes] * seen)).astype(BF16)
+                    scaled = (boxed * scale_ref[scale, group : group + 1, lanes]).astype(BF16)
                     stage_ref[slot, scale, row * PT : (row + 1) * PT, :, lanes] = scaled.reshape(PT, TILE_X, wide)
             out_copy(phase, slot, scale).start()
 
@@ -392,33 +411,32 @@
             out_copy(phase, phase % slots, scale).wait()
 
 
-def finish(kernel_sigmas, spectral_taps, footprint, own, far, sums, main, halo, weights, box):
-    senders, _, ch, _ = own.shape
+def finish(kernel_sigmas, far, sums, scales, main, halo, weights, box):
+    senders, _, ch, _ = far.shape
     channels = senders * ch
     wide = min(channels, WIDE)
     span = SPAN if channels <= WIDE else 1
     phases = TILE_Y // PT // span
+    slots = min(2, phases)
     rows = (SMAX, TILE_Y // PT, HALO, PT, wide)
-    need = 2 * int(np.prod(rows)) + 2 * channels * (2 * span * NSC + SMAX * TILE_Y // PT) * PT * TILE_X
-    smem = pl.BlockSpec(memory_space=pltpu.SMEM)
+    need = 2 * int(np.prod(rows)) + 2 * channels * (slots * span * NSC + SMAX * TILE_Y // PT) * PT * TILE_X
     vmem = pl.BlockSpec(memory_space=pltpu.VMEM)
     return pl.pallas_call(
         finish_kernel,
         out_shape=jax.ShapeDtypeStruct((NSC, TILE_Y, TILE_X, channels), BF16),
-        in_specs=[smem] * 3 + [vmem] * (7 + len(weights)),
+        in_specs=[pl.BlockSpec(memory_space=pltpu.SMEM)] + [vmem] * (6 + len(weights)),
         out_specs=pl.BlockSpec(memory_space=pltpu.MemorySpace.HBM),
         scratch_shapes=[
             pltpu.VMEM(rows, BF16),
-            pltpu.VMEM((NSC, 8, channels), F32),
-            pltpu.VMEM((2, NSC, span * PT, TILE_X, channels), BF16),
-            pltpu.SemaphoreType.DMA((2, NSC)),
+            pltpu.VMEM((slots, NSC, span * PT, TILE_X, channels), BF16),
+            pltpu.SemaphoreType.DMA((slots, NSC)),
         ]
         + [pltpu.VMEM((SMAX, span, PT * TILE_X, channels), BF16)] * phases,
         compiler_params=pltpu.CompilerParams(
             vmem_limit_bytes=need + 6 * 2**20 if channels <= WIDE else 62 * 2**20
         ),
         name="finish",
-    )(kernel_sigmas, spectral_taps, footprint.T, footprint.T, own, far, sums, main, halo, *weights, box)
+    )(kernel_sigmas, far, sums, scales, main, halo, *weights, box)
 
 
 def local(channel_cube, footprint, kernel_sigmas, spectral_taps):
@@ -435,8 +453,8 @@
     far = lax.ppermute(far, "tx", both(far_pairs))
     near = lax.ppermute(near, "tx", both(near_pairs))
     main, halo, *weights, box = tables(spectral_taps, channels)
-    sums = begin(own, near, main, halo, weights[:SMAX])
-    return finish(kernel_sigmas, spectral_taps, footprint, own, far, sums, main, halo, weights[SMAX:], box)
+    sums, scales = begin(kernel_sigmas, spectral_taps, footprint, own, near, main, halo, weights[:SMAX])
+    return finish(kernel_sigmas, far, sums, scales, main, halo, weights[SMAX:], box)
 
 
 def solution(mesh):

time: 60.2 us -> 59.3 us (0.985)
    pallas_call x1, Pallas kernels: 3.29 us -> 3.96 us  [begin(): pl.pallas_call(begin_kernel, out_shape=[jax.ShapeDtypeStruct(sums, F32),...]
    pallas_call x1, Pallas kernels: 3.54 us -> 2.93 us  [pack(): pl.pallas_call(pack_kernel, out_shape=jax.ShapeDtypeStruct((n_rows * n_co...]
  transfers between devices with their start and end apart: 2 -> 2, of which waited for: 1 -> 1; matrix products, arithmetic and copies ran while one was open for 0% -> 0% of each run, Pallas kernels for 11% -> 12%
where the time goes in v4:
time: 59.3 us; the launch traced here: 59.1 us
  blocking collectives  38.5 us (65%)
  Pallas kernels  14.8 us (25%)
  waiting for transfers between devices  3.36 us (6%)
  starting transfers between devices  2.32 us (4%)
    all_to_all x1, blocking collectives, local(): lax.all_to_all(packed, ('ty', 'tx'), split_axis=0, concat_axis=0, tiled=T...  38.5 us
    pallas_call x1, Pallas kernels, finish(): pl.pallas_call(finish_kernel, out_shape=jax.ShapeDtypeStruct((NSC, TILE_Y...  4.56 us
    pallas_call x1, Pallas kernels, begin(): pl.pallas_call(begin_kernel, out_shape=[jax.ShapeDtypeStruct(sums, F32),...  3.96 us
    ppermute x1, waiting for transfers between devices, local(): far = lax.ppermute(far, 'tx', both(far_pairs))  3.36 us
    pallas_call x1, Pallas kernels, tables(): pl.pallas_call(functools.partial(tables_kernel, channels), out_shape=[jax...  3.28 us
    pallas_call x1, Pallas kernels, pack(): pl.pallas_call(pack_kernel, out_shape=jax.ShapeDtypeStruct((n_rows * n_co...  2.93 us
    ppermute x1, starting transfers between devices, local(): far = lax.ppermute(far, 'tx', both(far_pairs))  1.94 us
  transfers between devices with their start and end apart: 2, of which 1 were waited for; matrix products, arithmetic and copies ran while one was open for 0% of the time, Pallas kernels for 12%

profile of v4, /device:TPU:1, one launch (start us, length us, event | category | flops | bytes accessed | tf_op | source)
XLA Modules:
  0.0 59.1 jit_solution(3530892591205746560)
XLA Ops:
  0.0 0.0 copy-start.2
  0.0 0.0 copy-start
  0.0 0.0 copy-start.1
  0.0 2.9 %pack.1 = bf16[32,152,128]{2,1,0:T(8,128)(2,1)S(1)} custom-call(bf16[8,512,128]{2,1,0:T(8,128)(2,1)} %cube_ref.1, s32[8,32]{1,0:T(8,128)} %bitcast.5), custom_call_target="tpu_custom_call" | custom-call | tf_op jit(solution)/shard_map/pack/pallas_call | solution.py:227
  2.9 38.5 %all_to_all.5 = bf16[32,152,128]{2,1,0:T(8,128)(2,1)S(1)} all-to-all(bf16[32,152,128]{2,1,0:T(8,128)(2,1)S(1)} %pack.1), channel_id=1, replica_groups=mesh['ty'=4,'tx'=8] {'ty','tx'}, dimensions={0} | all-to-all | bytes 2490368 | tf_op jit(solution)/shard_map/all_to_all | solution.py:447
  41.5 0.1 cut_near.1
  41.5 0.4 collective-permute-start.1
  41.9 0.1 cut_far.1
  42.0 1.9 %collective-permute-start = (bf16[32,11,8,128]{3,2,1,0:T(8,128)(2,1)S(1)}, bf16[32,11,8,128]{3,2,1,0:T(8,128)(2,1)S(1)}, u32[]{:S(2)}, u32[]{:S(2)}) collective-permute-start(bf16[32,11,8,128]{3,2,1,0:T(8,128)(2,1)S(1)} %cut_far.1), channel_id=1, source_target_pairs={{1,2},{3,4},{5,6},{2,1},{4,3},{6,5},{9,10},{11,12},{13,14},{10,9},... | collective-permute-start | bytes 2162696 | tf_op jit(solution)/shard_map/ppermute | solution.py:453
  43.9 0.0 copy-done.2
  43.9 3.3 %tables.1 = (bf16[384,128]{1,0:T(8,128)(2,1)S(1)}, bf16[7,384,128]{2,1,0:T(8,128)(2,1)S(1)}, bf16[256,304]{1,0:T(8,128)(2,1)S(1)}, bf16[256,352]{1,0:T(8,128)(2,...) custom-call(s32[2,4]{1,0:T(2,128)S(1)} %copy-done.2), custom_call_target="tpu_custom_call" | custom-call | flops 10000000 | bytes 4000000 | tf_op jit(solution)/shard_map/tables/pallas_call | solution.py:124
  47.2 0.0 collective-permute-done.1.near_ref
  47.2 0.0 copy-done
  47.2 0.0 copy-done.1
  47.2 4.0 %begin.1 = (f32[3,8,256,256]{3,2,1,0:T(8,128)S(1)}, f32[4,8,256]{2,1,0:T(8,128)S(1)}) custom-call(s32[4]{0:T(128)S(1)} %copy-done.1, s32[2,4]{1,0:T(2,128)S(1)} %copy-done.2, s32[8,32]{1,0:T(8,128)S(1)} %bitcast.6, s32[8,32]{1,0:T(8,128)S(1)} %bitcast.7, bf16[32,19,8,128]{3,2,1,0:T(8,128)(2,1)S(1)} %bitcast.4, ...), custom_call_target="tpu_custom_call" | custom-call | flops 1000000000 | bytes 8000000 | tf_op jit(solution)/shard_map/begin/pallas_call | solution.py:343
  51.2 3.4 %collective-permute-done.far_ref = bf16[32,11,8,128]{3,2,1,0:T(8,128)(2,1)S(1)} collective-permute-done((bf16[32,11,8,128]{3,2,1,0:T(8,128)(2,1)S(1)}, bf16[32,11,8,128]{3,2,1,0:T(8,128)(2,1)S(1)}, u32[]{:S(2)}, u32[]{:S(2)}) %collective-permute-start) | collective-permute-done | bytes 720928 | tf_op jit(solution)/shard_map/ppermute | solution.py:453
  54.6 4.6 %finish.1 = bf16[4,128,16,256]{3,2,1,0:T(8,128)(2,1)} custom-call(s32[4]{0:T(128)S(1)} %copy-done.1, bf16[32,11,8,128]{3,2,1,0:T(8,128)(2,1)S(1)} %collective-permute-done.far_ref, f32[3,8,256,256]{3,2,1,0:T(8,128)S(1)} %get-tuple-element.21.sum_ref, f32[4,8,256]{2,1,0:T(8,128)S(1)} %get-tuple-element.22.scale_ref, ...), custom_call_target="tpu_custom_call" | custom-call | tf_op jit(solution)/shard_map/finish/pallas_call | solution.py:424
Async XLA Ops:
  0.0 43.9 %copy-start.2 = (s32[2,4]{1,0:T(2,128)S(1)}, s32[2,4]{1,0:T(2,128)}, u32[]{:S(2)}) copy-start(s32[2,4]{1,0:T(2,128)} %taps_ref.3) | copy-start | bytes 100
  0.0 47.2 %copy-start = (s32[32,8]{0,1:T(8,128)S(1)}, s32[32,8]{0,1:T(8,128)}, u32[]{:S(2)}) copy-start(s32[32,8]{0,1:T(8,128)} %param.5) | copy-start | bytes 3076
  0.0 47.2 %copy-start.1 = (s32[4]{0:T(128)S(1)}, s32[4]{0:T(128)}, u32[]{:S(2)}) copy-start(s32[4]{0:T(128)} %sigma_ref.3) | copy-start | bytes 52
  41.5 5.7 %collective-permute-start.1 = (bf16[32,11,8,128]{3,2,1,0:T(8,128)(2,1)S(1)}, bf16[32,11,8,128]{3,2,1,0:T(8,128)(2,1)S(1)}, u32[]{:S(2)}, u32[]{:S(2)}) collective-permute-start(bf16[32,11,8,128]{3,2,1,0:T(8,128)(2,1)S(1)} %cut_near.1), channel_id=1, source_target_pairs={{0,1},{2,3},{4,5},{6,7},{1,0},{3,2},{5,4},{7,6},{8,9},{10,11},{12,... | collective-permute-start | bytes 2162696 | tf_op jit(solution)/shard_map/ppermute | solution.py:454
  42.0 12.6 %collective-permute-start = (bf16[32,11,8,128]{3,2,1,0:T(8,128)(2,1)S(1)}, bf16[32,11,8,128]{3,2,1,0:T(8,128)(2,1)S(1)}, u32[]{:S(2)}, u32[]{:S(2)}) collective-permute-start(bf16[32,11,8,128]{3,2,1,0:T(8,128)(2,1)S(1)} %cut_far.1), channel_id=1, source_target_pairs={{1,2},{3,4},{5,6},{2,1},{4,3},{6,5},{9,10},{11,12},{13,14},{10,9},... | collective-permute-start | bytes 2162696 | tf_op jit(solution)/shard_map/ppermute | solution.py:453

commit v5 on v4

--- a/solution.py
+++ b/solution.py
@@ -11,6 +11,7 @@
 
 TILE_Y = 128
 TILE_X = 16
+HALF = TILE_X // 2
 NSC = 4
 WMAX = 5
 PT = 16
@@ -102,8 +103,10 @@
         reach = 3 * sigma
         for ref, shift in ((x_refs[index], choose(odd, -reach, 0)), (far_refs[index], choose(odd, TILE_X, -reach))):
             row, col = iota(ref.shape, 0), iota(ref.shape, 1)
-            weight = taps_at(col // PT - row % TILE_X + shift, taps[index], sigma)
-            ref[...] = jnp.where(row // TILE_X == col % PT, weight, F32(0.0)).astype(BF16)
+            first = 0 if ref.shape[0] == PT * TILE_X else odd * HALF
+            out_x = first + row // (PT * HALF) * HALF + row % HALF
+            weight = taps_at(col // PT - out_x + shift, taps[index], sigma)
+            ref[...] = jnp.where(row % (PT * HALF) // HALF == col % PT, weight, F32(0.0)).astype(BF16)
     for scale in range(NSC):
         width, dilation = taps_ref[0, scale], taps_ref[1, scale]
         shape = box_ref.shape[1:]
@@ -118,7 +121,7 @@
 def tables(spectral_taps, channels):
     shapes = [(SMAX * TILE_Y, LANES), (PACK, SMAX * TILE_Y, LANES)]
     shapes += [(PT * TILE_X, (TILE_X + 3 * (i + 1)) * PT) for i in range(SMAX)]
-    shapes += [(PT * TILE_X, 3 * (i + 1) * PT) for i in range(SMAX)]
+    shapes += [(PT * (HALF if 3 * (i + 1) <= HALF else TILE_X), 3 * (i + 1) * PT) for i in range(SMAX)]
     wide = min(channels, WIDE)
     shapes += [(NSC, wide + 2 * margin(channels), wide)]
     return pl.pallas_call(
@@ -132,7 +135,7 @@
     )(spectral_taps)
 
 
-def pack_kernel(cube_ref, cover_hbm, out_ref, land_ref, cover_ref, flat_ref, turned_ref, sums_ref, pick_ref, edge_ref, sems):
+def pack_kernel(cube_ref, cover_hbm, out_ref, land_ref, cover_ref, turned_ref, sums_ref, sems):
     ch, ny, nx = cube_ref.shape
     n_rows, spans = ny // TILE_Y, nx // LANES
     n_cols, tiles = nx // TILE_X, LANES // TILE_X
@@ -141,16 +144,7 @@
     cover_copy.start()
     for copy in copies:
         copy.start()
-
-    h_rows = len(HALO_GROUPS) * ch
-    h_row, h_col = iota((h_rows, LANES), 0), iota((h_rows, LANES), 1)
-    h_code = jnp.where((h_col % TILE_X) // PACK == h_row // ch, h_col // TILE_X * ch + h_row % ch, -1)
-    for t in range(tiles):
-        for c in range(ch):
-            hit = jnp.where(h_code == t * ch + c, F32(1.0), F32(0.0)).astype(BF16)
-            pick_ref[t * h_rows : (t + 1) * h_rows, c * LANES : (c + 1) * LANES] = hit
     sums_ref[...] = jnp.zeros(sums_ref.shape, F32)
-
     cover_copy.wait()
     tile_x, tile_y = cover_ref.shape
     eye = jnp.where(iota((tile_y, tile_y), 0) == iota((tile_y, tile_y), 1), F32(1.0), F32(0.0)).astype(BF16)
@@ -166,16 +160,28 @@
                 copies[c].wait()
             plane = jnp.where(mask, land_ref[c, :, pl.ds(at, LANES)].astype(F32), F32(0.0))
             sums_ref[c : c + 1, :] += jnp.sum(plane * plane, axis=0, keepdims=True)
-            flat_ref[span, :, c * LANES : (c + 1) * LANES] = plane.astype(BF16)
             turned = plane.T
             for r in range(n_rows):
-                turned_ref[r, c * TURN : c * TURN + LANES, :] = turned[:, r * TILE_Y : (r + 1) * TILE_Y]
-        for x in range(LANES):
-            group = column_group(x % TILE_X)
-            for r in range(n_rows):
-                dest = r * n_cols + span * tiles + x // TILE_X
-                column = turned_ref[r, pl.ds(x, ch, stride=TURN), :]
-                out_ref[dest, group * ch : (group + 1) * ch, :] = column.astype(BF16)
+                turned_ref[span, r, c * TURN : c * TURN + LANES, :] = turned[:, r * TILE_Y : (r + 1) * TILE_Y]
+
+    def send(span, firsts):
+        lane = iota((ch, LANES), 1)
+        for t in range(tiles):
+            for index, halo_group in enumerate(HALO_GROUPS):
+                halos = [firsts[index]] * n_rows
+                for x in range(index * PACK, min((index + 1) * PACK, TILE_X)):
+                    slot, group = x % PACK * 2 * HALO, column_group(x)
+                    columns = [turned_ref[span, r, pl.ds(t * TILE_X + x, ch, stride=TURN), :] for r in range(n_rows)]
+                    ends = [jnp.zeros((ch, LANES), F32)]
+                    around = ends + columns + ends
+                    for r in range(n_rows):
+                        dest = r * n_cols + span * tiles + t
+                        out_ref[dest, group * ch : (group + 1) * ch, :] = columns[r].astype(BF16)
+                        edge = pltpu.roll(jnp.where(lane < LANES // 2, around[r + 2], around[r]), slot + HALO, 1)
+                        halos[r] = jnp.where((lane >= slot) & (lane < slot + 2 * HALO), edge, halos[r])
+                for r in range(n_rows):
+                    dest = r * n_cols + span * tiles + t
+                    out_ref[dest, halo_group * ch : (halo_group + 1) * ch, :] = halos[r].astype(BF16)
 
     if spans == 1:
         transpose(0, True)
@@ -184,46 +190,24 @@
             copy.wait()
         lax.fori_loop(0, spans, lambda span, carry: (transpose(span, False), carry)[1], 0)
 
-    squares = jnp.minimum(jnp.sum(sums_ref[...], axis=1, keepdims=True), F32(BIG))
+    squares = jnp.minimum(jnp.sum(sums_ref[...], axis=1, keepdims=True) * F32(0.25), F32(BIG))
     high = squares.astype(BF16).astype(F32)
     mid = (squares - high).astype(BF16).astype(F32)
     low = squares - high - mid
-    keep = (iota((LANES, ch * LANES), 1) % TILE_X) % PACK == iota((LANES, ch * LANES), 0) // (2 * HALO)
-    spread_row, spread_col = iota((LANES, 2 * PT), 0), iota((LANES, 2 * PT), 1)
-    part = spread_row % (2 * HALO)
-    spread = jnp.where((spread_col == part + PT - HALO) & (spread_row < PACK * 2 * HALO), F32(1.0), F32(0.0)).astype(BF16)
-    s_row, s_col = iota((h_rows, LANES), 0), iota((h_rows, LANES), 1)
-    three = lambda value: jnp.concatenate([jnp.broadcast_to(value, (ch, LANES))] * len(HALO_GROUPS), axis=0)
-    extra = jnp.where((s_row < ch) & (s_col == LANES - 2), three(high), F32(0.0))
-    extra = jnp.where((s_row < ch) & (s_col == LANES - 1), three(mid), extra)
-    extra = jnp.where((s_row >= ch) & (s_row < 2 * ch) & (s_col == LANES - 2), three(low), extra)
-    zeros = jnp.zeros((PT, ch * LANES), BF16)
-
-    def halos(span):
-        for r in range(n_rows):
-            above = flat_ref[span, r * TILE_Y - PT : r * TILE_Y, :] if r else zeros
-            below = flat_ref[span, (r + 1) * TILE_Y : (r + 1) * TILE_Y + PT, :] if r < n_rows - 1 else zeros
-            edge = jnp.dot(spread, jnp.concatenate([above, below], axis=0), preferred_element_type=F32)
-            edge_ref[r * LANES : (r + 1) * LANES, :] = jnp.where(keep, edge, F32(0.0)).astype(BF16)
-        packed = lax.dot_general(pick_ref[...], edge_ref[...], NT, preferred_element_type=F32)
-        for r in range(n_rows):
-            for t in range(tiles):
-                halo = (packed[t * h_rows : (t + 1) * h_rows, r * LANES : (r + 1) * LANES] + extra).astype(BF16)
-                for index, group in enumerate(HALO_GROUPS):
-                    rows = halo[index * ch : (index + 1) * ch]
-                    out_ref[r * n_cols + span * tiles + t, group * ch : (group + 1) * ch, :] = rows
-
+    lane = iota((ch, LANES), 1)
+    put = lambda at, value, base: jnp.where(lane == at, jnp.broadcast_to(value, (ch, LANES)), base)
+    zeros = jnp.zeros((ch, LANES), F32)
+    firsts = (put(LANES - 1, mid, put(LANES - 2, high, zeros)), put(LANES - 2, low, zeros), zeros)
     if spans == 1:
-        halos(0)
+        send(0, firsts)
     else:
-        lax.fori_loop(0, spans, lambda span, carry: (halos(span), carry)[1], 0)
+        lax.fori_loop(0, spans, lambda span, carry: (send(span, firsts), carry)[1], 0)
 
 
 def pack(cube, footprint):
     ch, ny, nx = cube.shape
     n_rows, n_cols, spans = ny // TILE_Y, nx // TILE_X, nx // LANES
-    h_rows = len(HALO_GROUPS) * ch * (LANES // TILE_X)
-    need = 2 * ch * (3 * ny * nx + (2 * ny + h_rows + n_rows * LANES) * LANES)
+    need = 2 * ch * 4 * ny * nx
     return pl.pallas_call(
         pack_kernel,
         out_shape=jax.ShapeDtypeStruct((n_rows * n_cols, GROUPS * ch, LANES), BF16),
@@ -232,14 +216,11 @@
         scratch_shapes=[
             pltpu.VMEM((ch, ny, nx), BF16),
             pltpu.VMEM((nx // PT, ny // PT), jnp.int32),
-            pltpu.VMEM((spans, ny, ch * LANES), BF16),
-            pltpu.VMEM((n_rows, ch * TURN, TILE_Y), F32),
+            pltpu.VMEM((spans, n_rows, ch * TURN, TILE_Y), F32),
             pltpu.VMEM((ch, LANES), F32),
-            pltpu.VMEM((h_rows, ch * LANES), BF16),
-            pltpu.VMEM((n_rows * LANES, ch * LANES), BF16),
             pltpu.SemaphoreType.DMA((ch + 1,)),
         ],
-        compiler_params=pltpu.CompilerParams(vmem_limit_bytes=min(need + 12 * 2**20, 62 * 2**20)),
+        compiler_params=pltpu.CompilerParams(vmem_limit_bytes=need + 12 * 2**20),
         name="pack",
     )(in_hbm(cube), in_hbm(footprint.T))
 
@@ -284,8 +265,7 @@
     lane = iota((8, 2 * LANES), 1)
     pick = jnp.where((lane >= LANES - 2) & (lane < LANES) | (lane == 2 * LANES - 2), F32(1.0), F32(0.0)).astype(BF16)
     both = jnp.concatenate([load(own_ref, first, part, group) for group in HALO_GROUPS[:2]], axis=1)
-    squares = lax.dot_general(pick, both, NT, preferred_element_type=F32)
-    squares = jnp.where(squares >= F32(BIG), F32(jnp.inf), squares)
+    squares = lax.dot_general(pick, both, NT, preferred_element_type=F32) * F32(4.0)
     count = jnp.maximum(jnp.sum(footprint_ref[...].astype(F32), keepdims=True) * F32(PT * PT), F32(1.0))
     noise = jnp.sqrt(squares / count + F32(1e-06))
     tile_x, tile_y = lax.axis_index("tx") * (TILE_X // PT), lax.axis_index("ty") * (TILE_Y // PT)
@@ -322,7 +302,8 @@
             for kind in range(SMAX):
                 reach = 3 * (kind + 1)
                 start = choose(odd, HALO - reach, 0)
-                sum_ref[kind, group, :, lanes] = x_pass(rows_ref, kind, group, start, TILE_X + reach, x_refs[kind])
+                field = x_pass(rows_ref, kind, group, start, TILE_X + reach, x_refs[kind])
+                sum_ref[kind, group, :, :, lanes] = field.reshape(2, PT * HALF, part * ch)
         return carry
 
     if senders == part:
@@ -336,7 +317,7 @@
     channels = senders * ch
     wide = min(channels, WIDE)
     rows = (SMAX, TILE_Y // PT, TILE_X + HALO, PT, wide)
-    sums = (SMAX, TILE_Y // PT, PT * TILE_X, channels)
+    sums = (SMAX, TILE_Y // PT, 2, PT * HALF, channels)
     smem = pl.BlockSpec(memory_space=pltpu.SMEM)
     vmem = pl.BlockSpec(memory_space=pltpu.VMEM)
     limit = 2 * int(np.prod(rows)) + 6 * 2**20 if channels <= WIDE else 62 * 2**20
@@ -379,7 +360,12 @@
             for row in range(span):
                 group = phase * span + row
                 added = x_pass(rows_ref, kind, group, choose(odd, 0, HALO - reach), reach, far_refs[kind])
-                smooth_refs[phase][kind, row, :, lanes] = (sum_ref[kind, group, :, lanes] + added).astype(BF16)
+                added = added.reshape(-1, PT * HALF, part * ch)
+                if added.shape[0] == 2:
+                    smooth_refs[phase][kind, row, :, :, lanes] = (sum_ref[kind, group, :, :, lanes] + added).astype(BF16)
+                else:
+                    smooth_refs[phase][kind, row, odd, :, lanes] = (sum_ref[kind, group, odd, :, lanes] + added[0]).astype(BF16)
+                    smooth_refs[phase][kind, row, 1 - odd, :, lanes] = sum_ref[kind, group, 1 - odd, :, lanes].astype(BF16)
 
     def box_pass(phase, slot):
         for scale in range(NSC):
@@ -390,10 +376,13 @@
                 for at in range(0, channels, wide):
                     lanes, first = slice(at, at + wide), at - edge
                     low, high = max(first, 0), min(at + wide + edge, channels)
-                    field = smooth_refs[phase][sigma_ref[scale] - 1, row, :, low:high]
+                    field = smooth_refs[phase][sigma_ref[scale] - 1, row, :, :, low:high]
+                    field = field.reshape(PT * TILE_X, high - low)
                     boxed = jnp.dot(field, box_ref[scale, low - first : high - first], preferred_element_type=F32)
                     scaled = (boxed * scale_ref[scale, group : group + 1, lanes]).astype(BF16)
-                    stage_ref[slot, scale, row * PT : (row + 1) * PT, :, lanes] = scaled.reshape(PT, TILE_X, wide)
+                    scaled = scaled.reshape(2, PT, HALF, wide)
+                    for half in range(2):
+                        stage_ref[slot, scale, row * PT : (row + 1) * PT, half * HALF : (half + 1) * HALF, lanes] = scaled[half]
             out_copy(phase, slot, scale).start()
 
     whole = senders == part
@@ -431,7 +420,7 @@
             pltpu.VMEM((slots, NSC, span * PT, TILE_X, channels), BF16),
             pltpu.SemaphoreType.DMA((slots, NSC)),
         ]
-        + [pltpu.VMEM((SMAX, span, PT * TILE_X, channels), BF16)] * phases,
+        + [pltpu.VMEM((SMAX, span, 2, PT * HALF, channels), BF16)] * phases,
         compiler_params=pltpu.CompilerParams(
             vmem_limit_bytes=need + 6 * 2**20 if channels <= WIDE else 62 * 2**20
         ),

time: 59.3 us -> 58.5 us (0.987)
  Pallas kernels: 14.8 us -> 14 us
where the time goes in v5:
time: 58.5 us; the launch traced here: 58.3 us
  blocking collectives  38.5 us (66%)
  Pallas kernels  14 us (24%)
  waiting for transfers between devices  3.44 us (6%)
  starting transfers between devices  2.32 us (4%)
    all_to_all x1, blocking collectives, local(): lax.all_to_all(packed, ('ty', 'tx'), split_axis=0, concat_axis=0, tiled=T...  38.5 us
    pallas_call x1, Pallas kernels, finish(): pl.pallas_call(finish_kernel, out_shape=jax.ShapeDtypeStruct((NSC, TILE_Y...  4.27 us
    pallas_call x1, Pallas kernels, begin(): pl.pallas_call(begin_kernel, out_shape=[jax.ShapeDtypeStruct(sums, F32),...  3.96 us
    ppermute x1, waiting for transfers between devices, local(): far = lax.ppermute(far, 'tx', both(far_pairs))  3.44 us
    pallas_call x1, Pallas kernels, tables(): pl.pallas_call(functools.partial(tables_kernel, channels), out_shape=[jax...  3.2 us
    pallas_call x1, Pallas kernels, pack(): pl.pallas_call(pack_kernel, out_shape=jax.ShapeDtypeStruct((n_rows * n_co...  2.43 us
    ppermute x1, starting transfers between devices, local(): far = lax.ppermute(far, 'tx', both(far_pairs))  1.94 us
  transfers between devices with their start and end apart: 2, of which 1 were waited for; matrix products, arithmetic and copies ran while one was open for 0% of the time, Pallas kernels for 12%

profile of v5, /device:TPU:1, one launch (start us, length us, event | category | flops | bytes accessed | tf_op | source)
XLA Modules:
  0.0 58.3 jit_solution(9182041824025488885)
XLA Ops:
  0.0 0.0 copy-start.2
  0.0 0.0 copy-start
  0.0 0.0 copy-start.1
  0.0 2.4 %pack.1 = bf16[32,152,128]{2,1,0:T(8,128)(2,1)S(1)} custom-call(bf16[8,512,128]{2,1,0:T(8,128)(2,1)} %cube_ref.1, s32[8,32]{1,0:T(8,128)} %bitcast.5), custom_call_target="tpu_custom_call" | custom-call | tf_op jit(solution)/shard_map/pack/pallas_call | solution.py:211
  2.4 38.5 %all_to_all.5 = bf16[32,152,128]{2,1,0:T(8,128)(2,1)S(1)} all-to-all(bf16[32,152,128]{2,1,0:T(8,128)(2,1)S(1)} %pack.1), channel_id=1, replica_groups=mesh['ty'=4,'tx'=8] {'ty','tx'}, dimensions={0} | all-to-all | bytes 2490368 | tf_op jit(solution)/shard_map/all_to_all | solution.py:436
  41.0 0.1 cut_near.1
  41.0 0.4 collective-permute-start.1
  41.4 0.1 cut_far.1
  41.5 1.9 %collective-permute-start = (bf16[32,11,8,128]{3,2,1,0:T(8,128)(2,1)S(1)}, bf16[32,11,8,128]{3,2,1,0:T(8,128)(2,1)S(1)}, u32[]{:S(2)}, u32[]{:S(2)}) collective-permute-start(bf16[32,11,8,128]{3,2,1,0:T(8,128)(2,1)S(1)} %cut_far.1), channel_id=1, source_target_pairs={{1,2},{3,4},{5,6},{2,1},{4,3},{6,5},{9,10},{11,12},{13,14},{10,9},... | collective-permute-start | bytes 2162696 | tf_op jit(solution)/shard_map/ppermute | solution.py:442
  43.4 0.0 copy-done.2
  43.4 3.2 %tables.1 = (bf16[384,128]{1,0:T(8,128)(2,1)S(1)}, bf16[7,384,128]{2,1,0:T(8,128)(2,1)S(1)}, bf16[256,304]{1,0:T(8,128)(2,1)S(1)}, bf16[256,352]{1,0:T(8,128)(2,...) custom-call(s32[2,4]{1,0:T(2,128)S(1)} %copy-done.2), custom_call_target="tpu_custom_call" | custom-call | flops 10000000 | bytes 4000000 | tf_op jit(solution)/shard_map/tables/pallas_call | solution.py:127
  46.6 0.0 collective-permute-done.1.near_ref
  46.6 0.0 copy-done
  46.6 0.0 copy-done.1
  46.7 4.0 %begin.1 = (f32[3,8,2,128,256]{4,3,2,1,0:T(8,128)S(1)}, f32[4,8,256]{2,1,0:T(8,128)S(1)}) custom-call(s32[4]{0:T(128)S(1)} %copy-done.1, s32[2,4]{1,0:T(2,128)S(1)} %copy-done.2, s32[8,32]{1,0:T(8,128)S(1)} %bitcast.6, s32[8,32]{1,0:T(8,128)S(1)} %bitcast.7, bf16[32,19,8,128]{3,2,1,0:T(8,128)(2,1)S(1)} %bitcast.4, ...), custom_call_target="tpu_custom_call" | custom-call | flops 1000000000 | bytes 8000000 | tf_op jit(solution)/shard_map/begin/pallas_call | solution.py:324
  50.6 3.4 %collective-permute-done.far_ref = bf16[32,11,8,128]{3,2,1,0:T(8,128)(2,1)S(1)} collective-permute-done((bf16[32,11,8,128]{3,2,1,0:T(8,128)(2,1)S(1)}, bf16[32,11,8,128]{3,2,1,0:T(8,128)(2,1)S(1)}, u32[]{:S(2)}, u32[]{:S(2)}) %collective-permute-start) | collective-permute-done | bytes 720928 | tf_op jit(solution)/shard_map/ppermute | solution.py:442
  54.1 4.3 %finish.1 = bf16[4,128,16,256]{3,2,1,0:T(8,128)(2,1)} custom-call(s32[4]{0:T(128)S(1)} %copy-done.1, bf16[32,11,8,128]{3,2,1,0:T(8,128)(2,1)S(1)} %collective-permute-done.far_ref, f32[3,8,2,128,256]{4,3,2,1,0:T(8,128)S(1)} %get-tuple-element.21.sum_ref, f32[4,8,256]{2,1,0:T(8,128)S(1)} %get-tuple-element.22.scale_ref, ...), custom_call_target="tpu_custom_call" | custom-call | tf_op jit(solution)/shard_map/finish/pallas_call | solution.py:413
Async XLA Ops:
  0.0 43.4 %copy-start.2 = (s32[2,4]{1,0:T(2,128)S(1)}, s32[2,4]{1,0:T(2,128)}, u32[]{:S(2)}) copy-start(s32[2,4]{1,0:T(2,128)} %taps_ref.3) | copy-start | bytes 100
  0.0 46.6 %copy-start = (s32[32,8]{0,1:T(8,128)S(1)}, s32[32,8]{0,1:T(8,128)}, u32[]{:S(2)}) copy-start(s32[32,8]{0,1:T(8,128)} %param.5) | copy-start | bytes 3076
  0.0 46.6 %copy-start.1 = (s32[4]{0:T(128)S(1)}, s32[4]{0:T(128)}, u32[]{:S(2)}) copy-start(s32[4]{0:T(128)} %sigma_ref.3) | copy-start | bytes 52
  41.0 5.6 %collective-permute-start.1 = (bf16[32,11,8,128]{3,2,1,0:T(8,128)(2,1)S(1)}, bf16[32,11,8,128]{3,2,1,0:T(8,128)(2,1)S(1)}, u32[]{:S(2)}, u32[]{:S(2)}) collective-permute-start(bf16[32,11,8,128]{3,2,1,0:T(8,128)(2,1)S(1)} %cut_near.1), channel_id=1, source_target_pairs={{0,1},{2,3},{4,5},{6,7},{1,0},{3,2},{5,4},{7,6},{8,9},{10,11},{12,... | collective-permute-start | bytes 2162696 | tf_op jit(solution)/shard_map/ppermute | solution.py:443
  41.5 12.6 %collective-permute-start = (bf16[32,11,8,128]{3,2,1,0:T(8,128)(2,1)S(1)}, bf16[32,11,8,128]{3,2,1,0:T(8,128)(2,1)S(1)}, u32[]{:S(2)}, u32[]{:S(2)}) collective-permute-start(bf16[32,11,8,128]{3,2,1,0:T(8,128)(2,1)S(1)} %cut_far.1), channel_id=1, source_target_pairs={{1,2},{3,4},{5,6},{2,1},{4,3},{6,5},{9,10},{11,12},{13,14},{10,9},... | collective-permute-start | bytes 2162696 | tf_op jit(solution)/shard_map/ppermute | solution.py:442

commit v6 on v5

--- a/solution.py
+++ b/solution.py
@@ -17,13 +17,14 @@
 PT = 16
 HALO = 9
 SMAX = 3
+REACH = [3 * (i + 1) for i in range(SMAX)]
 LANES = 128
 TURN = LANES + 8
 PACK = 7
-HALO_GROUPS = (0, 10, 18)
-GROUPS = TILE_X + 3
+HALO_GROUPS = (1, 10, 17)
+GROUPS = TILE_X + 4
 SIDE = 11
-SPAN = 4
+FAR = HALO - 1
 WIDE = 256
 BF16 = jnp.bfloat16
 F32 = jnp.float32
@@ -32,16 +33,11 @@
 
 
 def column_group(x):
-    return x + 1 if x < HALO else x + 2
-
-
-def left_column(i):
-    x, base = TILE_X - HALO + i, GROUPS - SIDE
+    return x if x == 0 else x + 1 if x < HALO else x + 2 if x < TILE_X - 1 else x + 3
+
+
+def column(x, base=0):
     return column_group(x) - base, HALO_GROUPS[x // PACK] - base, x % PACK
-
-
-def right_column(i):
-    return column_group(i), HALO_GROUPS[i // PACK], i % PACK
 
 
 def odd_tile():
@@ -87,7 +83,7 @@
 
 
 def tables_kernel(channels, taps_ref, main_ref, halo_ref, *rest):
-    x_refs, far_refs, box_ref = rest[:SMAX], rest[SMAX : 2 * SMAX], rest[2 * SMAX]
+    near_refs, here_refs, far_refs, box_ref = rest[:SMAX], rest[SMAX : 2 * SMAX], rest[2 * SMAX : 3 * SMAX], rest[3 * SMAX]
     odd = odd_tile()
     taps = tap_table()
     for index in range(SMAX):
@@ -101,12 +97,11 @@
         for member in range(PACK):
             halo_ref[member, rows, :] = jnp.where(slot == member, halo, F32(0.0)).astype(BF16)
         reach = 3 * sigma
-        for ref, shift in ((x_refs[index], choose(odd, -reach, 0)), (far_refs[index], choose(odd, TILE_X, -reach))):
+        shifts = (-reach, choose(odd, -reach, -1), choose(odd, HALO, -reach))
+        for ref, shift in zip((near_refs[index], here_refs[index], far_refs[index]), shifts):
             row, col = iota(ref.shape, 0), iota(ref.shape, 1)
-            first = 0 if ref.shape[0] == PT * TILE_X else odd * HALF
-            out_x = first + row // (PT * HALF) * HALF + row % HALF
-            weight = taps_at(col // PT - out_x + shift, taps[index], sigma)
-            ref[...] = jnp.where(row % (PT * HALF) // HALF == col % PT, weight, F32(0.0)).astype(BF16)
+            weight = taps_at(col // PT - row % HALF + shift, taps[index], sigma)
+            ref[...] = jnp.where(row // HALF == col % PT, weight, F32(0.0)).astype(BF16)
     for scale in range(NSC):
         width, dilation = taps_ref[0, scale], taps_ref[1, scale]
         shape = box_ref.shape[1:]
@@ -120,8 +115,8 @@
 
 def tables(spectral_taps, channels):
     shapes = [(SMAX * TILE_Y, LANES), (PACK, SMAX * TILE_Y, LANES)]
-    shapes += [(PT * TILE_X, (TILE_X + 3 * (i + 1)) * PT) for i in range(SMAX)]
-    shapes += [(PT * (HALF if 3 * (i + 1) <= HALF else TILE_X), 3 * (i + 1) * PT) for i in range(SMAX)]
+    for counts in ([HALF + 2 * r for r in REACH], [HALO + r for r in REACH], [r - 1 for r in REACH]):
+        shapes += [(PT * HALF, count * PT) for count in counts]
     wide = min(channels, WIDE)
     shapes += [(NSC, wide + 2 * margin(channels), wide)]
     return pl.pallas_call(
@@ -164,21 +159,36 @@
             for r in range(n_rows):
                 turned_ref[span, r, c * TURN : c * TURN + LANES, :] = turned[:, r * TILE_Y : (r + 1) * TILE_Y]
 
+    def place(span, t, columns, group, slot, halos):
+        ends = [jnp.zeros((ch, LANES), F32)]
+        around = ends + columns + ends
+        lane = iota((ch, LANES), 1)
+        for r in range(n_rows):
+            out_ref[r * n_cols + span * tiles + t, group * ch : (group + 1) * ch, :] = columns[r].astype(BF16)
+            edge = pltpu.roll(jnp.where(lane < LANES // 2, around[r + 2], around[r]), slot + HALO, 1)
+            halos[r] = jnp.where((lane >= slot) & (lane < slot + 2 * HALO), edge, halos[r])
+
+    def beyond(span, t, r):
+        x = t * TILE_X + TILE_X if t % 2 else t * TILE_X - 1
+        if 0 <= x < LANES:
+            return turned_ref[span, r, pl.ds(x, ch, stride=TURN), :]
+        if spans == 1:
+            return jnp.zeros((ch, LANES), F32)
+        there = span + 1 if x > 0 else span - 1
+        inside = jnp.where((there >= 0) & (there < spans), F32(1.0), F32(0.0))
+        there = jnp.minimum(jnp.maximum(there, 0), spans - 1)
+        return turned_ref[there, r, pl.ds(x % LANES, ch, stride=TURN), :] * inside
+
     def send(span, firsts):
-        lane = iota((ch, LANES), 1)
         for t in range(tiles):
             for index, halo_group in enumerate(HALO_GROUPS):
                 halos = [firsts[index]] * n_rows
                 for x in range(index * PACK, min((index + 1) * PACK, TILE_X)):
                     slot, group = x % PACK * 2 * HALO, column_group(x)
                     columns = [turned_ref[span, r, pl.ds(t * TILE_X + x, ch, stride=TURN), :] for r in range(n_rows)]
-                    ends = [jnp.zeros((ch, LANES), F32)]
-                    around = ends + columns + ends
-                    for r in range(n_rows):
-                        dest = r * n_cols + span * tiles + t
-                        out_ref[dest, group * ch : (group + 1) * ch, :] = columns[r].astype(BF16)
-                        edge = pltpu.roll(jnp.where(lane < LANES // 2, around[r + 2], around[r]), slot + HALO, 1)
-                        halos[r] = jnp.where((lane >= slot) & (lane < slot + 2 * HALO), edge, halos[r])
+                    place(span, t, columns, group, slot, halos)
+                if index == len(HALO_GROUPS) - 1:
+                    place(span, t, [beyond(span, t, r) for r in range(n_rows)], GROUPS - 1, 2 * 2 * HALO, halos)
                 for r in range(n_rows):
                     dest = r * n_cols + span * tiles + t
                     out_ref[dest, halo_group * ch : (halo_group + 1) * ch, :] = halos[r].astype(BF16)
@@ -227,15 +237,15 @@
 
 def cut_kernel(far, own_ref, out_ref):
     odd = odd_tile()
-    first = (odd if far else 1 - odd) * (GROUPS - SIDE)
-    out_ref[...] = own_ref[:, pl.ds(first, SIDE)]
+    first = choose(odd, GROUPS - 1 - SIDE, 1) if far else choose(odd, 0, GROUPS - 1 - SIDE)
+    out_ref[...] = own_ref[:, pl.ds(first, out_ref.shape[1])]
 
 
 def cut(own, far):
     senders, _, ch, lanes = own.shape
     return pl.pallas_call(
         functools.partial(cut_kernel, far),
-        out_shape=jax.ShapeDtypeStruct((senders, SIDE, ch, lanes), BF16),
+        out_shape=jax.ShapeDtypeStruct((senders, SIDE - 1 if far else SIDE, ch, lanes), BF16),
         in_specs=[pl.BlockSpec(memory_space=pltpu.VMEM)],
         out_specs=pl.BlockSpec(memory_space=pltpu.VMEM),
         compiler_params=pltpu.CompilerParams(vmem_limit_bytes=6 * 2**20 if senders <= 32 else 24 * 2**20),
@@ -281,151 +291,152 @@
         yield scale, seen / (noise * (knorm / jnp.sqrt(width)) * width)
 
 
+def box_half(half, sigma_ref, scale_ref, box_ref, smooth_ref, stage_ref, out_ref, sems):
+    channels = smooth_ref.shape[-1]
+    wide, edge = min(channels, WIDE), margin(channels)
+    copies = []
+    for scale in range(NSC):
+        for group in range(0, TILE_Y // PT, 2):
+            for at in range(0, channels, wide):
+                lanes, first = slice(at, at + wide), at - edge
+                low, high = max(first, 0), min(at + wide + edge, channels)
+                field = smooth_ref[sigma_ref[scale] - 1, group : group + 2, :, low:high].reshape(2 * PT * HALF, high - low)
+                boxed = jnp.dot(field, box_ref[scale, low - first : high - first], preferred_element_type=F32)
+                boxed = boxed.reshape(2, PT * HALF, wide)
+                for row in range(2):
+                    scaled = (boxed[row] * scale_ref[scale, group + row : group + row + 1, lanes]).astype(BF16)
+                    rows = slice((group + row) * PT, (group + row + 1) * PT)
+                    stage_ref[scale, rows, :, lanes] = scaled.reshape(PT, HALF, wide)
+        there = out_ref.at[scale, :, pl.ds(pl.multiple_of(half * HALF, HALF), HALF)]
+        copies.append(pltpu.make_async_copy(stage_ref.at[scale], there, sems.at[scale]))
+        copies[-1].start()
+    return copies
+
+
 def begin_kernel(sigma_ref, taps_ref, cover_ref, footprint_ref, own_ref, near_ref, main_ref, halo_ref, *rest):
-    x_refs, sum_ref, scale_ref, rows_ref = rest[:SMAX], *rest[SMAX : SMAX + 3]
+    near_refs, here_refs, box_ref = rest[:SMAX], rest[SMAX : 2 * SMAX], rest[2 * SMAX]
+    out_ref, sum_ref, scale_ref, rows_ref, smooth_ref, stage_ref, sems = rest[2 * SMAX + 1 :]
     senders, _, ch, _ = own_ref.shape
     part = min(senders, WIDE // ch)
+    groups = range(TILE_Y // PT)
     odd = odd_tile()
+
+    def lanes_of(index):
+        return pl.ds(pl.multiple_of(index * part * ch, part * ch), part * ch)
 
     def one(index, carry):
         first = index * part
-        passed = functools.partial(y_pass, main_ref=main_ref, halo_ref=halo_ref, rows_ref=rows_ref)
-        for i in range(HALO):
-            where = [choose(odd, a, b) for a, b in zip(left_column(i), right_column(i))]
-            passed(near_ref, first, part, *where, x=choose(odd, i, TILE_X + i))
-        for x in range(TILE_X):
-            passed(own_ref, first, part, *right_column(x), x=choose(odd, HALO + x, x))
-        lanes = pl.ds(pl.multiple_of(first * ch, part * ch), part * ch)
+        lanes = lanes_of(index)
         for scale, value in scale_rows(sigma_ref, taps_ref, cover_ref, footprint_ref, own_ref, first, part):
             scale_ref[scale, :, lanes] = value
-        for group in range(TILE_Y // PT):
-            for kind in range(SMAX):
-                reach = 3 * (kind + 1)
-                start = choose(odd, HALO - reach, 0)
-                field = x_pass(rows_ref, kind, group, start, TILE_X + reach, x_refs[kind])
-                sum_ref[kind, group, :, :, lanes] = field.reshape(2, PT * HALF, part * ch)
+        passed = functools.partial(y_pass, main_ref=main_ref, halo_ref=halo_ref, rows_ref=rows_ref)
+        base = GROUPS - 1 - SIDE
+        for i in range(HALO):
+            where = [choose(odd, a, b) for a, b in zip(column(TILE_X - HALO + i, base), column(i))]
+            passed(near_ref, first, part, *where, x=choose(odd, i, TILE_X + 1 + i))
+        for x in range(TILE_X):
+            passed(own_ref, first, part, *column(x), x=choose(odd, HALO + x, 1 + x))
+        passed(own_ref, first, part, GROUPS - 1, HALO_GROUPS[-1], 2, x=choose(odd, HALO + TILE_X, 0))
+        for group in groups:
+            for kind, reach in enumerate(REACH):
+                field = x_pass(rows_ref, kind, group, HALO - reach, HALF + 2 * reach, near_refs[kind])
+                smooth_ref[kind, group, :, lanes] = field.astype(BF16)
+        return carry
+
+    def two(index, carry):
+        lanes = lanes_of(index)
+        for group in groups:
+            for kind, reach in enumerate(REACH):
+                start = choose(odd, HALO + HALF - reach, 0)
+                sum_ref[kind, group, :, lanes] = x_pass(rows_ref, kind, group, start, HALO + reach, here_refs[kind])
         return carry
 
     if senders == part:
         one(0, 0)
     else:
-        lax.fori_loop(0, senders // part, one, 0)
-
-
-def begin(kernel_sigmas, spectral_taps, footprint, own, near, main, halo, weights):
+        lax.fori_loop(0, senders // part, lambda index, carry: two(index, one(index, carry)), 0)
+    copies = box_half(1 - odd, sigma_ref, scale_ref, box_ref, smooth_ref, stage_ref, out_ref, sems)
+    if senders == part:
+        two(0, 0)
+    for copy in copies:
+        copy.wait()
+
+
+def begin(kernel_sigmas, spectral_taps, footprint, own, near, main, halo, weights, box):
     senders, _, ch, _ = own.shape
     channels = senders * ch
     wide = min(channels, WIDE)
-    rows = (SMAX, TILE_Y // PT, TILE_X + HALO, PT, wide)
-    sums = (SMAX, TILE_Y // PT, 2, PT * HALF, channels)
+    rows = (SMAX, TILE_Y // PT, TILE_X + HALO + 1, PT, wide)
+    sums = (SMAX, TILE_Y // PT, PT * HALF, channels)
+    stage = (NSC, TILE_Y, HALF, channels)
     smem = pl.BlockSpec(memory_space=pltpu.SMEM)
     vmem = pl.BlockSpec(memory_space=pltpu.VMEM)
-    limit = 2 * int(np.prod(rows)) + 6 * 2**20 if channels <= WIDE else 62 * 2**20
+    limit = 2 * int(np.prod(rows) + np.prod(sums) + np.prod(stage)) + 6 * 2**20 if channels <= WIDE else 62 * 2**20
     return pl.pallas_call(
         begin_kernel,
-        out_shape=[jax.ShapeDtypeStruct(sums, F32), jax.ShapeDtypeStruct((NSC, TILE_Y // PT, channels), F32)],
-        in_specs=[smem] * 3 + [vmem] * (5 + len(weights)),
-        out_specs=[vmem] * 2,
-        scratch_shapes=[pltpu.VMEM(rows, BF16)],
+        out_shape=[
+            jax.ShapeDtypeStruct((NSC, TILE_Y, TILE_X, channels), BF16),
+            jax.ShapeDtypeStruct(sums, F32),
+            jax.ShapeDtypeStruct((NSC, TILE_Y // PT, channels), F32),
+        ],
+        in_specs=[smem] * 3 + [vmem] * (6 + len(weights)),
+        out_specs=[pl.BlockSpec(memory_space=pltpu.MemorySpace.HBM)] + [vmem] * 2,
+        scratch_shapes=[
+            pltpu.VMEM(rows, BF16),
+            pltpu.VMEM(sums, BF16),
+            pltpu.VMEM(stage, BF16),
+            pltpu.SemaphoreType.DMA((NSC,)),
+        ],
         compiler_params=pltpu.CompilerParams(vmem_limit_bytes=limit),
         cost_estimate=pl.CostEstimate(flops=10**9, bytes_accessed=8 * 10**6, transcendentals=0),
         name="begin",
-    )(kernel_sigmas, spectral_taps, footprint.T, footprint.T, own, near, main, halo, *weights)
-
-
-def finish_kernel(sigma_ref, far_ref, sum_ref, scale_ref, main_ref, halo_ref, *rest):
-    far_refs, box_ref, out_ref, rows_ref, stage_ref, sems = rest[:SMAX], *rest[SMAX : SMAX + 5]
-    smooth_refs = rest[SMAX + 5 :]
+    )(kernel_sigmas, spectral_taps, footprint.T, footprint.T, own, near, main, halo, *weights, box)
+
+
+def finish_kernel(sigma_ref, _, far_ref, sum_ref, scale_ref, main_ref, halo_ref, *rest):
+    far_refs, box_ref, out_ref, rows_ref, smooth_ref, stage_ref, sems = rest[:SMAX], *rest[SMAX:]
     senders, _, ch, _ = far_ref.shape
-    channels = senders * ch
     part = min(senders, WIDE // ch)
     odd = odd_tile()
-    slots, _, tall = stage_ref.shape[:3]
-    span, phases = tall // PT, TILE_Y // tall
-    wide, edge = min(channels, WIDE), margin(channels)
-
-    def out_copy(phase, slot, scale):
-        there = out_ref.at[scale, pl.ds(phase * tall, tall)]
-        return pltpu.make_async_copy(stage_ref.at[slot, scale], there, sems.at[slot, scale])
-
-    def far_y(first):
-        for i in range(HALO):
-            where = [choose(odd, a, b) for a, b in zip(right_column(i), left_column(i))]
+    for first in range(0, senders, part):
+        lanes = slice(first * ch, (first + part) * ch)
+        for i in range(FAR):
+            pair = zip(column(1 + i, 1), column(TILE_X - HALO + i, GROUPS - 1 - SIDE))
+            where = [choose(odd, a, b) for a, b in pair]
             y_pass(far_ref, first, part, *where, main_ref, halo_ref, rows_ref, i)
-
-    def far_x(first, phase):
-        lanes = slice(first * ch, (first + part) * ch)
-        for kind in range(SMAX):
-            reach = 3 * (kind + 1)
-            for row in range(span):
-                group = phase * span + row
-                added = x_pass(rows_ref, kind, group, choose(odd, 0, HALO - reach), reach, far_refs[kind])
-                added = added.reshape(-1, PT * HALF, part * ch)
-                if added.shape[0] == 2:
-                    smooth_refs[phase][kind, row, :, :, lanes] = (sum_ref[kind, group, :, :, lanes] + added).astype(BF16)
-                else:
-                    smooth_refs[phase][kind, row, odd, :, lanes] = (sum_ref[kind, group, odd, :, lanes] + added[0]).astype(BF16)
-                    smooth_refs[phase][kind, row, 1 - odd, :, lanes] = sum_ref[kind, group, 1 - odd, :, lanes].astype(BF16)
-
-    def box_pass(phase, slot):
-        for scale in range(NSC):
-            if phase >= slots:
-                out_copy(phase - slots, slot, scale).wait()
-            for row in range(span):
-                group = phase * span + row
-                for at in range(0, channels, wide):
-                    lanes, first = slice(at, at + wide), at - edge
-                    low, high = max(first, 0), min(at + wide + edge, channels)
-                    field = smooth_refs[phase][sigma_ref[scale] - 1, row, :, :, low:high]
-                    field = field.reshape(PT * TILE_X, high - low)
-                    boxed = jnp.dot(field, box_ref[scale, low - first : high - first], preferred_element_type=F32)
-                    scaled = (boxed * scale_ref[scale, group : group + 1, lanes]).astype(BF16)
-                    scaled = scaled.reshape(2, PT, HALF, wide)
-                    for half in range(2):
-                        stage_ref[slot, scale, row * PT : (row + 1) * PT, half * HALF : (half + 1) * HALF, lanes] = scaled[half]
-            out_copy(phase, slot, scale).start()
-
-    whole = senders == part
-    for first in range(0, senders, part):
-        far_y(first)
-        if not whole:
-            for phase in range(phases):
-                far_x(first, phase)
-    for phase in range(phases):
-        if whole:
-            far_x(0, phase)
-        box_pass(phase, phase % slots)
-    for phase in range(phases - slots, phases):
-        for scale in range(NSC):
-            out_copy(phase, phase % slots, scale).wait()
-
-
-def finish(kernel_sigmas, far, sums, scales, main, halo, weights, box):
+        for group in range(TILE_Y // PT):
+            for kind, reach in enumerate(REACH):
+                added = x_pass(rows_ref, kind, group, choose(odd, 0, HALO - reach), reach - 1, far_refs[kind])
+                smooth_ref[kind, group, :, lanes] = (sum_ref[kind, group, :, lanes] + added).astype(BF16)
+    for copy in box_half(odd, sigma_ref, scale_ref, box_ref, smooth_ref, stage_ref, out_ref, sems):
+        copy.wait()
+
+
+def finish(kernel_sigmas, out, far, sums, scales, main, halo, weights, box):
     senders, _, ch, _ = far.shape
     channels = senders * ch
-    wide = min(channels, WIDE)
-    span = SPAN if channels <= WIDE else 1
-    phases = TILE_Y // PT // span
-    slots = min(2, phases)
-    rows = (SMAX, TILE_Y // PT, HALO, PT, wide)
-    need = 2 * int(np.prod(rows)) + 2 * channels * (slots * span * NSC + SMAX * TILE_Y // PT) * PT * TILE_X
+    rows = (SMAX, TILE_Y // PT, FAR, PT, min(channels, WIDE))
+    stage = (NSC, TILE_Y, HALF, channels)
     vmem = pl.BlockSpec(memory_space=pltpu.VMEM)
+    hbm = pl.BlockSpec(memory_space=pltpu.MemorySpace.HBM)
+    need = 2 * int(np.prod(rows) + np.prod(sums.shape) + np.prod(stage))
     return pl.pallas_call(
         finish_kernel,
-        out_shape=jax.ShapeDtypeStruct((NSC, TILE_Y, TILE_X, channels), BF16),
-        in_specs=[pl.BlockSpec(memory_space=pltpu.SMEM)] + [vmem] * (6 + len(weights)),
-        out_specs=pl.BlockSpec(memory_space=pltpu.MemorySpace.HBM),
+        out_shape=jax.ShapeDtypeStruct(out.shape, BF16),
+        in_specs=[pl.BlockSpec(memory_space=pltpu.SMEM), hbm] + [vmem] * (6 + len(weights)),
+        out_specs=hbm,
+        input_output_aliases={1: 0},
         scratch_shapes=[
             pltpu.VMEM(rows, BF16),
-            pltpu.VMEM((slots, NSC, span * PT, TILE_X, channels), BF16),
-            pltpu.SemaphoreType.DMA((slots, NSC)),
-        ]
-        + [pltpu.VMEM((SMAX, span, 2, PT * HALF, channels), BF16)] * phases,
+            pltpu.VMEM(sums.shape, BF16),
+            pltpu.VMEM(stage, BF16),
+            pltpu.SemaphoreType.DMA((NSC,)),
+        ],
         compiler_params=pltpu.CompilerParams(
             vmem_limit_bytes=need + 6 * 2**20 if channels <= WIDE else 62 * 2**20
         ),
         name="finish",
-    )(kernel_sigmas, far, sums, scales, main, halo, *weights, box)
+    )(kernel_sigmas, out, far, sums, scales, main, halo, *weights, box)
 
 
 def local(channel_cube, footprint, kernel_sigmas, spectral_taps):
@@ -442,8 +453,10 @@
     far = lax.ppermute(far, "tx", both(far_pairs))
     near = lax.ppermute(near, "tx", both(near_pairs))
     main, halo, *weights, box = tables(spectral_taps, channels)
-    sums, scales = begin(kernel_sigmas, spectral_taps, footprint, own, near, main, halo, weights[:SMAX])
-    return finish(kernel_sigmas, far, sums, scales, main, halo, weights[SMAX:], box)
+    out, sums, scales = begin(
+        kernel_sigmas, spectral_taps, footprint, own, near, main, halo, weights[: 2 * SMAX], box
+    )
+    return finish(kernel_sigmas, out, far, sums, scales, main, halo, weights[2 * SMAX :], box)
 
 
 def solution(mesh):

time: 58.5 us -> 58.2 us (level)
  blocking collectives: 38.5 us -> 39.9 us
  waiting for transfers between devices: 3.44 us -> 2.09 us
    ppermute x1, waiting for transfers between devices: 3.44 us -> 2.09 us  [local(): far = lax.ppermute(far, 'tx', both(far_pairs))]
    all_to_all x1, blocking collectives: 38.5 us -> 39.9 us  [local(): lax.all_to_all(packed, ('ty', 'tx'), split_axis=0, concat_axis=0, tiled=T...]
  transfers between devices with their start and end apart: 2 -> 2, of which waited for: 1 -> 1; matrix products, arithmetic and copies ran while one was open for 0% -> 0% of each run, Pallas kernels for 12% -> 14%
where the time goes in v6:
time: 58.2 us; the launch traced here: 58 us
  blocking collectives  39.9 us (69%)
  Pallas kernels  13.6 us (23%)
  starting transfers between devices  2.37 us (4%)
  waiting for transfers between devices  2.09 us (4%)
    all_to_all x1, blocking collectives, local(): lax.all_to_all(packed, ('ty', 'tx'), split_axis=0, concat_axis=0, tiled=T...  39.9 us
    pallas_call x1, Pallas kernels, begin(): pl.pallas_call(begin_kernel, out_shape=[jax.ShapeDtypeStruct((NSC, TILE_Y...  4.99 us
    pallas_call x1, Pallas kernels, finish(): pl.pallas_call(finish_kernel, out_shape=jax.ShapeDtypeStruct(out.shape, B...  3.28 us
    pallas_call x1, Pallas kernels, tables(): pl.pallas_call(functools.partial(tables_kernel, channels), out_shape=[jax...  2.84 us
    pallas_call x1, Pallas kernels, pack(): pl.pallas_call(pack_kernel, out_shape=jax.ShapeDtypeStruct((n_rows * n_co...  2.37 us
    ppermute x1, waiting for transfers between devices, local(): far = lax.ppermute(far, 'tx', both(far_pairs))  2.09 us
    ppermute x1, starting transfers between devices, local(): far = lax.ppermute(far, 'tx', both(far_pairs))  1.92 us
  transfers between devices with their start and end apart: 2, of which 1 were waited for; matrix products, arithmetic and copies ran while one was open for 0% of the time, Pallas kernels for 14%

profile of v6, /device:TPU:1, one launch (start us, length us, event | category | flops | bytes accessed | tf_op | source)
XLA Modules:
  0.0 58.0 jit_solution(15434994266583718972)
XLA Ops:
  0.0 2.4 %pack.1 = bf16[32,160,128]{2,1,0:T(8,128)(2,1)S(1)} custom-call(bf16[8,512,128]{2,1,0:T(8,128)(2,1)} %cube_ref.1, s32[8,32]{1,0:T(8,128)} %bitcast.5), custom_call_target="tpu_custom_call" | custom-call | tf_op jit(solution)/shard_map/pack/pallas_call | solution.py:221
  2.4 0.0 copy-start.2
  2.4 0.0 copy-start
  2.4 0.0 copy-start.1
  2.4 39.9 %all_to_all.5 = bf16[32,160,128]{2,1,0:T(8,128)(2,1)S(1)} all-to-all(bf16[32,160,128]{2,1,0:T(8,128)(2,1)S(1)} %pack.1), channel_id=1, replica_groups=mesh['ty'=4,'tx'=8] {'ty','tx'}, dimensions={0} | all-to-all | bytes 2621440 | tf_op jit(solution)/shard_map/all_to_all | solution.py:447
  42.3 0.1 cut_near.1
  42.3 0.4 collective-permute-start
  42.8 1.9 %collective-permute-start.1 = (bf16[32,10,8,128]{3,2,1,0:T(8,128)(2,1)S(1)}, bf16[32,10,8,128]{3,2,1,0:T(8,128)(2,1)S(1)}, u32[]{:S(2)}, u32[]{:S(2)}) collective-permute-start(bf16[32,10,8,128]{3,2,1,0:T(8,128)(2,1)S(1)} %cut_far.1), channel_id=1, source_target_pairs={{1,2},{3,4},{5,6},{2,1},{4,3},{6,5},{9,10},{11,12},{13,14},{10,9},... | collective-permute-start | bytes 1966088 | tf_op jit(solution)/shard_map/ppermute | solution.py:453
  44.8 0.0 copy-done.2
  44.8 2.8 %tables.1 = (bf16[384,128]{1,0:T(8,128)(2,1)S(1)}, bf16[7,384,128]{2,1,0:T(8,128)(2,1)S(1)}, bf16[128,224]{1,0:T(8,128)(2,1)S(1)}, bf16[128,320]{1,0:T(8,128)(2,...) custom-call(s32[2,4]{1,0:T(2,128)S(1)} %copy-done.2), custom_call_target="tpu_custom_call" | custom-call | flops 10000000 | bytes 4000000 | tf_op jit(solution)/shard_map/tables/pallas_call | solution.py:122
  47.6 0.0 collective-permute-done.near_ref
  47.6 0.0 copy-done
  47.6 0.0 copy-done.1
  47.6 5.0 %begin.1 = (bf16[4,128,16,256]{3,2,1,0:T(8,128)(2,1)}, f32[3,8,128,256]{3,2,1,0:T(8,128)S(1)}, f32[4,8,256]{2,1,0:T(8,128)S(1)}) custom-call(s32[4]{0:T(128)S(1)} %copy-done.1, s32[2,4]{1,0:T(2,128)S(1)} %copy-done.2, s32[8,32]{1,0:T(8,128)S(1)} %bitcast.6, s32[8,32]{1,0:T(8,128)S(1)} %bitcast.7, bf16[32,20,8,128]{3,2,1,0:T(8,128)(2,1)S(1)} %bitcast.4, ...), custom_call_target="tpu_custom_call" | custom-call | flops 1000000000 | bytes 8000000 | tf_op jit(solution)/shard_map/begin/pallas_call | solution.py:375
  52.6 2.1 %collective-permute-done.1.far_ref = bf16[32,10,8,128]{3,2,1,0:T(8,128)(2,1)S(1)} collective-permute-done((bf16[32,10,8,128]{3,2,1,0:T(8,128)(2,1)S(1)}, bf16[32,10,8,128]{3,2,1,0:T(8,128)(2,1)S(1)}, u32[]{:S(2)}, u32[]{:S(2)}) %collective-permute-start.1) | collective-permute-done | bytes 655392 | tf_op jit(solution)/shard_map/ppermute | solution.py:453
  54.7 3.3 %finish.1 = bf16[4,128,16,256]{3,2,1,0:T(8,128)(2,1)} custom-call(s32[4]{0:T(128)S(1)} %copy-done.1, bf16[4,128,16,256]{3,2,1,0:T(8,128)(2,1)} %get-tuple-element.29._, bf16[32,10,8,128]{3,2,1,0:T(8,128)(2,1)S(1)} %collective-permute-done.1.far_ref, f32[3,8,128,256]{3,2,1,0:T(8,128)S(1)} %get-tuple-element.30.sum_ref, ...), custom_call_target="tpu_custom_call", output_to_operand_aliasing={{}: (1, {})} | custom-call | tf_op jit(solution)/shard_map/finish/pallas_call | solution.py:423
  (1 shorter events, 0.0 us)
Async XLA Ops:
  2.4 42.4 %copy-start.2 = (s32[2,4]{1,0:T(2,128)S(1)}, s32[2,4]{1,0:T(2,128)}, u32[]{:S(2)}) copy-start(s32[2,4]{1,0:T(2,128)} %taps_ref.3) | copy-start | bytes 100
  2.4 45.2 %copy-start = (s32[32,8]{0,1:T(8,128)S(1)}, s32[32,8]{0,1:T(8,128)}, u32[]{:S(2)}) copy-start(s32[32,8]{0,1:T(8,128)} %param.5) | copy-start | bytes 3076
  2.4 45.2 %copy-start.1 = (s32[4]{0:T(128)S(1)}, s32[4]{0:T(128)}, u32[]{:S(2)}) copy-start(s32[4]{0:T(128)} %sigma_ref.3) | copy-start | bytes 52
  42.3 5.3 %collective-permute-start = (bf16[32,11,8,128]{3,2,1,0:T(8,128)(2,1)S(1)}, bf16[32,11,8,128]{3,2,1,0:T(8,128)(2,1)S(1)}, u32[]{:S(2)}, u32[]{:S(2)}) collective-permute-start(bf16[32,11,8,128]{3,2,1,0:T(8,128)(2,1)S(1)} %cut_near.1), channel_id=1, source_target_pairs={{0,1},{2,3},{4,5},{6,7},{1,0},{3,2},{5,4},{7,6},{8,9},{10,11},{12,... | collective-permute-start | bytes 2162696 | tf_op jit(solution)/shard_map/ppermute | solution.py:454
  42.8 11.9 %collective-permute-start.1 = (bf16[32,10,8,128]{3,2,1,0:T(8,128)(2,1)S(1)}, bf16[32,10,8,128]{3,2,1,0:T(8,128)(2,1)S(1)}, u32[]{:S(2)}, u32[]{:S(2)}) collective-permute-start(bf16[32,10,8,128]{3,2,1,0:T(8,128)(2,1)S(1)} %cut_far.1), channel_id=1, source_target_pairs={{1,2},{3,4},{5,6},{2,1},{4,3},{6,5},{9,10},{11,12},{13,14},{10,9},... | collective-permute-start | bytes 1966088 | tf_op jit(solution)/shard_map/ppermute | solution.py:453

commit v7 on v6

--- a/solution.py
+++ b/solution.py
@@ -24,6 +24,7 @@
 HALO_GROUPS = (1, 10, 17)
 GROUPS = TILE_X + 4
 SIDE = 11
+RUN = 4
 FAR = HALO - 1
 WIDE = 256
 BF16 = jnp.bfloat16
@@ -296,14 +297,14 @@
     wide, edge = min(channels, WIDE), margin(channels)
     copies = []
     for scale in range(NSC):
-        for group in range(0, TILE_Y // PT, 2):
+        for group in range(0, TILE_Y // PT, RUN):
             for at in range(0, channels, wide):
                 lanes, first = slice(at, at + wide), at - edge
                 low, high = max(first, 0), min(at + wide + edge, channels)
-                field = smooth_ref[sigma_ref[scale] - 1, group : group + 2, :, low:high].reshape(2 * PT * HALF, high - low)
+                field = smooth_ref[sigma_ref[scale] - 1, group : group + RUN, :, low:high].reshape(RUN * PT * HALF, high - low)
                 boxed = jnp.dot(field, box_ref[scale, low - first : high - first], preferred_element_type=F32)
-                boxed = boxed.reshape(2, PT * HALF, wide)
-                for row in range(2):
+                boxed = boxed.reshape(RUN, PT * HALF, wide)
+                for row in range(RUN):
                     scaled = (boxed[row] * scale_ref[scale, group + row : group + row + 1, lanes]).astype(BF16)
                     rows = slice((group + row) * PT, (group + row + 1) * PT)
                     stage_ref[scale, rows, :, lanes] = scaled.reshape(PT, HALF, wide)

time: 58.2 us -> 58.2 us (level)
  no operation moved by 1% of the time
where the time goes in v7:
time: 58.2 us; the launch traced here: 58 us
  blocking collectives  39.9 us (69%)
  Pallas kernels  13.6 us (23%)
  starting transfers between devices  2.37 us (4%)
  waiting for transfers between devices  2.1 us (4%)
    all_to_all x1, blocking collectives, local(): lax.all_to_all(packed, ('ty', 'tx'), split_axis=0, concat_axis=0, tiled=T...  39.9 us
    pallas_call x1, Pallas kernels, begin(): pl.pallas_call(begin_kernel, out_shape=[jax.ShapeDtypeStruct((NSC, TILE_Y...  4.99 us
    pallas_call x1, Pallas kernels, finish(): pl.pallas_call(finish_kernel, out_shape=jax.ShapeDtypeStruct(out.shape, B...  3.29 us
    pallas_call x1, Pallas kernels, tables(): pl.pallas_call(functools.partial(tables_kernel, channels), out_shape=[jax...  2.84 us
    pallas_call x1, Pallas kernels, pack(): pl.pallas_call(pack_kernel, out_shape=jax.ShapeDtypeStruct((n_rows * n_co...  2.37 us
    ppermute x1, waiting for transfers between devices, local(): far = lax.ppermute(far, 'tx', both(far_pairs))  2.1 us
    ppermute x1, starting transfers between devices, local(): far = lax.ppermute(far, 'tx', both(far_pairs))  1.92 us
  transfers between devices with their start and end apart: 2, of which 1 were waited for; matrix products, arithmetic and copies ran while one was open for 0% of the time, Pallas kernels for 14%

profile of v7, /device:TPU:1, one launch (start us, length us, event | category | flops | bytes accessed | tf_op | source)
XLA Modules:
  0.0 58.0 jit_solution(4253832528212725719)
XLA Ops:
  0.0 2.4 %pack.1 = bf16[32,160,128]{2,1,0:T(8,128)(2,1)S(1)} custom-call(bf16[8,512,128]{2,1,0:T(8,128)(2,1)} %cube_ref.1, s32[8,32]{1,0:T(8,128)} %bitcast.5), custom_call_target="tpu_custom_call" | custom-call | tf_op jit(solution)/shard_map/pack/pallas_call | solution.py:222
  2.4 0.0 copy-start.2
  2.4 0.0 copy-start
  2.4 0.0 copy-start.1
  2.4 39.9 %all_to_all.5 = bf16[32,160,128]{2,1,0:T(8,128)(2,1)S(1)} all-to-all(bf16[32,160,128]{2,1,0:T(8,128)(2,1)S(1)} %pack.1), channel_id=1, replica_groups=mesh['ty'=4,'tx'=8] {'ty','tx'}, dimensions={0} | all-to-all | bytes 2621440 | tf_op jit(solution)/shard_map/all_to_all | solution.py:448
  42.3 0.1 cut_near.1
  42.3 0.4 collective-permute-start
  42.8 1.9 %collective-permute-start.1 = (bf16[32,10,8,128]{3,2,1,0:T(8,128)(2,1)S(1)}, bf16[32,10,8,128]{3,2,1,0:T(8,128)(2,1)S(1)}, u32[]{:S(2)}, u32[]{:S(2)}) collective-permute-start(bf16[32,10,8,128]{3,2,1,0:T(8,128)(2,1)S(1)} %cut_far.1), channel_id=1, source_target_pairs={{1,2},{3,4},{5,6},{2,1},{4,3},{6,5},{9,10},{11,12},{13,14},{10,9},... | collective-permute-start | bytes 1966088 | tf_op jit(solution)/shard_map/ppermute | solution.py:454
  44.8 0.0 copy-done.2
  44.8 2.8 %tables.1 = (bf16[384,128]{1,0:T(8,128)(2,1)S(1)}, bf16[7,384,128]{2,1,0:T(8,128)(2,1)S(1)}, bf16[128,224]{1,0:T(8,128)(2,1)S(1)}, bf16[128,320]{1,0:T(8,128)(2,...) custom-call(s32[2,4]{1,0:T(2,128)S(1)} %copy-done.2), custom_call_target="tpu_custom_call" | custom-call | flops 10000000 | bytes 4000000 | tf_op jit(solution)/shard_map/tables/pallas_call | solution.py:123
  47.6 0.0 collective-permute-done.near_ref
  47.6 0.0 copy-done
  47.6 0.0 copy-done.1
  47.6 5.0 %begin.1 = (bf16[4,128,16,256]{3,2,1,0:T(8,128)(2,1)}, f32[3,8,128,256]{3,2,1,0:T(8,128)S(1)}, f32[4,8,256]{2,1,0:T(8,128)S(1)}) custom-call(s32[4]{0:T(128)S(1)} %copy-done.1, s32[2,4]{1,0:T(2,128)S(1)} %copy-done.2, s32[8,32]{1,0:T(8,128)S(1)} %bitcast.6, s32[8,32]{1,0:T(8,128)S(1)} %bitcast.7, bf16[32,20,8,128]{3,2,1,0:T(8,128)(2,1)S(1)} %bitcast.4, ...), custom_call_target="tpu_custom_call" | custom-call | flops 1000000000 | bytes 8000000 | tf_op jit(solution)/shard_map/begin/pallas_call | solution.py:376
  52.6 2.1 %collective-permute-done.1.far_ref = bf16[32,10,8,128]{3,2,1,0:T(8,128)(2,1)S(1)} collective-permute-done((bf16[32,10,8,128]{3,2,1,0:T(8,128)(2,1)S(1)}, bf16[32,10,8,128]{3,2,1,0:T(8,128)(2,1)S(1)}, u32[]{:S(2)}, u32[]{:S(2)}) %collective-permute-start.1) | collective-permute-done | bytes 655392 | tf_op jit(solution)/shard_map/ppermute | solution.py:454
  54.7 3.3 %finish.1 = bf16[4,128,16,256]{3,2,1,0:T(8,128)(2,1)} custom-call(s32[4]{0:T(128)S(1)} %copy-done.1, bf16[4,128,16,256]{3,2,1,0:T(8,128)(2,1)} %get-tuple-element.29._, bf16[32,10,8,128]{3,2,1,0:T(8,128)(2,1)S(1)} %collective-permute-done.1.far_ref, f32[3,8,128,256]{3,2,1,0:T(8,128)S(1)} %get-tuple-element.30.sum_ref, ...), custom_call_target="tpu_custom_call", output_to_operand_aliasing={{}: (1, {})} | custom-call | tf_op jit(solution)/shard_map/finish/pallas_call | solution.py:424
  (1 shorter events, 0.0 us)
Async XLA Ops:
  2.4 42.4 %copy-start.2 = (s32[2,4]{1,0:T(2,128)S(1)}, s32[2,4]{1,0:T(2,128)}, u32[]{:S(2)}) copy-start(s32[2,4]{1,0:T(2,128)} %taps_ref.3) | copy-start | bytes 100
  2.4 45.2 %copy-start = (s32[32,8]{0,1:T(8,128)S(1)}, s32[32,8]{0,1:T(8,128)}, u32[]{:S(2)}) copy-start(s32[32,8]{0,1:T(8,128)} %param.5) | copy-start | bytes 3076
  2.4 45.2 %copy-start.1 = (s32[4]{0:T(128)S(1)}, s32[4]{0:T(128)}, u32[]{:S(2)}) copy-start(s32[4]{0:T(128)} %sigma_ref.3) | copy-start | bytes 52
  42.3 5.3 %collective-permute-start = (bf16[32,11,8,128]{3,2,1,0:T(8,128)(2,1)S(1)}, bf16[32,11,8,128]{3,2,1,0:T(8,128)(2,1)S(1)}, u32[]{:S(2)}, u32[]{:S(2)}) collective-permute-start(bf16[32,11,8,128]{3,2,1,0:T(8,128)(2,1)S(1)} %cut_near.1), channel_id=1, source_target_pairs={{0,1},{2,3},{4,5},{6,7},{1,0},{3,2},{5,4},{7,6},{8,9},{10,11},{12,... | collective-permute-start | bytes 2162696 | tf_op jit(solution)/shard_map/ppermute | solution.py:455
  42.8 11.9 %collective-permute-start.1 = (bf16[32,10,8,128]{3,2,1,0:T(8,128)(2,1)S(1)}, bf16[32,10,8,128]{3,2,1,0:T(8,128)(2,1)S(1)}, u32[]{:S(2)}, u32[]{:S(2)}) collective-permute-start(bf16[32,10,8,128]{3,2,1,0:T(8,128)(2,1)S(1)} %cut_far.1), channel_id=1, source_target_pairs={{1,2},{3,4},{5,6},{2,1},{4,3},{6,5},{9,10},{11,12},{13,14},{10,9},... | collective-permute-start | bytes 1966088 | tf_op jit(solution)/shard_map/ppermute | solution.py:454
